TPU v7x, 256 devices: a whole 4x4x8 slice. The times are simulated.
256 devices in a mesh: dp: 2 (over core), seq: 32 (over z, y), head: 4 (over x).
Axes of the slice: x: 4, y: 4, z: 8, core: 2. Of those that a mesh axis runs over, the one named last changes fastest.
Arguments:
- tokens: bfloat16 [8192, 2048], P(('dp', 'seq')), may hold values from -6 to 6
- tangents: bfloat16 [8192, 2048], P(('dp', 'seq')), may hold values from -6 to 6
- attn_gain: float32 [2048], replicated, may hold values from 0.5 to 1.5
- ffn_gain: float32 [2048], replicated, may hold values from 0.5 to 1.5
- w_query: bfloat16 [2048, 2048], P(None, 'head'), may hold values from -0.125 to 0.125
- w_key: bfloat16 [2048, 256], replicated, may hold values from -0.125 to 0.125
- w_value: bfloat16 [2048, 256], replicated, may hold values from -0.125 to 0.125
- w_out: bfloat16 [2048, 2048], P('head'), may hold values from -0.125 to 0.125
- query_gain: float32 [128], replicated, may hold values from 0.5 to 8
- key_gain: float32 [128], replicated, may hold values from 0.5 to 8
- expert_gate: bfloat16 [128, 2048, 768], P(('seq', 'head'), None, 'dp'), may hold values from -0.125 to 0.125
- expert_up: bfloat16 [128, 2048, 768], P(('seq', 'head'), None, 'dp'), may hold values from -0.125 to 0.125
- expert_down: bfloat16 [128, 2048, 768], P(('seq', 'head'), None, 'dp'), may hold values from -0.21875 to 0.21875
- routes: int32 [8192, 8], P(('dp', 'seq', 'head')), may hold values from 0 to 127, all different within a row; in each aligned block of 32 rows (0 to 31, 32 to 63, ...) at most 3 rows name the same one
- route_weights: float32 [8192, 8], P(('dp', 'seq', 'head')), may hold values from 0.3 to 1.2
Outputs:
- layer_out: bfloat16 [8192, 2048], P(('dp', 'seq', 'head'))
- layer_tangent: bfloat16 [8192, 2048], P(('dp', 'seq', 'head'))
Inputs may be any that keep to these rules, and one draw needn't show every extreme that they name: `routes`: in each aligned block of 32 rows (the rows of one device) every row names 8 different experts, no expert is named by more than 3 rows, a bound that some block reaches.
All inputs are finite; a program needn't handle non-finite values.
Results may differ from a plain program's by a relative error of at most 0.025.
The roundings to bfloat16 on the way count: a program that leaves them out, or rounds other values in their place, can miss the bound.
Values may be sent and summed in bfloat16 or wider, within the bound.
No kernel may reach another device: no remote copies, remote signals or barrier semaphores. Data moves between devices by JAX's collectives and lax.ppermute only.
A program may use at most 128 MiB of HBM per device.

v0:
```python
import functools

import jax
import jax.numpy as jnp
from jax import lax
from jax.experimental import pallas as pl
from jax.experimental.pallas import tpu as pltpu
from jax.sharding import Mesh
from jax.sharding import PartitionSpec as P


SEQ_HEAD = ("seq_0", "seq_1", "head")
DP_SEQ = ("dp", "seq_0", "seq_1")
DP_SEQ_HEAD = ("dp", "seq_0", "seq_1", "head")


epsilon = 1e-06
rope_base = 1000000.0
masked_score = -1e30


def rms_norm(values, gain):
    mean_square = jnp.mean(values * values, axis=-1, keepdims=True)
    return values * lax.rsqrt(mean_square + epsilon) * gain


def turns_of(positions, head_width):
    half_width = head_width // 2
    exponent = jnp.arange(half_width, dtype=jnp.float32) * (2.0 / head_width)
    frequency = jnp.power(jnp.float32(rope_base), -exponent)
    angle = positions.astype(jnp.float32)[:, None] * frequency[None, :]
    return lax.optimization_barrier((jnp.cos(angle), jnp.sin(angle)))


def rotate(values, turns):
    half_width = values.shape[-1] // 2
    cosine, sine = (jnp.concatenate([t, t], -1)[:, None, :] for t in turns)
    first_half = values[..., :half_width]
    second_half = values[..., half_width:]
    turned = jnp.concatenate([-second_half, first_half], -1)
    return values * cosine + turned * sine


def head_prep(values, gain, turns):
    return rotate(rms_norm(values, gain), turns)


def head_pair(values, tangent, gain, turns):
    return jax.jvp(lambda inner: head_prep(inner, gain, turns), (values,), (tangent,))


def shifted(array, axis, offset):
    size = lax.axis_size(axis)
    return lax.ppermute(array, axis, [(i, (i + offset) % size) for i in range(size)])


def ring_blocks(block, axis):
    size = lax.axis_size(axis)
    found = {0: block}
    up = down = block
    for step in range(1, size // 2 + 1):
        up = shifted(up, axis, 1)
        found[-step] = up
        if 2 * step < size:
            down = shifted(down, axis, -1)
            found[step] = down
    return found


def three_parts(values):
    high = values.astype(jnp.bfloat16).astype(jnp.float32)
    rest = values - high
    middle = rest.astype(jnp.bfloat16).astype(jnp.float32)
    low = rest - middle
    row = lax.broadcasted_iota(jnp.int32, values.shape, 0)
    return jnp.where(row == 0, high, jnp.where(row == 1, middle, jnp.where(row == 2, low, 0.0)))


def attend_kernel(scale, group_rows, moe_rows, span_ref, joint_ref, *refs):
    blocks, (out_ref, held_ref, score_ref) = refs[:-3], refs[-3:]
    rows, width = joint_ref.shape[0], joint_ref.shape[1] // 2
    keys = blocks[0].shape[0]
    chunk = held_ref.shape[1]
    each_chunk = chunk // keys

    @pl.when(pl.program_id(0) == 0)
    def _():
        for number, block in enumerate(blocks):
            start = number % each_chunk * keys
            held_ref[number // each_chunk, start : start + keys] = block[...]

    joint = joint_ref[...]
    query = joint[:, width:]
    contract = (((1,), (1,)), ((), ()))
    shape = (rows, chunk)
    row = pl.program_id(0) * rows + lax.broadcasted_iota(jnp.int32, shape, 0)
    own = row // group_rows * keys + row % group_rows // keys * moe_rows + row % moe_rows
    lane = lax.broadcasted_iota(jnp.int32, shape, 1)
    own = own - lane % keys
    top = jnp.full(shape, masked_score, jnp.float32)
    for number in range(held_ref.shape[0]):
        score = lax.dot_general(
            query, held_ref[number, :, :width], contract, preferred_element_type=jnp.float32
        )
        first = number * each_chunk
        span = jnp.where(lane < keys, span_ref[first], span_ref[first + 1])
        score = jnp.where(span <= own, score * scale, masked_score)
        score_ref[number] = score
        top = jnp.maximum(top, score)
    top = jnp.max(top, axis=1, keepdims=True)
    total = jnp.zeros(shape, jnp.float32)
    slope = jnp.zeros(shape, jnp.float32)
    sums = jnp.zeros((rows, 2 * width), jnp.float32)
    tilted = jnp.zeros((rows, width), jnp.float32)
    for number in range(held_ref.shape[0]):
        score = score_ref[number]
        d_score = lax.dot_general(
            joint, held_ref[number, :, : 2 * width], contract, preferred_element_type=jnp.float32
        ) * scale
        weight = jnp.where(score > 0.5 * masked_score, jnp.exp(score - top), 0.0)
        tilt = weight * d_score
        total = total + weight
        slope = slope + tilt
        sums = sums + jnp.dot(
            weight.astype(jnp.bfloat16),
            held_ref[number, :, 2 * width :],
            preferred_element_type=jnp.float32,
        )
        tilted = tilted + jnp.dot(
            tilt.astype(jnp.bfloat16),
            held_ref[number, :, 2 * width : 3 * width],
            preferred_element_type=jnp.float32,
        )
    total = jnp.sum(total, axis=1, keepdims=True)
    slope = jnp.sum(slope, axis=1, keepdims=True)
    some = total > 0.0
    share = jnp.where(some, 1.0 / jnp.where(some, total, 1.0), 0.0)
    output = sums[:, :width] * share
    mean_slope = slope * share
    d_output = (sums[:, width:] + tilted) * share - mean_slope * output
    level = jnp.where(some, top + jnp.log(jnp.where(some, total, 1.0)), masked_score)
    both = jnp.concatenate([output, d_output], axis=1).astype(jnp.bfloat16)
    lane = lax.broadcasted_iota(jnp.int32, (rows, width), 1)
    figures = jnp.where(lane < width // 2, level, mean_slope)
    each = out_ref.shape[1] - 8
    for number in range(out_ref.shape[0]):
        out_ref[number, :each] = both[number * each : (number + 1) * each]
        turned = figures[number * each : (number + 1) * each].T
        stats = jnp.concatenate(
            [three_parts(turned[:8]), three_parts(turned[width // 2 : width // 2 + 8])], axis=1
        )
        out_ref[number, each:] = stats.astype(jnp.bfloat16)


def attend(spans, joint_query, blocks, receivers, rows_each, group_rows, moe_rows):
    width = joint_query.shape[1]
    count = 2
    rows = count * rows_each
    whole = pl.BlockSpec(blocks[0].shape, lambda i: (0, 0))
    return pl.pallas_call(
        functools.partial(attend_kernel, (width // 2) ** (-0.5), group_rows, moe_rows),
        grid=(receivers // count,),
        in_specs=[
            pl.BlockSpec(memory_space=pltpu.SMEM),
            pl.BlockSpec((rows, width), lambda i: (i, 0)),
            *[whole] * len(blocks),
        ],
        out_specs=pl.BlockSpec((count, rows_each + 8, width), lambda i: (i, 0, 0)),
        out_shape=jax.ShapeDtypeStruct((receivers, rows_each + 8, width), jnp.bfloat16),
        scratch_shapes=[
            pltpu.VMEM((len(blocks) // 2, 2 * blocks[0].shape[0], blocks[0].shape[1]), jnp.bfloat16),
            pltpu.VMEM((len(blocks) // 2, rows, 2 * blocks[0].shape[0]), jnp.float32),
        ],
        compiler_params=pltpu.CompilerParams(vmem_limit_bytes=40 << 20),
        name="attend",
    )(spans, joint_query, *blocks)


def merge_kernel(
    place_ref,
    arrived_ref,
    tokens_ref,
    tangents_ref,
    gain_ref,
    routing_ref,
    w_own,
    w_near_own,
    w_near_other,
    w_far_own,
    w_far_other,
    residual_ref,
    block_ref,
    held_ref,
    sum_ref,
):
    parts, each = arrived_ref.shape[0], arrived_ref.shape[1] - 8
    width = arrived_ref.shape[2] // 2
    groups = held_ref.shape[0] // 2
    row_groups = parts // groups
    moe_rows = held_ref.shape[1] // 2
    half_cols = held_ref.shape[2]

    def merge_group(group, carry):
        stats = [
            jnp.sum(
                arrived_ref[part * groups + group, each:].astype(jnp.float32),
                axis=0,
                keepdims=True,
            )
            for part in range(row_groups)
        ]
        level = jnp.concatenate([v[:, :width] for v in stats], axis=0)
        slopes = jnp.concatenate([v[:, width:] for v in stats], axis=0)
        raw = jnp.exp(level - jnp.max(level, axis=0, keepdims=True))
        mix = raw / jnp.sum(raw, axis=0, keepdims=True)
        slope = jnp.sum(mix * slopes, axis=0, keepdims=True)
        turned = jnp.concatenate([mix, mix * (slopes - slope)], axis=0).T
        output = d_output = None
        for part in range(row_groups):
            data = arrived_ref[part * groups + group, :each].astype(jnp.float32)
            share = turned[:, part : part + 1]
            tilt = turned[:, row_groups + part : row_groups + part + 1]
            term = share * data[:, :width]
            d_term = share * data[:, width:] + tilt * data[:, :width]
            output = term if output is None else output + term
            d_output = d_term if d_output is None else d_output + d_term
        per_half = half_cols // width
        for head in range(each // moe_rows):
            place = 2 * group + head // per_half
            cols = slice(head % per_half * width, (head % per_half + 1) * width)
            rows = slice(head * moe_rows, (head + 1) * moe_rows)
            held_ref[place, :moe_rows, cols] = output[rows].astype(jnp.bfloat16)
            held_ref[place, moe_rows:, cols] = d_output[rows].astype(jnp.bfloat16)
        return carry

    lax.fori_loop(0, groups, merge_group, 0)
    here, near_own, near_other, far, core = (place_ref[k] for k in range(5))
    order = [
        (2 * here, w_own, 0),
        (2 * here + 1, w_own, 1),
        (2 * near_own, w_near_own, 0),
        (2 * near_own + 1, w_near_own, 1),
        (2 * near_other, w_near_other, 0),
        (2 * near_other + 1, w_near_other, 1),
        (2 * far + core, w_far_own, 0),
        (2 * far + 1 - core, w_far_other, 0),
    ]
    step = sum_ref.shape[1] // 4

    def project(n, carry):
        cols = pl.ds(pl.multiple_of(n * step, step), step)
        total = None
        for place, piece, half in order:
            term = jnp.dot(
                held_ref[place],
                piece[half * half_cols : (half + 1) * half_cols, cols],
                preferred_element_type=jnp.float32,
            )
            total = term if total is None else total + term
        sum_ref[:, cols] = total
        return carry

    lax.fori_loop(0, sum_ref.shape[1] // step, project, 0)
    start = pl.multiple_of(here * moe_rows, moe_rows)
    own = pl.ds(start, moe_rows)
    residual = tokens_ref[own].astype(jnp.float32) + sum_ref[:moe_rows]
    d_residual = tangents_ref[own].astype(jnp.float32) + sum_ref[moe_rows:]
    residual_ref[:moe_rows] = residual
    residual_ref[moe_rows:] = d_residual
    gain = gain_ref[...]
    root = lax.rsqrt(jnp.mean(residual * residual, axis=1, keepdims=True) + epsilon)
    slope = jnp.mean(residual * d_residual, axis=1, keepdims=True) * root * root * root
    block_ref[:moe_rows] = (residual * root * gain).astype(jnp.bfloat16)
    d_normed = (d_residual * root - residual * slope) * gain
    block_ref[moe_rows : 2 * moe_rows] = d_normed.astype(jnp.bfloat16)
    block_ref[2 * moe_rows :] = routing_ref[...]


def merge(places, arrived, tokens, tangents, gain, routing, pieces, head_count, moe_rows):
    model_width = tokens.shape[1]
    half_cols = pieces[0].shape[0] // 2
    vmem = pl.BlockSpec(memory_space=pltpu.VMEM)
    return pl.pallas_call(
        merge_kernel,
        in_specs=[pl.BlockSpec(memory_space=pltpu.SMEM)] + [vmem] * (5 + len(pieces)),
        out_specs=(vmem, vmem),
        out_shape=(
            jax.ShapeDtypeStruct((2 * moe_rows, model_width), jnp.float32),
            jax.ShapeDtypeStruct((2 * moe_rows + 8, model_width), jnp.bfloat16),
        ),
        scratch_shapes=[
            pltpu.VMEM((2 * head_count, 2 * moe_rows, half_cols), jnp.bfloat16),
            pltpu.VMEM((2 * moe_rows, model_width), jnp.float32),
        ],
        compiler_params=pltpu.CompilerParams(vmem_limit_bytes=48 << 20),
        name="merge",
    )(places, arrived, tokens, tangents, gain, routing, *pieces)


def norm_kernel(tokens_ref, tangents_ref, gain_ref, out_ref):
    values = tokens_ref[...].astype(jnp.float32)
    tangent = tangents_ref[...].astype(jnp.float32)
    gain = gain_ref[...]
    root = lax.rsqrt(jnp.mean(values * values, axis=1, keepdims=True) + epsilon)
    slope = jnp.mean(values * tangent, axis=1, keepdims=True) * root * root * root
    out_ref[0] = (values * root * gain).astype(jnp.bfloat16)
    out_ref[1] = ((tangent * root - values * slope) * gain).astype(jnp.bfloat16)


def norm_rows(tokens, tangents, gain):
    count, width = tokens.shape
    rows = count // 4
    row_block = pl.BlockSpec((rows, width), lambda i: (i, 0))
    return pl.pallas_call(
        norm_kernel,
        grid=(count // rows,),
        in_specs=[row_block, row_block, pl.BlockSpec((1, width), lambda i: (0, 0))],
        out_specs=pl.BlockSpec((2, rows, width), lambda i: (0, i, 0)),
        out_shape=jax.ShapeDtypeStruct((2, count, width), jnp.bfloat16),
        name="norm_rows",
    )(tokens, tangents, gain)


def table_of(refs, rows, number):
    lanes = slice(128 * number, 128 * (number + 1))
    tiles = [ref[rows : rows + 8, lanes].astype(jnp.float32) for ref in refs]
    pairs = [tiles[k] + pltpu.roll(tiles[k + 1], 64, 1) for k in range(0, len(tiles), 2)]
    return jnp.concatenate(pairs, axis=1)


def placing(first_expert, routes, experts, capacity, slot_rows, moe_rows):
    count, cols = routes.shape
    expert = first_expert + lax.broadcasted_iota(jnp.int32, (experts, cols), 0)
    named = [
        jnp.broadcast_to(routes[k : k + 1], (experts, cols)) == expert.astype(jnp.float32)
        for k in range(count)
    ]
    hit = jnp.zeros((experts, cols), jnp.float32)
    for each in named:
        hit = hit + jnp.where(each, 1.0, 0.0)
    source = lax.broadcasted_iota(jnp.int32, (cols, cols), 0)
    target = lax.broadcasted_iota(jnp.int32, (cols, cols), 1)
    before = (source // moe_rows == target // moe_rows) & (source < target)
    rank = jnp.dot(
        hit.astype(jnp.bfloat16),
        jnp.where(before, 1.0, 0.0).astype(jnp.bfloat16),
        preferred_element_type=jnp.float32,
    )
    block = (lax.broadcasted_iota(jnp.int32, (experts, cols), 1) // (2 * moe_rows)).astype(jnp.float32)
    slot = jnp.where(hit > 0.0, block * capacity + rank, -1.0)
    row = lax.broadcasted_iota(jnp.int32, (slot_rows, cols), 0)
    half = lax.broadcasted_iota(jnp.int32, (slot_rows, cols), 1) // moe_rows % 2
    is_tangent = jnp.where((row // 8 == 1) | (row >= 20), 1, 0)
    row_slot = jnp.where(row < 8, row, jnp.where(row < 20, row - 8, row - 12))
    code = jnp.where(half == is_tangent, row_slot, -2).astype(jnp.float32)
    chosen = [
        jnp.broadcast_to(slot[j : j + 1], (slot_rows, cols)) == code for j in range(experts)
    ]
    return chosen, named


def pack_kernel(experts, capacity, slot_rows, moe_rows, first_ref, *refs):
    blocks, out_ref = refs[:-1], refs[-1]
    rows = 2 * moe_rows
    routes = table_of(blocks, rows, 0)
    chosen, _ = placing(first_ref[0], routes, experts, capacity, slot_rows, moe_rows)
    pick = jnp.concatenate([jnp.where(c, 1.0, 0.0) for c in chosen], axis=0).astype(jnp.bfloat16)
    source = jnp.concatenate([block[:rows] for block in blocks], axis=0)
    out_ref[...] = jnp.dot(pick, source, preferred_element_type=jnp.float32).astype(jnp.bfloat16)


def mix_kernel(experts, capacity, slot_rows, moe_rows, first_ref, returned_ref, *refs):
    tables, out_ref = refs[:-1], refs[-1]
    routes = table_of(tables, 0, 0)
    chosen, named = placing(first_ref[0], routes, experts, capacity, slot_rows, moe_rows)
    shares = table_of(tables, 0, 1)
    share = jnp.zeros(named[0].shape, jnp.float32)
    for k, each in enumerate(named):
        share = share + jnp.where(each, jnp.broadcast_to(shares[k : k + 1], each.shape), 0.0)
    held = jnp.concatenate(
        [
            jnp.where(c, jnp.broadcast_to(share[j : j + 1], c.shape), 0.0)
            for j, c in enumerate(chosen)
        ],
        axis=0,
    )
    out_ref[...] = jnp.dot(
        held.T.astype(jnp.bfloat16), returned_ref[...], preferred_element_type=jnp.float32
    )


def pack(first, blocks, experts, capacity, slot_rows, moe_rows):
    vmem = pl.BlockSpec(memory_space=pltpu.VMEM)
    return pl.pallas_call(
        functools.partial(pack_kernel, experts, capacity, slot_rows, moe_rows),
        in_specs=[pl.BlockSpec(memory_space=pltpu.SMEM)] + [vmem] * len(blocks),
        out_specs=vmem,
        out_shape=jax.ShapeDtypeStruct((experts * slot_rows, blocks[0].shape[1]), jnp.bfloat16),
        compiler_params=pltpu.CompilerParams(vmem_limit_bytes=40 << 20),
        name="pack",
    )(first, *blocks)


def mixed(first, returned, blocks, experts, capacity, slot_rows, moe_rows):
    vmem = pl.BlockSpec(memory_space=pltpu.VMEM)
    table = pl.BlockSpec((8, 256), lambda i: (2 * moe_rows // 8, 0))
    rows = 2 * moe_rows * len(blocks)
    return pl.pallas_call(
        functools.partial(mix_kernel, experts, capacity, slot_rows, moe_rows),
        grid=(1,),
        in_specs=[
            pl.BlockSpec(memory_space=pltpu.SMEM),
            pl.BlockSpec(returned.shape, lambda i: (0, 0)),
            *[table] * len(blocks),
        ],
        out_specs=pl.BlockSpec((rows, returned.shape[1]), lambda i: (0, 0)),
        out_shape=jax.ShapeDtypeStruct((rows, returned.shape[1]), jnp.float32),
        compiler_params=pltpu.CompilerParams(vmem_limit_bytes=40 << 20),
        name="mixed",
    )(first, returned, *blocks)


def expert_kernel(rows_ref, gate_a, up_a, gate_b, up_b, down_a, down_b, out_ref, sum_ref, hidden_ref):
    count, depth = rows_ref.shape
    units = gate_a.shape[1]
    step = depth // 4
    sum_ref[...] = jnp.zeros_like(sum_ref)

    def contract(k, carry):
        part = pl.ds(pl.multiple_of(k * step, step), step)
        for number, weight_ref in enumerate((gate_a, up_a, gate_b, up_b)):
            sum_ref[number] += jnp.dot(
                rows_ref[:, part], weight_ref[part], preferred_element_type=jnp.float32
            )
        return carry

    lax.fori_loop(0, depth // step, contract, 0)

    def pair(gate_value, gate_tangent, up_value, up_tangent):
        sigmoid_gate = jax.nn.sigmoid(gate_value)
        active = gate_value * sigmoid_gate
        active_slope = sigmoid_gate * (1.0 + gate_value * (1.0 - sigmoid_gate))
        primal = active * up_value
        return primal, active_slope * gate_tangent * up_value + active * up_tangent

    groups = 48 if count % 96 else 96

    def activate(number, carry):
        half = number // (count // groups)
        part = pl.ds(pl.multiple_of(number % (count // groups) * groups, groups), groups)
        gate = sum_ref[2 * half, part].reshape(groups // 24, 3, 8, units)
        up = sum_ref[2 * half + 1, part].reshape(groups // 24, 3, 8, units)
        primal, tangent = pair(gate[:, 0], gate[:, 1], up[:, 0], up[:, 1])
        mixed_gate, mixed_up = gate[:, 2], up[:, 2]
        turned_gate = pltpu.roll(mixed_gate, 4, 1)
        turned_up = pltpu.roll(mixed_up, 4, 1)
        first = lax.broadcasted_iota(jnp.int32, mixed_gate.shape, 1) < 4
        last_primal, last_tangent = pair(
            jnp.where(first, mixed_gate, turned_gate),
            jnp.where(first, turned_gate, mixed_gate),
            jnp.where(first, mixed_up, turned_up),
            jnp.where(first, turned_up, mixed_up),
        )
        last = jnp.where(first, last_primal, last_tangent)
        hidden = jnp.stack([primal, tangent, last], 1).reshape(groups, units)
        hidden_ref[half, part] = hidden.astype(jnp.bfloat16)
        return carry

    lax.fori_loop(0, 2 * (count // groups), activate, 0)

    def produce(n, carry):
        part = pl.ds(pl.multiple_of(n * step, step), step)
        across = (((1,), (1,)), ((), ()))
        result = lax.dot_general(
            hidden_ref[0], down_a[part], across, preferred_element_type=jnp.float32
        ) + lax.dot_general(
            hidden_ref[1], down_b[part], across, preferred_element_type=jnp.float32
        )
        out_ref[:, part] = result.astype(out_ref.dtype)
        return carry

    lax.fori_loop(0, depth // step, produce, 0)


def expert_rows(rows, weights):
    gate, up, down, gate_other, up_other, down_other = weights
    count, units = rows.shape[0], gate.shape[1]
    return pl.pallas_call(
        expert_kernel,
        out_shape=jax.ShapeDtypeStruct(rows.shape, jnp.bfloat16),
        scratch_shapes=[
            pltpu.VMEM((4, count, units), jnp.float32),
            pltpu.VMEM((2, count, units), jnp.bfloat16),
        ],
        compiler_params=pltpu.CompilerParams(vmem_limit_bytes=56 << 20),
        name="expert_rows",
    )(rows, gate, up, gate_other, up_other, down, down_other)


def layer(
    tokens,
    tangents,
    attn_gain,
    ffn_gain,
    w_query,
    w_key,
    w_value,
    w_out,
    query_gain,
    key_gain,
    expert_gate,
    expert_up,
    expert_down,
    routes,
    route_weights,
):
    tok_count, model_width = tokens.shape
    head_width = query_gain.shape[0]
    heads_here = w_query.shape[1] // head_width
    head_count = lax.axis_size("head")
    moe_rows = tok_count // head_count
    core = lax.axis_index("dp")
    other_core = [(0, 1), (1, 0)]

    half_rows = w_out.shape[0] // 2
    ring = range(head_count)
    sides = [(i, (i + 1) % head_count) for i in ring]
    sides += [(head_count + i, head_count + (i - 1) % head_count) for i in ring]
    far_rows = lax.dynamic_slice_in_dim(w_out, core * half_rows, half_rows, 0)
    near_own = lax.ppermute(w_out, ("dp", "head"), sides)
    far_own = shifted(far_rows, "head", head_count // 2)
    near_other = lax.ppermute(near_own, "dp", other_core)
    far_other = lax.ppermute(far_own, "dp", other_core)
    out_pieces = (w_out, near_own, near_other, far_own, far_other)

    own_halves = [expert_gate[0], expert_up[0], expert_down[0]]
    expert_halves = own_halves + [lax.ppermute(half, "dp", other_core) for half in own_halves]

    plane = lax.axis_index("seq_0")
    row_in_plane = lax.axis_index("seq_1")
    plane_rows = lax.axis_size("seq_1") * tok_count
    plane_count = lax.axis_size("seq_0")
    first_pos = plane * plane_rows + row_in_plane * tok_count
    positions = first_pos + jnp.arange(tok_count, dtype=jnp.int32)
    turns = turns_of(positions, head_width)
    kv_count = w_key.shape[1] // head_width
    devices_per_kv = lax.axis_size("head") // kv_count
    kv_start = lax.axis_index("head") // devices_per_kv * head_width
    key_cols = lax.dynamic_slice_in_dim(w_key, kv_start, head_width, 1)
    value_cols = lax.dynamic_slice_in_dim(w_value, kv_start, head_width, 1)
    stacked = norm_rows(tokens, tangents, attn_gain[None]).reshape(2 * tok_count, model_width)
    kv_cols = jnp.concatenate([key_cols, value_cols], 1)
    kv_all = jnp.dot(stacked, kv_cols, preferred_element_type=jnp.float32)
    key_all = kv_all[:, :head_width].reshape(2, tok_count, 1, head_width)
    value_all = kv_all[:, head_width:].reshape(2, tok_count, head_width)
    key, d_key = head_pair(key_all[0], key_all[1], key_gain, turns)
    packed = jnp.concatenate(
        [
            key.reshape(tok_count, head_width),
            d_key.reshape(tok_count, head_width),
            value_all[0],
            value_all[1],
        ],
        1,
    ).astype(jnp.bfloat16)
    blocks = ring_blocks(packed, "seq_0")

    top_count = routes.shape[1]
    tables = jnp.stack([routes.astype(jnp.bfloat16), route_weights.astype(jnp.bfloat16)], 0)
    tables = jnp.transpose(tables, (2, 0, 1))
    tables = jnp.concatenate([tables, tables, jnp.zeros_like(tables), jnp.zeros_like(tables)], 2)
    tables = tables.reshape(top_count, 2 * 4 * moe_rows)
    tables = jnp.pad(tables, ((0, 0), (0, model_width - tables.shape[1])))

    query_all = jnp.dot(stacked, w_query, preferred_element_type=jnp.float32)
    query_all = query_all.reshape(2, tok_count, heads_here, head_width)
    query, d_query = head_pair(query_all[0], query_all[1], query_gain, turns)

    def by_receiver(values):
        values = values.astype(jnp.bfloat16).reshape(head_count, moe_rows, heads_here, head_width)
        return jnp.transpose(values, (0, 2, 1, 3)).reshape(tok_count * heads_here, head_width)

    joint_own = jnp.concatenate([by_receiver(d_query), by_receiver(query)], 1)
    own_rows = joint_own.shape[0]
    row_groups = lax.axis_size("seq_1")
    copies = jnp.broadcast_to(joint_own[None], (row_groups, own_rows, 2 * head_width))
    joint_query = lax.all_to_all(copies, "seq_1", 0, 0, tiled=True)
    joint_query = joint_query.reshape(row_groups * own_rows, 2 * head_width)
    order = sorted(blocks)
    spans = jnp.stack(
        [
            (lax.rem(plane + k + plane_count, plane_count) - plane) * plane_rows
            + row_in_plane * tok_count
            for k in order
        ]
    ).astype(jnp.int32)
    receivers = row_groups * head_count
    rows_each = heads_here * moe_rows
    sent = attend(
        spans, joint_query, [blocks[k] for k in order], receivers, rows_each, own_rows, moe_rows
    )
    arrived = lax.all_to_all(sent, ("seq_1", "head"), 0, 0, tiled=True)
    here = lax.axis_index("head")
    side = 1 - 2 * core
    places = jnp.stack(
        [
            here,
            lax.rem(here - side + head_count, head_count),
            lax.rem(here + side + head_count, head_count),
            lax.rem(here + head_count // 2, head_count),
            core,
        ]
    ).astype(jnp.int32)
    residual, moe_in = merge(
        places,
        arrived,
        tokens,
        tangents,
        ffn_gain[None],
        tables,
        out_pieces,
        head_count,
        moe_rows,
    )
    gathered = ring_blocks(moe_in, "seq_0")

    plane_experts = row_groups * head_count
    capacity = 3
    first_expert = (plane * plane_experts).astype(jnp.int32)[None]
    near, far = [0, 1, -1, 2], [-2, 3, -3, -4]
    block_rows = 2 * moe_rows
    slot_rows = 2 * capacity * len(near)
    layout = (plane_experts, capacity, slot_rows, moe_rows)

    results = []
    for group in (near, far):
        outgoing = pack(first_expert, [gathered[k] for k in group], *layout)
        outgoing = outgoing.reshape(plane_experts, slot_rows, model_width)
        received = lax.all_to_all(outgoing, ("seq_1", "head"), 0, 0, tiled=True)
        results.append(
            expert_rows(received.reshape(plane_experts * slot_rows, model_width), expert_halves)
        )
    share_of = {}
    for group, result in ((far, results[1]), (near, results[0])):
        result = result.reshape(plane_experts, slot_rows, model_width)
        returned = lax.all_to_all(result, ("seq_1", "head"), 0, 0, tiled=True)
        returned = returned.reshape(plane_experts * slot_rows, model_width)
        sums = mixed(first_expert, returned, [gathered[k] for k in group], *layout)
        sums = sums.reshape(len(group), block_rows, model_width)
        for number, k in enumerate(group):
            share_of[k] = sums[number]
    low = jnp.bfloat16
    up = shifted(share_of[-4].astype(low), "seq_0", 1)
    down = shifted(share_of[-3].astype(low), "seq_0", -1)
    for k in (3, 2, 1):
        up = shifted((share_of[k] + up.astype(jnp.float32)).astype(low), "seq_0", 1)
    for k in (-2, -1):
        down = shifted((share_of[k] + down.astype(jnp.float32)).astype(low), "seq_0", -1)
    moe_sum = share_of[0] + up.astype(jnp.float32) + down.astype(jnp.float32)
    result = (residual + moe_sum).astype(jnp.bfloat16)
    layer_out, layer_tangent = result[:moe_rows], result[moe_rows:]
    return (layer_out, layer_tangent)


def solution(mesh):
    split = Mesh(
        mesh.devices.reshape(mesh.shape["dp"], 8, 4, mesh.shape["head"]),
        ("dp", "seq_0", "seq_1", "head"),
    )
    return jax.shard_map(
        layer,
        mesh=split,
        in_specs=(
            P(DP_SEQ, None),
            P(DP_SEQ, None),
            P(),
            P(),
            P(None, "head"),
            P(),
            P(),
            P("head", None),
            P(),
            P(),
            P(SEQ_HEAD, None, "dp"),
            P(SEQ_HEAD, None, "dp"),
            P(SEQ_HEAD, None, "dp"),
            P(DP_SEQ_HEAD, None),
            P(DP_SEQ_HEAD, None),
        ),
        out_specs=(P(DP_SEQ_HEAD, None), P(DP_SEQ_HEAD, None)),
        check_vma=False,
    )
```

profile of v0, /device:TPU:8, one launch (start us, length us, event | category | flops | bytes accessed | tf_op | source)
XLA Modules:
  0.0 279.1 jit_solution(13627021760509873140)
XLA Ops:
  0.6 1.6 collective-permute-start.7
  2.2 3.7 %norm_rows.1 = bf16[2,128,2048]{2,1,0:T(8,128)(2,1)} custom-call(bf16[128,2048]{1,0:T(8,128)(2,1)} %tokens_ref.3, bf16[128,2048]{1,0:T(8,128)(2,1)} %tangents_ref.3, f32[1,2048]{1,0:T(1,128)} %bitcast.110), custom_call_target="tpu_custom_call" | custom-call | tf_op jit(solution)/shard_map/norm_rows/pallas_call | solution.py:314
  5.9 1.9 fusion.39
  13.3 4.9 %all-to-all-start = ((bf16[4,512,256]{2,1,0:T(8,128)(2,1)}), bf16[4,512,256]{2,1,0:T(8,128)(2,1)S(1)}, u32[]{:S(2)}, u32[]{:S(2)}) async-start(bf16[4,512,256]{2,1,0:T(8,128)(2,1)} %broadcast_in_dim.9), calls=%async_computation | async-start | bytes 2097152 | tf_op jit(solution)/shard_map/all_to_all | solution.py:587
  18.2 2.3 constant_dynamic-slice_fusion
  20.6 2.7 collective-permute-start.9
  25.7 5.5 %collective-permute-done.7.w_near_own = bf16[512,2048]{1,0:T(8,128)(2,1)} collective-permute-done((bf16[512,2048]{1,0:T(8,128)(2,1)}, bf16[512,2048]{1,0:T(8,128)(2,1)}, u32[]{:S(2)}, u32[]{:S(2)}) %collective-permute-start.7) | collective-permute-done | bytes 2097184 | tf_op jit(solution)/shard_map/ppermute | solution.py:530
  31.3 17.6 %collective-permute-start.8 = (bf16[512,2048]{1,0:T(8,128)(2,1)}, bf16[512,2048]{1,0:T(8,128)(2,1)}, u32[]{:S(2)}, u32[]{:S(2)}) collective-permute-start(bf16[512,2048]{1,0:T(8,128)(2,1)} %collective-permute-done.7.w_near_own), channel_id=1, source_target_pairs={{0,128},{128,0},{1,129},{129,1},{2,130},{130,2},{3,131},{131,3},{4... | collective-permute-start | bytes 6291464 | tf_op jit(solution)/shard_map/ppermute | solution.py:532
  49.1 2.0 collective-permute-start
  51.0 4.0 %collective-permute-start.4 = (bf16[128,512]{1,0:T(8,128)(2,1)S(1)}, bf16[128,512]{1,0:T(8,128)(2,1)S(1)}, u32[]{:S(2)}, u32[]{:S(2)}) collective-permute-start(bf16[128,512]{1,0:T(8,128)(2,1)S(1)} %pad_maximum_fusion.1.refs_4_), channel_id=1, source_target_pairs={{0,112},{16,0},{32,16},{48,32},{64,48},{80,64},{96,80},{112,96},{1... | collective-permute-start | bytes 393224 | tf_op jit(solution)/shard_map/ppermute | solution.py:54
  55.1 3.6 %collective-permute-done.refs_3_ = bf16[128,512]{1,0:T(8,128)(2,1)S(1)} collective-permute-done((bf16[128,512]{1,0:T(8,128)(2,1)S(1)}, bf16[128,512]{1,0:T(8,128)(2,1)S(1)}, u32[]{:S(2)}, u32[]{:S(2)}) %collective-permute-start) | collective-permute-done | bytes 131104 | tf_op jit(solution)/shard_map/ppermute | solution.py:54
  58.7 3.2 %collective-permute-start.5 = (bf16[128,512]{1,0:T(8,128)(2,1)S(1)}, bf16[128,512]{1,0:T(8,128)(2,1)}, u32[]{:S(2)}, u32[]{:S(2)}) collective-permute-start(bf16[128,512]{1,0:T(8,128)(2,1)S(1)} %collective-permute-done.4.refs_5_), channel_id=1, source_target_pairs={{0,112},{16,0},{32,16},{48,32},{64,48},{80,64},{96,80},{112,96},{1... | collective-permute-start | bytes 393224 | tf_op jit(solution)/shard_map/ppermute | solution.py:54
  61.9 2.9 %collective-permute-done.1.refs_2_ = bf16[128,512]{1,0:T(8,128)(2,1)S(1)} collective-permute-done((bf16[128,512]{1,0:T(8,128)(2,1)S(1)}, bf16[128,512]{1,0:T(8,128)(2,1)S(1)}, u32[]{:S(2)}, u32[]{:S(2)}) %collective-permute-start.1) | collective-permute-done | bytes 131104 | tf_op jit(solution)/shard_map/ppermute | solution.py:54
  65.5 3.2 %collective-permute-start.6 = (bf16[128,512]{1,0:T(8,128)(2,1)}, bf16[128,512]{1,0:T(8,128)(2,1)}, u32[]{:S(2)}, u32[]{:S(2)}) collective-permute-start(bf16[128,512]{1,0:T(8,128)(2,1)} %collective-permute-done.5.refs_6_), channel_id=1, source_target_pairs={{0,112},{16,0},{32,16},{48,32},{64,48},{80,64},{96,80},{112,96},{1... | collective-permute-start | bytes 393224 | tf_op jit(solution)/shard_map/ppermute | solution.py:54
  68.7 2.4 collective-permute-done.2.refs_1_
  71.6 6.0 %collective-permute-done.3.refs_0_ = bf16[128,512]{1,0:T(8,128)(2,1)} collective-permute-done((bf16[128,512]{1,0:T(8,128)(2,1)}, bf16[128,512]{1,0:T(8,128)(2,1)}, u32[]{:S(2)}, u32[]{:S(2)}) %collective-permute-start.3) | collective-permute-done | bytes 131104 | tf_op jit(solution)/shard_map/ppermute | solution.py:54
  78.5 12.3 %attend.1 = bf16[16,136,256]{2,1,0:T(8,128)(2,1)S(1)} custom-call(s32[8]{0:T(128)S(1)} %stack.68.span_ref, bf16[2048,256]{1,0:T(8,128)(2,1)S(1)} %bitcast.87, bf16[128,512]{1,0:T(8,128)(2,1)} %collective-permute-done.3.refs_0_, bf16[128,512]{1,0:T(8,128)(2,1)} %collective-permute-done.2.refs_1_, bf16[128,512]{1,0:T(8,128)(2,1)S(1)} %copy-done.12, ...), custom_call_target="tpu_custom_call" | custom-call | tf_op jit(solution)/shard_map/attend/pallas_call | solution.py:160
  91.9 7.9 %all-to-all-start.1 = ((bf16[16,136,256]{2,1,0:T(8,128)(2,1)}), bf16[16,136,256]{2,1,0:T(8,128)(2,1)S(1)}, u32[]{:S(2)}, u32[]{:S(2)}) async-start(bf16[16,136,256]{2,1,0:T(8,128)(2,1)} %copy-done.3), calls=%async_computation.1 | async-start | bytes 2228224 | tf_op jit(solution)/shard_map/all_to_all | solution.py:602
  100.0 12.1 %all-to-all-done.1.arrived_ref = bf16[16,136,256]{2,1,0:T(8,128)(2,1)S(1)} async-done(((bf16[16,136,256]{2,1,0:T(8,128)(2,1)}), bf16[16,136,256]{2,1,0:T(8,128)(2,1)S(1)}, u32[]{:S(2)}, u32[]{:S(2)}) %all-to-all-start.1) | async-done | bytes 1114144 | tf_op jit(solution)/shard_map/all_to_all | solution.py:602
  114.2 7.1 %merge.1 = (f32[64,2048]{1,0:T(8,128)S(1)}, bf16[72,2048]{1,0:T(8,128)(2,1)S(1)}) custom-call(s32[5]{0:T(128)S(1)} %stack.59.place_ref, bf16[16,136,256]{2,1,0:T(8,128)(2,1)S(1)} %all-to-all-done.1.arrived_ref, bf16[128,2048]{1,0:T(8,128)(2,1)S(1)} %copy-done.4, bf16[128,2048]{1,0:T(8,128)(2,1)S(1)} %copy-done.5, f32[1,2048]{1,0:T(1,128)S(1)} %bitcast.88, ...), custom_call_target="tpu_custom_call" | custom-call | tf_op jit(solution)/shard_map/merge/pallas_call | solution.py:283
  122.1 3.2 %collective-permute-start.11 = (bf16[72,2048]{1,0:T(8,128)(2,1)S(1)}, bf16[72,2048]{1,0:T(8,128)(2,1)S(1)}, u32[]{:S(2)}, u32[]{:S(2)}) collective-permute-start(bf16[72,2048]{1,0:T(8,128)(2,1)S(1)} %get-tuple-element.9.refs_0_), channel_id=1, source_target_pairs={{0,112},{16,0},{32,16},{48,32},{64,48},{80,64},{96,80},{112,96},{1... | collective-permute-start | bytes 884744 | tf_op jit(solution)/shard_map/ppermute | solution.py:54
  125.3 6.6 %collective-permute-done.12.refs_2_ = bf16[72,2048]{1,0:T(8,128)(2,1)S(1)} collective-permute-done((bf16[72,2048]{1,0:T(8,128)(2,1)S(1)}, bf16[72,2048]{1,0:T(8,128)(2,1)S(1)}, u32[]{:S(2)}, u32[]{:S(2)}) %collective-permute-start.12) | collective-permute-done | bytes 294944 | tf_op jit(solution)/shard_map/ppermute | solution.py:54
  132.0 3.5 %collective-permute-start.13 = (bf16[72,2048]{1,0:T(8,128)(2,1)S(1)}, bf16[72,2048]{1,0:T(8,128)(2,1)S(1)}, u32[]{:S(2)}, u32[]{:S(2)}) collective-permute-start(bf16[72,2048]{1,0:T(8,128)(2,1)S(1)} %collective-permute-done.11.refs_1_), channel_id=1, source_target_pairs={{0,112},{16,0},{32,16},{48,32},{64,48},{80,64},{96,80},{112,96},{1... | collective-permute-start | bytes 884744 | tf_op jit(solution)/shard_map/ppermute | solution.py:54
  135.5 7.5 %collective-permute-done.17.refs_0_ = bf16[72,2048]{1,0:T(8,128)(2,1)S(1)} collective-permute-done((bf16[72,2048]{1,0:T(8,128)(2,1)S(1)}, bf16[72,2048]{1,0:T(8,128)(2,1)S(1)}, u32[]{:S(2)}, u32[]{:S(2)}) %collective-permute-start.17) | collective-permute-done | bytes 294944 | tf_op jit(solution)/shard_map/ppermute | solution.py:54
  143.7 3.2 %collective-permute-start.18 = (bf16[72,2048]{1,0:T(8,128)(2,1)S(1)}, bf16[72,2048]{1,0:T(8,128)(2,1)}, u32[]{:S(2)}, u32[]{:S(2)}) collective-permute-start(bf16[72,2048]{1,0:T(8,128)(2,1)S(1)} %collective-permute-done.13.refs_3_), channel_id=1, source_target_pairs={{0,112},{16,0},{32,16},{48,32},{64,48},{80,64},{96,80},{112,96},{1... | collective-permute-start | bytes 884744 | tf_op jit(solution)/shard_map/ppermute | solution.py:54
  146.9 6.6 %collective-permute-done.19.refs_2_ = bf16[72,2048]{1,0:T(8,128)(2,1)} collective-permute-done((bf16[72,2048]{1,0:T(8,128)(2,1)S(1)}, bf16[72,2048]{1,0:T(8,128)(2,1)}, u32[]{:S(2)}, u32[]{:S(2)}) %collective-permute-start.19) | collective-permute-done | bytes 294944 | tf_op jit(solution)/shard_map/ppermute | solution.py:54
  153.5 8.2 %collective-permute-done.20.refs_3_ = bf16[72,2048]{1,0:T(8,128)(2,1)} collective-permute-done((bf16[72,2048]{1,0:T(8,128)(2,1)}, bf16[72,2048]{1,0:T(8,128)(2,1)}, u32[]{:S(2)}, u32[]{:S(2)}) %collective-permute-start.20) | collective-permute-done | bytes 294944 | tf_op jit(solution)/shard_map/ppermute | solution.py:54
  162.7 1.9 pack.3
  165.8 6.5 %all-to-all-start.4 = ((bf16[16,24,2048]{2,1,0:T(8,128)(2,1)}), bf16[16,24,2048]{2,1,0:T(8,128)(2,1)}, u32[]{:S(2)}, u32[]{:S(2)}) async-start(bf16[16,24,2048]{2,1,0:T(8,128)(2,1)} %bitcast.86), calls=%async_computation.4 | async-start | bytes 3145728 | tf_op jit(solution)/shard_map/all_to_all | solution.py:639
  174.9 12.9 %all-to-all-done.4 = bf16[16,24,2048]{2,1,0:T(8,128)(2,1)} async-done(((bf16[16,24,2048]{2,1,0:T(8,128)(2,1)}), bf16[16,24,2048]{2,1,0:T(8,128)(2,1)}, u32[]{:S(2)}, u32[]{:S(2)}) %all-to-all-start.4) | async-done | bytes 1572896 | tf_op jit(solution)/shard_map/all_to_all | solution.py:639
  187.8 6.3 %all-to-all-start.2 = ((bf16[16,24,2048]{2,1,0:T(8,128)(2,1)}), bf16[16,24,2048]{2,1,0:T(8,128)(2,1)}, u32[]{:S(2)}, u32[]{:S(2)}) async-start(bf16[16,24,2048]{2,1,0:T(8,128)(2,1)} %bitcast.85), calls=%async_computation.2 | async-start | bytes 3145728 | tf_op jit(solution)/shard_map/all_to_all | solution.py:639
  194.2 12.5 %expert_rows.3 = bf16[384,2048]{1,0:T(8,128)(2,1)} custom-call(bf16[384,2048]{1,0:T(8,128)(2,1)} %bitcast.46.rows_ref, bf16[2048,384]{1,0:T(8,128)(2,1)} %bitcast.90, bf16[2048,384]{1,0:T(8,128)(2,1)} %bitcast.93, bf16[2048,384]{1,0:T(8,128)(2,1)} %collective-permute-done.14.gate_b, bf16[2048,384]{1,0:T(8,128)(2,1)} %collective-permute-done.15.up_b, ...), custom_call_target="tpu_custom_call" | custom-call | tf_op jit(solution)/shard_map/expert_rows/pallas_call | solution.py:488
  206.7 3.5 %all-to-all-done.2 = bf16[16,24,2048]{2,1,0:T(8,128)(2,1)} async-done(((bf16[16,24,2048]{2,1,0:T(8,128)(2,1)}), bf16[16,24,2048]{2,1,0:T(8,128)(2,1)}, u32[]{:S(2)}, u32[]{:S(2)}) %all-to-all-start.2) | async-done | bytes 1572896 | tf_op jit(solution)/shard_map/all_to_all | solution.py:639
  210.1 5.9 %all-to-all-start.5 = ((bf16[16,24,2048]{2,1,0:T(8,128)(2,1)}), bf16[16,24,2048]{2,1,0:T(8,128)(2,1)}, u32[]{:S(2)}, u32[]{:S(2)}) async-start(bf16[16,24,2048]{2,1,0:T(8,128)(2,1)} %bitcast.99), calls=%async_computation.5 | async-start | bytes 3145728 | tf_op jit(solution)/shard_map/all_to_all | solution.py:646
  216.0 12.5 %expert_rows.2 = bf16[384,2048]{1,0:T(8,128)(2,1)} custom-call(bf16[384,2048]{1,0:T(8,128)(2,1)} %bitcast.39.rows_ref, bf16[2048,384]{1,0:T(8,128)(2,1)} %bitcast.91, bf16[2048,384]{1,0:T(8,128)(2,1)} %bitcast.94, bf16[2048,384]{1,0:T(8,128)(2,1)} %collective-permute-done.14.gate_b, bf16[2048,384]{1,0:T(8,128)(2,1)} %collective-permute-done.15.up_b, ...), custom_call_target="tpu_custom_call" | custom-call | tf_op jit(solution)/shard_map/expert_rows/pallas_call | solution.py:488
  228.5 3.3 %all-to-all-done.5 = bf16[16,24,2048]{2,1,0:T(8,128)(2,1)} async-done(((bf16[16,24,2048]{2,1,0:T(8,128)(2,1)}), bf16[16,24,2048]{2,1,0:T(8,128)(2,1)}, u32[]{:S(2)}, u32[]{:S(2)}) %all-to-all-start.5) | async-done | bytes 1572896 | tf_op jit(solution)/shard_map/all_to_all | solution.py:646
  231.8 6.5 %all-to-all-start.3 = ((bf16[16,24,2048]{2,1,0:T(8,128)(2,1)}), bf16[16,24,2048]{2,1,0:T(8,128)(2,1)}, u32[]{:S(2)}, u32[]{:S(2)}) async-start(bf16[16,24,2048]{2,1,0:T(8,128)(2,1)} %bitcast.98), calls=%async_computation.3 | async-start | bytes 3145728 | tf_op jit(solution)/shard_map/all_to_all | solution.py:646
  239.3 2.4 mixed.3
  241.9 3.2 %collective-permute-start.25 = (bf16[64,2048]{1,0:T(8,128)(2,1)S(1)}, bf16[64,2048]{1,0:T(8,128)(2,1)S(1)}, u32[]{:S(2)}, u32[]{:S(2)}) collective-permute-start(bf16[64,2048]{1,0:T(8,128)(2,1)S(1)} %get-tuple-element.19), channel_id=1, source_target_pairs={{0,112},{16,0},{32,16},{48,32},{64,48},{80,64},{96,80},{112,96},{1... | collective-permute-start | bytes 786440 | tf_op jit(solution)/shard_map/ppermute | solution.py:54
  245.2 4.3 %collective-permute-done.21 = bf16[64,2048]{1,0:T(8,128)(2,1)S(1)} collective-permute-done((bf16[64,2048]{1,0:T(8,128)(2,1)S(1)}, bf16[64,2048]{1,0:T(8,128)(2,1)S(1)}, u32[]{:S(2)}, u32[]{:S(2)}) %collective-permute-start.21) | collective-permute-done | bytes 262176 | tf_op jit(solution)/shard_map/ppermute | solution.py:54
  249.5 1.4 collective-permute-done.25
  251.8 2.0 all-to-all-done.3
  253.8 2.4 mixed.2
  256.3 1.8 collective-permute-start.26
  258.1 4.7 %collective-permute-done.22 = bf16[64,2048]{1,0:T(8,128)(2,1)S(1)} collective-permute-done((bf16[64,2048]{1,0:T(8,128)(2,1)}, bf16[64,2048]{1,0:T(8,128)(2,1)S(1)}, u32[]{:S(2)}, u32[]{:S(2)}) %collective-permute-start.22) | collective-permute-done | bytes 262176 | tf_op jit(solution)/shard_map/ppermute | solution.py:54
  264.2 6.3 %collective-permute-done.23 = bf16[64,2048]{1,0:T(8,128)(2,1)S(1)} collective-permute-done((bf16[64,2048]{1,0:T(8,128)(2,1)S(1)}, bf16[64,2048]{1,0:T(8,128)(2,1)S(1)}, u32[]{:S(2)}, u32[]{:S(2)}) %collective-permute-start.23) | collective-permute-done | bytes 262176 | tf_op jit(solution)/shard_map/ppermute | solution.py:54
  270.7 3.2 %collective-permute-start.27 = (bf16[64,2048]{1,0:T(8,128)(2,1)S(1)}, bf16[64,2048]{1,0:T(8,128)(2,1)S(1)}, u32[]{:S(2)}, u32[]{:S(2)}) collective-permute-start(bf16[64,2048]{1,0:T(8,128)(2,1)S(1)} %get-tuple-element.15), channel_id=1, source_target_pairs={{0,112},{16,0},{32,16},{48,32},{64,48},{80,64},{96,80},{112,96},{1... | collective-permute-start | bytes 786440 | tf_op jit(solution)/shard_map/ppermute | solution.py:54
  273.9 4.3 %collective-permute-done.24 = bf16[64,2048]{1,0:T(8,128)(2,1)S(1)} collective-permute-done((bf16[64,2048]{1,0:T(8,128)(2,1)S(1)}, bf16[64,2048]{1,0:T(8,128)(2,1)S(1)}, u32[]{:S(2)}, u32[]{:S(2)}) %collective-permute-start.24) | collective-permute-done | bytes 262176 | tf_op jit(solution)/shard_map/ppermute | solution.py:54
  (120 shorter events, 24.0 us)
Async XLA Ops:
  0.6 5.3 %copy-start = (bf16[2048,512]{1,0:T(8,128)(2,1)S(1)}, bf16[2048,512]{1,0:T(8,128)(2,1)}, u32[]{:S(2)}) copy-start(bf16[2048,512]{1,0:T(8,128)(2,1)} %param.19) | copy-start | bytes 6291460
  0.6 30.6 %collective-permute-start.7 = (bf16[512,2048]{1,0:T(8,128)(2,1)}, bf16[512,2048]{1,0:T(8,128)(2,1)}, u32[]{:S(2)}, u32[]{:S(2)}) collective-permute-start(bf16[512,2048]{1,0:T(8,128)(2,1)} %w_own.1), channel_id=1, source_target_pairs={{0,1},{1,2},{2,3},{3,0},{128,131},{129,128},{130,129},{131,130},{4... | collective-permute-start | bytes 6291464 | tf_op jit(solution)/shard_map/ppermute | solution.py:530
  7.9 2.5 copy-start.18
  13.3 64.3 %all-to-all-start = ((bf16[4,512,256]{2,1,0:T(8,128)(2,1)}), bf16[4,512,256]{2,1,0:T(8,128)(2,1)S(1)}, u32[]{:S(2)}, u32[]{:S(2)}) async-start(bf16[4,512,256]{2,1,0:T(8,128)(2,1)} %broadcast_in_dim.9), calls=%async_computation | async-start | bytes 2097152 | tf_op jit(solution)/shard_map/all_to_all | solution.py:587
  20.6 50.5 %collective-permute-start.9 = (bf16[256,2048]{1,0:T(8,128)(2,1)}, bf16[256,2048]{1,0:T(8,128)(2,1)}, u32[]{:S(2)}, u32[]{:S(2)}) collective-permute-start(bf16[256,2048]{1,0:T(8,128)(2,1)} %constant_dynamic-slice_fusion), channel_id=1, source_target_pairs={{0,2},{1,3},{2,0},{3,1},{4,6},{5,7},{6,4},{7,5},{8,10},{9,11},{10,... | collective-permute-start | bytes 3145736 | tf_op jit(solution)/shard_map/ppermute | solution.py:54
  23.3 1.5 copy-start.14
  31.3 80.8 %collective-permute-start.8 = (bf16[512,2048]{1,0:T(8,128)(2,1)}, bf16[512,2048]{1,0:T(8,128)(2,1)}, u32[]{:S(2)}, u32[]{:S(2)}) collective-permute-start(bf16[512,2048]{1,0:T(8,128)(2,1)} %collective-permute-done.7.w_near_own), channel_id=1, source_target_pairs={{0,128},{128,0},{1,129},{129,1},{2,130},{130,2},{3,131},{131,3},{4... | collective-permute-start | bytes 6291464 | tf_op jit(solution)/shard_map/ppermute | solution.py:532
  49.1 9.6 %collective-permute-start = (bf16[128,512]{1,0:T(8,128)(2,1)S(1)}, bf16[128,512]{1,0:T(8,128)(2,1)S(1)}, u32[]{:S(2)}, u32[]{:S(2)}) collective-permute-start(bf16[128,512]{1,0:T(8,128)(2,1)S(1)} %pad_maximum_fusion.1.refs_4_), channel_id=1, source_target_pairs={{0,16},{16,32},{32,48},{48,64},{64,80},{80,96},{96,112},{112,0},{1... | collective-permute-start | bytes 393224 | tf_op jit(solution)/shard_map/ppermute | solution.py:54
  51.0 7.6 %collective-permute-start.4 = (bf16[128,512]{1,0:T(8,128)(2,1)S(1)}, bf16[128,512]{1,0:T(8,128)(2,1)S(1)}, u32[]{:S(2)}, u32[]{:S(2)}) collective-permute-start(bf16[128,512]{1,0:T(8,128)(2,1)S(1)} %pad_maximum_fusion.1.refs_4_), channel_id=1, source_target_pairs={{0,112},{16,0},{32,16},{48,32},{64,48},{80,64},{96,80},{112,96},{1... | collective-permute-start | bytes 393224 | tf_op jit(solution)/shard_map/ppermute | solution.py:54
  58.7 6.2 %collective-permute-start.1 = (bf16[128,512]{1,0:T(8,128)(2,1)S(1)}, bf16[128,512]{1,0:T(8,128)(2,1)S(1)}, u32[]{:S(2)}, u32[]{:S(2)}) collective-permute-start(bf16[128,512]{1,0:T(8,128)(2,1)S(1)} %collective-permute-done.refs_3_), channel_id=1, source_target_pairs={{0,16},{16,32},{32,48},{48,64},{64,80},{80,96},{96,112},{112,0},{1... | collective-permute-start | bytes 393224 | tf_op jit(solution)/shard_map/ppermute | solution.py:54
  58.7 6.8 %collective-permute-start.5 = (bf16[128,512]{1,0:T(8,128)(2,1)S(1)}, bf16[128,512]{1,0:T(8,128)(2,1)}, u32[]{:S(2)}, u32[]{:S(2)}) collective-permute-start(bf16[128,512]{1,0:T(8,128)(2,1)S(1)} %collective-permute-done.4.refs_5_), channel_id=1, source_target_pairs={{0,112},{16,0},{32,16},{48,32},{64,48},{80,64},{96,80},{112,96},{1... | collective-permute-start | bytes 393224 | tf_op jit(solution)/shard_map/ppermute | solution.py:54
  64.8 6.3 %collective-permute-start.2 = (bf16[128,512]{1,0:T(8,128)(2,1)S(1)}, bf16[128,512]{1,0:T(8,128)(2,1)}, u32[]{:S(2)}, u32[]{:S(2)}) collective-permute-start(bf16[128,512]{1,0:T(8,128)(2,1)S(1)} %collective-permute-done.1.refs_2_), channel_id=1, source_target_pairs={{0,16},{16,32},{32,48},{48,64},{64,80},{80,96},{96,112},{112,0},{1... | collective-permute-start | bytes 393224 | tf_op jit(solution)/shard_map/ppermute | solution.py:54
  65.5 6.1 %collective-permute-start.6 = (bf16[128,512]{1,0:T(8,128)(2,1)}, bf16[128,512]{1,0:T(8,128)(2,1)}, u32[]{:S(2)}, u32[]{:S(2)}) collective-permute-start(bf16[128,512]{1,0:T(8,128)(2,1)} %collective-permute-done.5.refs_6_), channel_id=1, source_target_pairs={{0,112},{16,0},{32,16},{48,32},{64,48},{80,64},{96,80},{112,96},{1... | collective-permute-start | bytes 393224 | tf_op jit(solution)/shard_map/ppermute | solution.py:54
  71.1 6.5 %collective-permute-start.3 = (bf16[128,512]{1,0:T(8,128)(2,1)}, bf16[128,512]{1,0:T(8,128)(2,1)}, u32[]{:S(2)}, u32[]{:S(2)}) collective-permute-start(bf16[128,512]{1,0:T(8,128)(2,1)} %collective-permute-done.2.refs_1_), channel_id=1, source_target_pairs={{0,16},{16,32},{32,48},{48,64},{64,80},{80,96},{96,112},{112,0},{1... | collective-permute-start | bytes 393224 | tf_op jit(solution)/shard_map/ppermute | solution.py:54
  71.1 41.0 %collective-permute-start.10 = (bf16[256,2048]{1,0:T(8,128)(2,1)}, bf16[256,2048]{1,0:T(8,128)(2,1)}, u32[]{:S(2)}, u32[]{:S(2)}) collective-permute-start(bf16[256,2048]{1,0:T(8,128)(2,1)} %collective-permute-done.9.w_far_own), channel_id=1, source_target_pairs={{0,128},{128,0},{1,129},{129,1},{2,130},{130,2},{3,131},{131,3},{4... | collective-permute-start | bytes 3145736 | tf_op jit(solution)/shard_map/ppermute | solution.py:533
  78.5 21.3 %copy-start.16 = (f32[32,8]{0,1:T(8,128)S(1)}, f32[32,8]{0,1:T(8,128)}, u32[]{:S(2)}) copy-start(f32[32,8]{0,1:T(8,128)} %param.29) | copy-start | bytes 3076
  78.5 33.6 %copy-start.13 = (f32[2048]{0:T(1024)S(1)}, f32[2048]{0:T(1024)}, u32[]{:S(2)}) copy-start(f32[2048]{0:T(1024)} %param.18) | copy-start | bytes 24580
  90.9 1.0 copy-start.3
  91.9 8.0 %copy-start.17 = (s32[32,8]{0,1:T(8,128)S(1)}, s32[32,8]{0,1:T(8,128)}, u32[]{:S(2)}) copy-start(s32[32,8]{0,1:T(8,128)} %param.28) | copy-start | bytes 3076
  91.9 20.2 %all-to-all-start.1 = ((bf16[16,136,256]{2,1,0:T(8,128)(2,1)}), bf16[16,136,256]{2,1,0:T(8,128)(2,1)S(1)}, u32[]{:S(2)}, u32[]{:S(2)}) async-start(bf16[16,136,256]{2,1,0:T(8,128)(2,1)} %copy-done.3), calls=%async_computation.1 | async-start | bytes 2228224 | tf_op jit(solution)/shard_map/all_to_all | solution.py:602
  112.1 1.0 copy-start.4
  113.2 1.0 copy-start.5
  122.1 9.9 %collective-permute-start.12 = (bf16[72,2048]{1,0:T(8,128)(2,1)S(1)}, bf16[72,2048]{1,0:T(8,128)(2,1)S(1)}, u32[]{:S(2)}, u32[]{:S(2)}) collective-permute-start(bf16[72,2048]{1,0:T(8,128)(2,1)S(1)} %get-tuple-element.9.refs_0_), channel_id=1, source_target_pairs={{0,16},{16,32},{32,48},{48,64},{64,80},{80,96},{96,112},{112,0},{1... | collective-permute-start | bytes 884744 | tf_op jit(solution)/shard_map/ppermute | solution.py:54
  122.1 9.9 %collective-permute-start.11 = (bf16[72,2048]{1,0:T(8,128)(2,1)S(1)}, bf16[72,2048]{1,0:T(8,128)(2,1)S(1)}, u32[]{:S(2)}, u32[]{:S(2)}) collective-permute-start(bf16[72,2048]{1,0:T(8,128)(2,1)S(1)} %get-tuple-element.9.refs_0_), channel_id=1, source_target_pairs={{0,112},{16,0},{32,16},{48,32},{64,48},{80,64},{96,80},{112,96},{1... | collective-permute-start | bytes 884744 | tf_op jit(solution)/shard_map/ppermute | solution.py:54
  131.9 11.0 %collective-permute-start.17 = (bf16[72,2048]{1,0:T(8,128)(2,1)S(1)}, bf16[72,2048]{1,0:T(8,128)(2,1)S(1)}, u32[]{:S(2)}, u32[]{:S(2)}) collective-permute-start(bf16[72,2048]{1,0:T(8,128)(2,1)S(1)} %collective-permute-done.12.refs_2_), channel_id=1, source_target_pairs={{0,16},{16,32},{32,48},{48,64},{64,80},{80,96},{96,112},{112,0},{1... | collective-permute-start | bytes 884744 | tf_op jit(solution)/shard_map/ppermute | solution.py:54
  132.0 11.7 %collective-permute-start.13 = (bf16[72,2048]{1,0:T(8,128)(2,1)S(1)}, bf16[72,2048]{1,0:T(8,128)(2,1)S(1)}, u32[]{:S(2)}, u32[]{:S(2)}) collective-permute-start(bf16[72,2048]{1,0:T(8,128)(2,1)S(1)} %collective-permute-done.11.refs_1_), channel_id=1, source_target_pairs={{0,112},{16,0},{32,16},{48,32},{64,48},{80,64},{96,80},{112,96},{1... | collective-permute-start | bytes 884744 | tf_op jit(solution)/shard_map/ppermute | solution.py:54
  142.9 10.6 %collective-permute-start.19 = (bf16[72,2048]{1,0:T(8,128)(2,1)S(1)}, bf16[72,2048]{1,0:T(8,128)(2,1)}, u32[]{:S(2)}, u32[]{:S(2)}) collective-permute-start(bf16[72,2048]{1,0:T(8,128)(2,1)S(1)} %collective-permute-done.17.refs_0_), channel_id=1, source_target_pairs={{0,16},{16,32},{32,48},{48,64},{64,80},{80,96},{96,112},{112,0},{1... | collective-permute-start | bytes 884744 | tf_op jit(solution)/shard_map/ppermute | solution.py:54
  143.7 9.8 %collective-permute-start.18 = (bf16[72,2048]{1,0:T(8,128)(2,1)S(1)}, bf16[72,2048]{1,0:T(8,128)(2,1)}, u32[]{:S(2)}, u32[]{:S(2)}) collective-permute-start(bf16[72,2048]{1,0:T(8,128)(2,1)S(1)} %collective-permute-done.13.refs_3_), channel_id=1, source_target_pairs={{0,112},{16,0},{32,16},{48,32},{64,48},{80,64},{96,80},{112,96},{1... | collective-permute-start | bytes 884744 | tf_op jit(solution)/shard_map/ppermute | solution.py:54
  153.5 8.2 %collective-permute-start.20 = (bf16[72,2048]{1,0:T(8,128)(2,1)}, bf16[72,2048]{1,0:T(8,128)(2,1)}, u32[]{:S(2)}, u32[]{:S(2)}) collective-permute-start(bf16[72,2048]{1,0:T(8,128)(2,1)} %collective-permute-done.19.refs_2_), channel_id=1, source_target_pairs={{0,16},{16,32},{32,48},{48,64},{64,80},{80,96},{96,112},{112,0},{1... | collective-permute-start | bytes 884744 | tf_op jit(solution)/shard_map/ppermute | solution.py:54
  161.8 1.0 copy-start.7
  164.6 1.1 copy-start.2
  165.8 22.0 %all-to-all-start.4 = ((bf16[16,24,2048]{2,1,0:T(8,128)(2,1)}), bf16[16,24,2048]{2,1,0:T(8,128)(2,1)}, u32[]{:S(2)}, u32[]{:S(2)}) async-start(bf16[16,24,2048]{2,1,0:T(8,128)(2,1)} %bitcast.86), calls=%async_computation.4 | async-start | bytes 3145728 | tf_op jit(solution)/shard_map/all_to_all | solution.py:639
  172.3 21.8 %collective-permute-start.14 = (bf16[2048,384]{1,0:T(8,128)(2,1)}, bf16[2048,384]{1,0:T(8,128)(2,1)}, u32[]{:S(2)}, u32[]{:S(2)}) collective-permute-start(bf16[2048,384]{1,0:T(8,128)(2,1)} %bitcast.89), channel_id=1, source_target_pairs={{0,128},{128,0},{1,129},{129,1},{2,130},{130,2},{3,131},{131,3},{4... | collective-permute-start | bytes 4718600 | tf_op jit(solution)/shard_map/ppermute | solution.py:537
  172.3 21.8 %collective-permute-start.15 = (bf16[2048,384]{1,0:T(8,128)(2,1)}, bf16[2048,384]{1,0:T(8,128)(2,1)}, u32[]{:S(2)}, u32[]{:S(2)}) collective-permute-start(bf16[2048,384]{1,0:T(8,128)(2,1)} %bitcast.92), channel_id=1, source_target_pairs={{0,128},{128,0},{1,129},{129,1},{2,130},{130,2},{3,131},{131,3},{4... | collective-permute-start | bytes 4718600 | tf_op jit(solution)/shard_map/ppermute | solution.py:537
  172.8 21.3 %collective-permute-start.16 = (bf16[2048,384]{1,0:T(8,128)(2,1)}, bf16[2048,384]{1,0:T(8,128)(2,1)}, u32[]{:S(2)}, u32[]{:S(2)}) collective-permute-start(bf16[2048,384]{1,0:T(8,128)(2,1)} %bitcast.95), channel_id=1, source_target_pairs={{0,128},{128,0},{1,129},{129,1},{2,130},{130,2},{3,131},{131,3},{4... | collective-permute-start | bytes 4718600 | tf_op jit(solution)/shard_map/ppermute | solution.py:537
  173.7 1.2 copy-start.1
  187.8 22.3 %all-to-all-start.2 = ((bf16[16,24,2048]{2,1,0:T(8,128)(2,1)}), bf16[16,24,2048]{2,1,0:T(8,128)(2,1)}, u32[]{:S(2)}, u32[]{:S(2)}) async-start(bf16[16,24,2048]{2,1,0:T(8,128)(2,1)} %bitcast.85), calls=%async_computation.2 | async-start | bytes 3145728 | tf_op jit(solution)/shard_map/all_to_all | solution.py:639
  210.1 21.6 %all-to-all-start.5 = ((bf16[16,24,2048]{2,1,0:T(8,128)(2,1)}), bf16[16,24,2048]{2,1,0:T(8,128)(2,1)}, u32[]{:S(2)}, u32[]{:S(2)}) async-start(bf16[16,24,2048]{2,1,0:T(8,128)(2,1)} %bitcast.99), calls=%async_computation.5 | async-start | bytes 3145728 | tf_op jit(solution)/shard_map/all_to_all | solution.py:646
  231.8 22.0 %all-to-all-start.3 = ((bf16[16,24,2048]{2,1,0:T(8,128)(2,1)}), bf16[16,24,2048]{2,1,0:T(8,128)(2,1)}, u32[]{:S(2)}, u32[]{:S(2)}) async-start(bf16[16,24,2048]{2,1,0:T(8,128)(2,1)} %bitcast.98), calls=%async_computation.3 | async-start | bytes 3145728 | tf_op jit(solution)/shard_map/all_to_all | solution.py:646
  241.9 7.7 %collective-permute-start.21 = (bf16[64,2048]{1,0:T(8,128)(2,1)S(1)}, bf16[64,2048]{1,0:T(8,128)(2,1)S(1)}, u32[]{:S(2)}, u32[]{:S(2)}) collective-permute-start(bf16[64,2048]{1,0:T(8,128)(2,1)S(1)} %get-tuple-element.18), channel_id=1, source_target_pairs={{0,16},{16,32},{32,48},{48,64},{64,80},{80,96},{96,112},{112,0},{1... | collective-permute-start | bytes 786440 | tf_op jit(solution)/shard_map/ppermute | solution.py:54
  241.9 9.0 %collective-permute-start.25 = (bf16[64,2048]{1,0:T(8,128)(2,1)S(1)}, bf16[64,2048]{1,0:T(8,128)(2,1)S(1)}, u32[]{:S(2)}, u32[]{:S(2)}) collective-permute-start(bf16[64,2048]{1,0:T(8,128)(2,1)S(1)} %get-tuple-element.19), channel_id=1, source_target_pairs={{0,112},{16,0},{32,16},{48,32},{64,48},{80,64},{96,80},{112,96},{1... | collective-permute-start | bytes 786440 | tf_op jit(solution)/shard_map/ppermute | solution.py:54
  251.8 11.0 %collective-permute-start.22 = (bf16[64,2048]{1,0:T(8,128)(2,1)}, bf16[64,2048]{1,0:T(8,128)(2,1)S(1)}, u32[]{:S(2)}, u32[]{:S(2)}) collective-permute-start(bf16[64,2048]{1,0:T(8,128)(2,1)} %get-tuple-element.16), channel_id=1, source_target_pairs={{0,16},{16,32},{32,48},{48,64},{64,80},{80,96},{96,112},{112,0},{1... | collective-permute-start | bytes 786440 | tf_op jit(solution)/shard_map/ppermute | solution.py:54
  253.8 2.5 copy-start.15
  256.2 22.0 %copy-start.10 = (f32[64,2048]{1,0:T(8,128)S(1)}, f32[64,2048]{1,0:T(8,128)}, u32[]{:S(2)}) copy-start(f32[64,2048]{1,0:T(8,128)} %copy-done.9) | copy-start | bytes 1572868
  256.3 7.9 %collective-permute-start.26 = (bf16[64,2048]{1,0:T(8,128)(2,1)S(1)}, bf16[64,2048]{1,0:T(8,128)(2,1)S(1)}, u32[]{:S(2)}, u32[]{:S(2)}) collective-permute-start(bf16[64,2048]{1,0:T(8,128)(2,1)S(1)} %copy-done.15), channel_id=1, source_target_pairs={{0,112},{16,0},{32,16},{48,32},{64,48},{80,64},{96,80},{112,96},{1... | collective-permute-start | bytes 786440 | tf_op jit(solution)/shard_map/ppermute | solution.py:54
  262.8 7.7 %collective-permute-start.23 = (bf16[64,2048]{1,0:T(8,128)(2,1)S(1)}, bf16[64,2048]{1,0:T(8,128)(2,1)S(1)}, u32[]{:S(2)}, u32[]{:S(2)}) collective-permute-start(bf16[64,2048]{1,0:T(8,128)(2,1)S(1)} %fusion.7), channel_id=1, source_target_pairs={{0,16},{16,32},{32,48},{48,64},{64,80},{80,96},{96,112},{112,0},{1... | collective-permute-start | bytes 786440 | tf_op jit(solution)/shard_map/ppermute | solution.py:54
  270.6 7.7 %collective-permute-start.24 = (bf16[64,2048]{1,0:T(8,128)(2,1)S(1)}, bf16[64,2048]{1,0:T(8,128)(2,1)S(1)}, u32[]{:S(2)}, u32[]{:S(2)}) collective-permute-start(bf16[64,2048]{1,0:T(8,128)(2,1)S(1)} %get-tuple-element.14), channel_id=1, source_target_pairs={{0,16},{16,32},{32,48},{48,64},{64,80},{80,96},{96,112},{112,0},{1... | collective-permute-start | bytes 786440 | tf_op jit(solution)/shard_map/ppermute | solution.py:54
  270.7 7.6 %collective-permute-start.27 = (bf16[64,2048]{1,0:T(8,128)(2,1)S(1)}, bf16[64,2048]{1,0:T(8,128)(2,1)S(1)}, u32[]{:S(2)}, u32[]{:S(2)}) collective-permute-start(bf16[64,2048]{1,0:T(8,128)(2,1)S(1)} %get-tuple-element.15), channel_id=1, source_target_pairs={{0,112},{16,0},{32,16},{48,32},{64,48},{80,64},{96,80},{112,96},{1... | collective-permute-start | bytes 786440 | tf_op jit(solution)/shard_map/ppermute | solution.py:54
  (6 other events, 4.8 us)
where the time goes:
time: 281 us; the launch traced here: 279 us
  waiting for transfers between devices  106 us (38%)
  starting transfers between devices  91.5 us (33%)
  Pallas kernels  55.7 us (20%)
  local copies, waits for them, and re-layouts  18.1 us (6%)
  other arithmetic  4.61 us (2%)
    ppermute x22, waiting for transfers between devices, shifted(): lax.ppermute(array, axis, [(i, (i + offset) % size) for i in range(size)])  66.6 us
    ppermute x22, starting transfers between devices, shifted(): lax.ppermute(array, axis, [(i, (i + offset) % size) for i in range(size)])  33.7 us
    pallas_call x2, Pallas kernels, expert_rows(): pl.pallas_call(expert_kernel, out_shape=jax.ShapeDtypeStruct(rows.shape,...  25 us
    ppermute x1, starting transfers between devices, layer(): near_other = lax.ppermute(near_own, 'dp', other_core)  17.6 us
    all_to_all x2, waiting for transfers between devices, layer(): received = lax.all_to_all(outgoing, ('seq_1', 'head'), 0, 0, tiled=True)  16.4 us
    all_to_all x2, starting transfers between devices, layer(): received = lax.all_to_all(outgoing, ('seq_1', 'head'), 0, 0, tiled=True)  12.9 us
    all_to_all x2, starting transfers between devices, layer(): returned = lax.all_to_all(result, ('seq_1', 'head'), 0, 0, tiled=True)  12.4 us
    pallas_call x1, Pallas kernels, attend(): pl.pallas_call(functools.partial(attend_kernel, (width // 2) ** (-0.5), g...  12.3 us
  transfers between devices with their start and end apart: 34, of which 21 were waited for; matrix products, arithmetic and copies ran while one was open for 5% of the time, Pallas kernels for 17%

commit v1 on v0

--- a/solution.py
+++ b/solution.py
@@ -19,34 +19,13 @@
 masked_score = -1e30
 
 
-def rms_norm(values, gain):
-    mean_square = jnp.mean(values * values, axis=-1, keepdims=True)
-    return values * lax.rsqrt(mean_square + epsilon) * gain
-
-
 def turns_of(positions, head_width):
     half_width = head_width // 2
     exponent = jnp.arange(half_width, dtype=jnp.float32) * (2.0 / head_width)
     frequency = jnp.power(jnp.float32(rope_base), -exponent)
     angle = positions.astype(jnp.float32)[:, None] * frequency[None, :]
-    return lax.optimization_barrier((jnp.cos(angle), jnp.sin(angle)))
-
-
-def rotate(values, turns):
-    half_width = values.shape[-1] // 2
-    cosine, sine = (jnp.concatenate([t, t], -1)[:, None, :] for t in turns)
-    first_half = values[..., :half_width]
-    second_half = values[..., half_width:]
-    turned = jnp.concatenate([-second_half, first_half], -1)
-    return values * cosine + turned * sine
-
-
-def head_prep(values, gain, turns):
-    return rotate(rms_norm(values, gain), turns)
-
-
-def head_pair(values, tangent, gain, turns):
-    return jax.jvp(lambda inner: head_prep(inner, gain, turns), (values,), (tangent,))
+    cosine, sine = jnp.cos(angle), jnp.sin(angle)
+    return jnp.concatenate([cosine, cosine], 1), jnp.concatenate([-sine, sine], 1)
 
 
 def shifted(array, axis, offset):
@@ -297,28 +276,119 @@
     )(places, arrived, tokens, tangents, gain, routing, *pieces)
 
 
-def norm_kernel(tokens_ref, tangents_ref, gain_ref, out_ref):
-    values = tokens_ref[...].astype(jnp.float32)
-    tangent = tangents_ref[...].astype(jnp.float32)
-    gain = gain_ref[...]
+def turned_pair(values, tangent, gain, cosine, sine):
     root = lax.rsqrt(jnp.mean(values * values, axis=1, keepdims=True) + epsilon)
     slope = jnp.mean(values * tangent, axis=1, keepdims=True) * root * root * root
-    out_ref[0] = (values * root * gain).astype(jnp.bfloat16)
-    out_ref[1] = ((tangent * root - values * slope) * gain).astype(jnp.bfloat16)
-
-
-def norm_rows(tokens, tangents, gain):
-    count, width = tokens.shape
-    rows = count // 4
-    row_block = pl.BlockSpec((rows, width), lambda i: (i, 0))
+    normed = values * root * gain
+    d_normed = (tangent * root - values * slope) * gain
+    half = values.shape[1] // 2
+    return (
+        normed * cosine + pltpu.roll(normed, half, 1) * sine,
+        d_normed * cosine + pltpu.roll(d_normed, half, 1) * sine,
+    )
+
+
+def keys_kernel(
+    head_ref,
+    tokens_ref,
+    tangents_ref,
+    gain_ref,
+    w_key_ref,
+    w_value_ref,
+    key_gain_ref,
+    cosine_ref,
+    sine_ref,
+    stacked_ref,
+    packed_ref,
+):
+    count = tokens_ref.shape[0]
+    step = count // 4
+    gain = gain_ref[...]
+
+    def norm(number, carry):
+        start = pl.multiple_of(number * step, step)
+        part = pl.ds(start, step)
+        values = tokens_ref[part].astype(jnp.float32)
+        tangent = tangents_ref[part].astype(jnp.float32)
+        root = lax.rsqrt(jnp.mean(values * values, axis=1, keepdims=True) + epsilon)
+        slope = jnp.mean(values * tangent, axis=1, keepdims=True) * root * root * root
+        stacked_ref[part] = (values * root * gain).astype(jnp.bfloat16)
+        d_normed = (tangent * root - values * slope) * gain
+        stacked_ref[pl.ds(count + start, step)] = d_normed.astype(jnp.bfloat16)
+        return carry
+
+    lax.fori_loop(0, count // step, norm, 0)
+    stacked = stacked_ref[...]
+    width = w_key_ref.shape[1]
+    key = jnp.dot(stacked, w_key_ref[...], preferred_element_type=jnp.float32)
+    value = jnp.dot(stacked, w_value_ref[...], preferred_element_type=jnp.float32)
+    key, d_key = turned_pair(
+        key[:count], key[count:], key_gain_ref[...], cosine_ref[...], sine_ref[...]
+    )
+    for number, part in enumerate((key, d_key, value[:count], value[count:])):
+        packed_ref[:, number * width : (number + 1) * width] = part.astype(jnp.bfloat16)
+
+
+def keys_of(head, tokens, tangents, gain, w_key, w_value, key_gain, cosine, sine):
+    count, model_width = tokens.shape
+    width = key_gain.shape[1]
+    whole = lambda array: pl.BlockSpec(array.shape, lambda i, head: (0, 0))
+    column = pl.BlockSpec((model_width, width), lambda i, head: (0, head[0]))
     return pl.pallas_call(
-        norm_kernel,
-        grid=(count // rows,),
-        in_specs=[row_block, row_block, pl.BlockSpec((1, width), lambda i: (0, 0))],
-        out_specs=pl.BlockSpec((2, rows, width), lambda i: (0, i, 0)),
-        out_shape=jax.ShapeDtypeStruct((2, count, width), jnp.bfloat16),
-        name="norm_rows",
-    )(tokens, tangents, gain)
+        keys_kernel,
+        grid_spec=pltpu.PrefetchScalarGridSpec(
+            num_scalar_prefetch=1,
+            grid=(1,),
+            in_specs=[
+                whole(tokens),
+                whole(tangents),
+                whole(gain),
+                column,
+                column,
+                whole(key_gain),
+                whole(cosine),
+                whole(sine),
+            ],
+            out_specs=(
+                pl.BlockSpec((2 * count, model_width), lambda i, head: (0, 0)),
+                pl.BlockSpec((count, 4 * width), lambda i, head: (0, 0)),
+            ),
+        ),
+        out_shape=(
+            jax.ShapeDtypeStruct((2 * count, model_width), jnp.bfloat16),
+            jax.ShapeDtypeStruct((count, 4 * width), jnp.bfloat16),
+        ),
+        name="keys_of",
+    )(head, tokens, tangents, gain, w_key, w_value, key_gain, cosine, sine)
+
+
+def queries_kernel(moe_rows, stacked_ref, weight_ref, gain_ref, cosine_ref, sine_ref, out_ref):
+    count = stacked_ref.shape[0] // 2
+    width = gain_ref.shape[1]
+    heads = weight_ref.shape[1] // width
+    query_all = jnp.dot(stacked_ref[...], weight_ref[...], preferred_element_type=jnp.float32)
+    for head in range(heads):
+        column = query_all[:, head * width : (head + 1) * width]
+        query, d_query = turned_pair(
+            column[:count], column[count:], gain_ref[...], cosine_ref[...], sine_ref[...]
+        )
+        joint = jnp.concatenate([d_query, query], axis=1).astype(jnp.bfloat16)
+        for receiver in range(count // moe_rows):
+            start = (receiver * heads + head) * moe_rows
+            for copy in range(out_ref.shape[0]):
+                out_ref[copy, start : start + moe_rows] = joint[
+                    receiver * moe_rows : (receiver + 1) * moe_rows
+                ]
+
+
+def queries_of(stacked, weight, gain, cosine, sine, copies, moe_rows):
+    width = gain.shape[1]
+    rows = stacked.shape[0] // 2 * (weight.shape[1] // width)
+    return pl.pallas_call(
+        functools.partial(queries_kernel, moe_rows),
+        out_shape=jax.ShapeDtypeStruct((copies, rows, 2 * width), jnp.bfloat16),
+        name="queries_of",
+    )(stacked, weight, gain, cosine, sine)
 
 
 def table_of(refs, rows, number):
@@ -360,20 +430,23 @@
 
 
 def pack_kernel(experts, capacity, slot_rows, moe_rows, first_ref, *refs):
-    blocks, out_ref = refs[:-1], refs[-1]
+    blocks, out_ref, table_ref = refs[:-2], refs[-2], refs[-1]
     rows = 2 * moe_rows
     routes = table_of(blocks, rows, 0)
+    table_ref[:8] = routes
+    table_ref[8:] = table_of(blocks, rows, 1)
     chosen, _ = placing(first_ref[0], routes, experts, capacity, slot_rows, moe_rows)
     pick = jnp.concatenate([jnp.where(c, 1.0, 0.0) for c in chosen], axis=0).astype(jnp.bfloat16)
     source = jnp.concatenate([block[:rows] for block in blocks], axis=0)
     out_ref[...] = jnp.dot(pick, source, preferred_element_type=jnp.float32).astype(jnp.bfloat16)
 
 
-def mix_kernel(experts, capacity, slot_rows, moe_rows, first_ref, returned_ref, *refs):
-    tables, out_ref = refs[:-1], refs[-1]
-    routes = table_of(tables, 0, 0)
+def mix_kernel(
+    experts, capacity, slot_rows, moe_rows, first_ref, returned_ref, table_ref, out_ref
+):
+    routes = table_ref[:8]
     chosen, named = placing(first_ref[0], routes, experts, capacity, slot_rows, moe_rows)
-    shares = table_of(tables, 0, 1)
+    shares = table_ref[8:]
     share = jnp.zeros(named[0].shape, jnp.float32)
     for k, each in enumerate(named):
         share = share + jnp.where(each, jnp.broadcast_to(shares[k : k + 1], each.shape), 0.0)
@@ -394,43 +467,53 @@
     return pl.pallas_call(
         functools.partial(pack_kernel, experts, capacity, slot_rows, moe_rows),
         in_specs=[pl.BlockSpec(memory_space=pltpu.SMEM)] + [vmem] * len(blocks),
-        out_specs=vmem,
-        out_shape=jax.ShapeDtypeStruct((experts * slot_rows, blocks[0].shape[1]), jnp.bfloat16),
+        out_specs=(vmem, vmem),
+        out_shape=(
+            jax.ShapeDtypeStruct((experts * slot_rows, blocks[0].shape[1]), jnp.bfloat16),
+            jax.ShapeDtypeStruct((16, 2 * moe_rows * len(blocks)), jnp.float32),
+        ),
         compiler_params=pltpu.CompilerParams(vmem_limit_bytes=40 << 20),
         name="pack",
     )(first, *blocks)
 
 
-def mixed(first, returned, blocks, experts, capacity, slot_rows, moe_rows):
+def mixed(first, returned, table, experts, capacity, slot_rows, moe_rows):
     vmem = pl.BlockSpec(memory_space=pltpu.VMEM)
-    table = pl.BlockSpec((8, 256), lambda i: (2 * moe_rows // 8, 0))
-    rows = 2 * moe_rows * len(blocks)
     return pl.pallas_call(
         functools.partial(mix_kernel, experts, capacity, slot_rows, moe_rows),
-        grid=(1,),
-        in_specs=[
-            pl.BlockSpec(memory_space=pltpu.SMEM),
-            pl.BlockSpec(returned.shape, lambda i: (0, 0)),
-            *[table] * len(blocks),
-        ],
-        out_specs=pl.BlockSpec((rows, returned.shape[1]), lambda i: (0, 0)),
-        out_shape=jax.ShapeDtypeStruct((rows, returned.shape[1]), jnp.float32),
+        in_specs=[pl.BlockSpec(memory_space=pltpu.SMEM), vmem, vmem],
+        out_specs=vmem,
+        out_shape=jax.ShapeDtypeStruct((table.shape[1], returned.shape[1]), jnp.float32),
         compiler_params=pltpu.CompilerParams(vmem_limit_bytes=40 << 20),
         name="mixed",
-    )(first, returned, *blocks)
-
-
-def expert_kernel(rows_ref, gate_a, up_a, gate_b, up_b, down_a, down_b, out_ref, sum_ref, hidden_ref):
+    )(first, returned, table)
+
+
+def expert_kernel(rows_ref, *refs):
+    sources, out_ref, held, (sum_ref, hidden_ref, sems) = refs[:6], refs[6], refs[7:13], refs[13:]
+    down_a, down_b = held[4:]
     count, depth = rows_ref.shape
-    units = gate_a.shape[1]
+    units = held[0].shape[1]
     step = depth // 4
+
+    def copy(number, k):
+        part = pl.ds(pl.multiple_of(k * step, step), step)
+        return pltpu.make_async_copy(
+            sources[number].at[part], held[number].at[part], sems.at[number, k]
+        )
+
+    for numbers in (range(4), range(4, 6)):
+        for k in range(depth // step):
+            for number in numbers:
+                copy(number, k).start()
     sum_ref[...] = jnp.zeros_like(sum_ref)
 
     def contract(k, carry):
         part = pl.ds(pl.multiple_of(k * step, step), step)
-        for number, weight_ref in enumerate((gate_a, up_a, gate_b, up_b)):
+        for number in range(4):
+            copy(number, k).wait()
             sum_ref[number] += jnp.dot(
-                rows_ref[:, part], weight_ref[part], preferred_element_type=jnp.float32
+                rows_ref[:, part], held[number][part], preferred_element_type=jnp.float32
             )
         return carry
 
@@ -470,6 +553,8 @@
 
     def produce(n, carry):
         part = pl.ds(pl.multiple_of(n * step, step), step)
+        copy(4, n).wait()
+        copy(5, n).wait()
         across = (((1,), (1,)), ((), ()))
         result = lax.dot_general(
             hidden_ref[0], down_a[part], across, preferred_element_type=jnp.float32
@@ -484,13 +569,18 @@
 
 def expert_rows(rows, weights):
     gate, up, down, gate_other, up_other, down_other = weights
-    count, units = rows.shape[0], gate.shape[1]
+    count, (depth, units) = rows.shape[0], gate.shape
+    vmem, hbm = (pl.BlockSpec(memory_space=space) for space in (pltpu.VMEM, pl.ANY))
     return pl.pallas_call(
         expert_kernel,
+        in_specs=[vmem] + [hbm] * 6,
+        out_specs=vmem,
         out_shape=jax.ShapeDtypeStruct(rows.shape, jnp.bfloat16),
         scratch_shapes=[
+            *[pltpu.VMEM((depth, units), jnp.bfloat16)] * 6,
             pltpu.VMEM((4, count, units), jnp.float32),
             pltpu.VMEM((2, count, units), jnp.bfloat16),
+            pltpu.SemaphoreType.DMA((6, 4)),
         ],
         compiler_params=pltpu.CompilerParams(vmem_limit_bytes=56 << 20),
         name="expert_rows",
@@ -542,27 +632,21 @@
     plane_count = lax.axis_size("seq_0")
     first_pos = plane * plane_rows + row_in_plane * tok_count
     positions = first_pos + jnp.arange(tok_count, dtype=jnp.int32)
-    turns = turns_of(positions, head_width)
+    cosine, sine = turns_of(positions, head_width)
     kv_count = w_key.shape[1] // head_width
     devices_per_kv = lax.axis_size("head") // kv_count
-    kv_start = lax.axis_index("head") // devices_per_kv * head_width
-    key_cols = lax.dynamic_slice_in_dim(w_key, kv_start, head_width, 1)
-    value_cols = lax.dynamic_slice_in_dim(w_value, kv_start, head_width, 1)
-    stacked = norm_rows(tokens, tangents, attn_gain[None]).reshape(2 * tok_count, model_width)
-    kv_cols = jnp.concatenate([key_cols, value_cols], 1)
-    kv_all = jnp.dot(stacked, kv_cols, preferred_element_type=jnp.float32)
-    key_all = kv_all[:, :head_width].reshape(2, tok_count, 1, head_width)
-    value_all = kv_all[:, head_width:].reshape(2, tok_count, head_width)
-    key, d_key = head_pair(key_all[0], key_all[1], key_gain, turns)
-    packed = jnp.concatenate(
-        [
-            key.reshape(tok_count, head_width),
-            d_key.reshape(tok_count, head_width),
-            value_all[0],
-            value_all[1],
-        ],
-        1,
-    ).astype(jnp.bfloat16)
+    kv_head = (lax.axis_index("head") // devices_per_kv).astype(jnp.int32)[None]
+    stacked, packed = keys_of(
+        kv_head,
+        tokens,
+        tangents,
+        attn_gain[None],
+        w_key,
+        w_value,
+        key_gain[None],
+        cosine,
+        sine,
+    )
     blocks = ring_blocks(packed, "seq_0")
 
     top_count = routes.shape[1]
@@ -572,18 +656,9 @@
     tables = tables.reshape(top_count, 2 * 4 * moe_rows)
     tables = jnp.pad(tables, ((0, 0), (0, model_width - tables.shape[1])))
 
-    query_all = jnp.dot(stacked, w_query, preferred_element_type=jnp.float32)
-    query_all = query_all.reshape(2, tok_count, heads_here, head_width)
-    query, d_query = head_pair(query_all[0], query_all[1], query_gain, turns)
-
-    def by_receiver(values):
-        values = values.astype(jnp.bfloat16).reshape(head_count, moe_rows, heads_here, head_width)
-        return jnp.transpose(values, (0, 2, 1, 3)).reshape(tok_count * heads_here, head_width)
-
-    joint_own = jnp.concatenate([by_receiver(d_query), by_receiver(query)], 1)
-    own_rows = joint_own.shape[0]
     row_groups = lax.axis_size("seq_1")
-    copies = jnp.broadcast_to(joint_own[None], (row_groups, own_rows, 2 * head_width))
+    copies = queries_of(stacked, w_query, query_gain[None], cosine, sine, row_groups, moe_rows)
+    own_rows = copies.shape[1]
     joint_query = lax.all_to_all(copies, "seq_1", 0, 0, tiled=True)
     joint_query = joint_query.reshape(row_groups * own_rows, 2 * head_width)
     order = sorted(blocks)
@@ -632,20 +707,20 @@
     slot_rows = 2 * capacity * len(near)
     layout = (plane_experts, capacity, slot_rows, moe_rows)
 
-    results = []
-    for group in (near, far):
-        outgoing = pack(first_expert, [gathered[k] for k in group], *layout)
+    results, lists = [], {}
+    for name, group in (("near", near), ("far", far)):
+        outgoing, lists[name] = pack(first_expert, [gathered[k] for k in group], *layout)
         outgoing = outgoing.reshape(plane_experts, slot_rows, model_width)
         received = lax.all_to_all(outgoing, ("seq_1", "head"), 0, 0, tiled=True)
         results.append(
             expert_rows(received.reshape(plane_experts * slot_rows, model_width), expert_halves)
         )
     share_of = {}
-    for group, result in ((far, results[1]), (near, results[0])):
+    for name, group, result in (("far", far, results[1]), ("near", near, results[0])):
         result = result.reshape(plane_experts, slot_rows, model_width)
         returned = lax.all_to_all(result, ("seq_1", "head"), 0, 0, tiled=True)
         returned = returned.reshape(plane_experts * slot_rows, model_width)
-        sums = mixed(first_expert, returned, [gathered[k] for k in group], *layout)
+        sums = mixed(first_expert, returned, lists[name], *layout)
         sums = sums.reshape(len(group), block_rows, model_width)
         for number, k in enumerate(group):
             share_of[k] = sums[number]

time: 281 us -> 281 us (level)
  waiting for transfers between devices: 106 us -> 133 us
  local copies, waits for them, and re-layouts: 18.1 us -> 4.18 us
  starting transfers between devices: 91.5 us -> 81.6 us
  other arithmetic: 4.61 us -> 1.72 us
    ppermute x1, waiting for transfers between devices: 5.54 us -> 32.2 us  [layer(): near_own = lax.ppermute(w_out, ('dp', 'head'), sides)]
    unnamed x41 -> x18, local copies, waits for them, and re-layouts: 11.6 us -> 0.81 us
    ppermute x1, starting transfers between devices: 17.6 us -> 9.32 us  [layer(): near_other = lax.ppermute(near_own, 'dp', other_core)]
    pallas_call x3 -> x4, Pallas kernels: 28.7 us -> 33.1 us  [the longest x2 25.6 us: expert_rows(): pl.pallas_call(expert_kernel, in_specs=[vmem] + [hbm] * 6, out_specs=vmem...]
    all_to_all x2, waiting for transfers between devices: 5.22 us -> 9.43 us  [layer(): returned = lax.all_to_all(result, ('seq_1', 'head'), 0, 0, tiled=True)]
    ppermute x22, starting transfers between devices: 33.7 us -> 29.7 us  [shifted(): lax.ppermute(array, axis, [(i, (i + offset) % size) for i in range(size)])]
    pallas_call x2, Pallas kernels: 4.82 us -> 1.87 us  [mixed(): pl.pallas_call(functools.partial(mix_kernel, experts, capacity, slot_rows...]
  transfers between devices with their start and end apart: 34 -> 34, of which waited for: 21 -> 20; matrix products, arithmetic and copies ran while one was open for 5% -> 1% of each run, Pallas kernels for 17% -> 18%
where the time goes in v1:
time: 281 us; the launch traced here: 280 us
  waiting for transfers between devices  133 us (47%)
  starting transfers between devices  81.6 us (29%)
  Pallas kernels  58.1 us (21%)
  local copies, waits for them, and re-layouts  4.18 us (1%)
    ppermute x22, waiting for transfers between devices, shifted(): lax.ppermute(array, axis, [(i, (i + offset) % size) for i in range(size)])  64.4 us
    ppermute x1, waiting for transfers between devices, layer(): near_own = lax.ppermute(w_out, ('dp', 'head'), sides)  32.2 us
    ppermute x22, starting transfers between devices, shifted(): lax.ppermute(array, axis, [(i, (i + offset) % size) for i in range(size)])  29.7 us
    pallas_call x2, Pallas kernels, expert_rows(): pl.pallas_call(expert_kernel, in_specs=[vmem] + [hbm] * 6, out_specs=vmem...  25.6 us
    all_to_all x2, waiting for transfers between devices, layer(): received = lax.all_to_all(outgoing, ('seq_1', 'head'), 0, 0, tiled=True)  15.6 us
    all_to_all x2, starting transfers between devices, layer(): received = lax.all_to_all(outgoing, ('seq_1', 'head'), 0, 0, tiled=True)  14 us
    pallas_call x1, Pallas kernels, attend(): pl.pallas_call(functools.partial(attend_kernel, (width // 2) ** (-0.5), g...  12.4 us
    all_to_all x1, waiting for transfers between devices, layer(): arrived = lax.all_to_all(sent, ('seq_1', 'head'), 0, 0, tiled=True)  11.8 us
  transfers between devices with their start and end apart: 34, of which 20 were waited for; matrix products, arithmetic and copies ran while one was open for 1% of the time, Pallas kernels for 18%

profile of v1, /device:TPU:8, one launch (start us, length us, event | category | flops | bytes accessed | tf_op | source)
XLA Modules:
  0.0 279.9 jit_solution(14089835233301105159)
XLA Ops:
  0.6 1.6 collective-permute-start.7
  2.2 2.4 constant_dynamic-slice_fusion
  4.6 2.7 collective-permute-start.9
  7.3 32.2 %collective-permute-done.7.w_near_own = bf16[512,2048]{1,0:T(8,128)(2,1)} collective-permute-done((bf16[512,2048]{1,0:T(8,128)(2,1)}, bf16[512,2048]{1,0:T(8,128)(2,1)}, u32[]{:S(2)}, u32[]{:S(2)}) %collective-permute-start.7) | collective-permute-done | bytes 2097184 | tf_op jit(solution)/shard_map/ppermute | solution.py:620
  39.5 9.3 %collective-permute-start.8 = (bf16[512,2048]{1,0:T(8,128)(2,1)}, bf16[512,2048]{1,0:T(8,128)(2,1)}, u32[]{:S(2)}, u32[]{:S(2)}) collective-permute-start(bf16[512,2048]{1,0:T(8,128)(2,1)} %collective-permute-done.7.w_near_own), channel_id=1, source_target_pairs={{0,128},{128,0},{1,129},{129,1},{2,130},{130,2},{3,131},{131,3},{4... | collective-permute-start | bytes 6291464 | tf_op jit(solution)/shard_map/ppermute | solution.py:622
  49.9 3.6 %keys_of.1 = (bf16[256,2048]{1,0:T(8,128)(2,1)}, bf16[128,512]{1,0:T(8,128)(2,1)}) custom-call(s32[1]{0:T(128)} %bitcast.13.head_ref, bf16[128,2048]{1,0:T(8,128)(2,1)} %tokens_ref.3, bf16[128,2048]{1,0:T(8,128)(2,1)} %tangents_ref.3, f32[1,2048]{1,0:T(1,128)} %bitcast.54, bf16[2048,256]{1,0:T(8,128)(2,1)} %w_key_ref.1, bf16[2048,256]{1,0:T(8,128)(2,1)} %w_value_ref.1, ...), custom_call_target="tpu_custom_call" | custom-call | tf_op jit(solution)/shard_map/keys_of/pallas_call | solution.py:337
  53.5 3.9 %queries_of.1 = bf16[4,512,256]{2,1,0:T(8,128)(2,1)} custom-call(bf16[256,2048]{1,0:T(8,128)(2,1)} %get-tuple-element.10.stacked_ref, bf16[2048,512]{1,0:T(8,128)(2,1)} %weight_ref.1, f32[1,128]{1,0:T(1,128)} %bitcast.56, f32[128,128]{1,0:T(8,128)} %get-tuple-element.29.cosine_ref, f32[128,128]{1,0:T(8,128)} %get-tuple-element.30.sine_ref), custom_call_target="tpu_custom_call" | custom-call | tf_op jit(solution)/shard_map/queries_of/pallas_call | solution.py:387
  57.4 7.7 %all-to-all-start = ((bf16[4,512,256]{2,1,0:T(8,128)(2,1)}), bf16[4,512,256]{2,1,0:T(8,128)(2,1)S(1)}, u32[]{:S(2)}, u32[]{:S(2)}) async-start(bf16[4,512,256]{2,1,0:T(8,128)(2,1)} %queries_of.1), calls=%async_computation | async-start | bytes 2097152 | tf_op jit(solution)/shard_map/all_to_all | solution.py:662
  65.1 3.2 %collective-permute-start.4 = (bf16[128,512]{1,0:T(8,128)(2,1)S(1)}, bf16[128,512]{1,0:T(8,128)(2,1)S(1)}, u32[]{:S(2)}, u32[]{:S(2)}) collective-permute-start(bf16[128,512]{1,0:T(8,128)(2,1)S(1)} %copy-done.4), channel_id=1, source_target_pairs={{0,112},{16,0},{32,16},{48,32},{64,48},{80,64},{96,80},{112,96},{1... | collective-permute-start | bytes 393224 | tf_op jit(solution)/shard_map/ppermute | solution.py:33
  68.3 3.6 %collective-permute-done.refs_3_ = bf16[128,512]{1,0:T(8,128)(2,1)S(1)} collective-permute-done((bf16[128,512]{1,0:T(8,128)(2,1)S(1)}, bf16[128,512]{1,0:T(8,128)(2,1)S(1)}, u32[]{:S(2)}, u32[]{:S(2)}) %collective-permute-start) | collective-permute-done | bytes 131104 | tf_op jit(solution)/shard_map/ppermute | solution.py:33
  71.9 3.2 %collective-permute-start.5 = (bf16[128,512]{1,0:T(8,128)(2,1)S(1)}, bf16[128,512]{1,0:T(8,128)(2,1)S(1)}, u32[]{:S(2)}, u32[]{:S(2)}) collective-permute-start(bf16[128,512]{1,0:T(8,128)(2,1)S(1)} %collective-permute-done.4.refs_5_), channel_id=1, source_target_pairs={{0,112},{16,0},{32,16},{48,32},{64,48},{80,64},{96,80},{112,96},{1... | collective-permute-start | bytes 393224 | tf_op jit(solution)/shard_map/ppermute | solution.py:33
  75.2 2.9 %collective-permute-done.1.refs_2_ = bf16[128,512]{1,0:T(8,128)(2,1)S(1)} collective-permute-done((bf16[128,512]{1,0:T(8,128)(2,1)S(1)}, bf16[128,512]{1,0:T(8,128)(2,1)S(1)}, u32[]{:S(2)}, u32[]{:S(2)}) %collective-permute-start.1) | collective-permute-done | bytes 131104 | tf_op jit(solution)/shard_map/ppermute | solution.py:33
  78.1 3.2 %collective-permute-start.6 = (bf16[128,512]{1,0:T(8,128)(2,1)S(1)}, bf16[128,512]{1,0:T(8,128)(2,1)S(1)}, u32[]{:S(2)}, u32[]{:S(2)}) collective-permute-start(bf16[128,512]{1,0:T(8,128)(2,1)S(1)} %collective-permute-done.5.refs_6_), channel_id=1, source_target_pairs={{0,112},{16,0},{32,16},{48,32},{64,48},{80,64},{96,80},{112,96},{1... | collective-permute-start | bytes 393224 | tf_op jit(solution)/shard_map/ppermute | solution.py:33
  81.3 2.9 %collective-permute-done.2.refs_1_ = bf16[128,512]{1,0:T(8,128)(2,1)S(1)} collective-permute-done((bf16[128,512]{1,0:T(8,128)(2,1)S(1)}, bf16[128,512]{1,0:T(8,128)(2,1)S(1)}, u32[]{:S(2)}, u32[]{:S(2)}) %collective-permute-start.2) | collective-permute-done | bytes 131104 | tf_op jit(solution)/shard_map/ppermute | solution.py:33
  84.4 6.0 %collective-permute-done.3.refs_0_ = bf16[128,512]{1,0:T(8,128)(2,1)S(1)} collective-permute-done((bf16[128,512]{1,0:T(8,128)(2,1)S(1)}, bf16[128,512]{1,0:T(8,128)(2,1)S(1)}, u32[]{:S(2)}, u32[]{:S(2)}) %collective-permute-start.3) | collective-permute-done | bytes 131104 | tf_op jit(solution)/shard_map/ppermute | solution.py:33
  90.5 12.4 %attend.1 = bf16[16,136,256]{2,1,0:T(8,128)(2,1)} custom-call(s32[8]{0:T(128)S(1)} %stack.68.span_ref, bf16[2048,256]{1,0:T(8,128)(2,1)S(1)} %bitcast.41, bf16[128,512]{1,0:T(8,128)(2,1)S(1)} %collective-permute-done.3.refs_0_, bf16[128,512]{1,0:T(8,128)(2,1)S(1)} %collective-permute-done.2.refs_1_, bf16[128,512]{1,0:T(8,128)(2,1)S(1)} %collective-permute-done.1.refs_2_, ...), custom_call_target="tpu_custom_call" | custom-call | tf_op jit(solution)/shard_map/attend/pallas_call | solution.py:139
  102.9 7.2 %all-to-all-start.1 = ((bf16[16,136,256]{2,1,0:T(8,128)(2,1)}), bf16[16,136,256]{2,1,0:T(8,128)(2,1)S(1)}, u32[]{:S(2)}, u32[]{:S(2)}) async-start(bf16[16,136,256]{2,1,0:T(8,128)(2,1)} %attend.1), calls=%async_computation.1 | async-start | bytes 2228224 | tf_op jit(solution)/shard_map/all_to_all | solution.py:677
  110.4 11.8 %all-to-all-done.1.arrived_ref = bf16[16,136,256]{2,1,0:T(8,128)(2,1)S(1)} async-done(((bf16[16,136,256]{2,1,0:T(8,128)(2,1)}), bf16[16,136,256]{2,1,0:T(8,128)(2,1)S(1)}, u32[]{:S(2)}, u32[]{:S(2)}) %all-to-all-start.1) | async-done | bytes 1114144 | tf_op jit(solution)/shard_map/all_to_all | solution.py:677
  122.3 6.8 %merge.1 = (f32[64,2048]{1,0:T(8,128)S(1)}, bf16[72,2048]{1,0:T(8,128)(2,1)S(1)}) custom-call(s32[5]{0:T(128)S(1)} %stack.59.place_ref, bf16[16,136,256]{2,1,0:T(8,128)(2,1)S(1)} %all-to-all-done.1.arrived_ref, bf16[128,2048]{1,0:T(8,128)(2,1)S(1)} %copy-done, bf16[128,2048]{1,0:T(8,128)(2,1)S(1)} %copy-done.1, f32[1,2048]{1,0:T(1,128)S(1)} %bitcast.42, ...), custom_call_target="tpu_custom_call" | custom-call | tf_op jit(solution)/shard_map/merge/pallas_call | solution.py:262
  129.1 0.8 copy-done.2
  129.8 3.2 %collective-permute-start.11 = (bf16[72,2048]{1,0:T(8,128)(2,1)S(1)}, bf16[72,2048]{1,0:T(8,128)(2,1)S(1)}, u32[]{:S(2)}, u32[]{:S(2)}) collective-permute-start(bf16[72,2048]{1,0:T(8,128)(2,1)S(1)} %get-tuple-element.13.refs_0_), channel_id=1, source_target_pairs={{0,112},{16,0},{32,16},{48,32},{64,48},{80,64},{96,80},{112,96},{1... | collective-permute-start | bytes 884744 | tf_op jit(solution)/shard_map/ppermute | solution.py:33
  133.1 5.8 %collective-permute-done.12.refs_2_ = bf16[72,2048]{1,0:T(8,128)(2,1)S(1)} collective-permute-done((bf16[72,2048]{1,0:T(8,128)(2,1)S(1)}, bf16[72,2048]{1,0:T(8,128)(2,1)S(1)}, u32[]{:S(2)}, u32[]{:S(2)}) %collective-permute-start.12) | collective-permute-done | bytes 294944 | tf_op jit(solution)/shard_map/ppermute | solution.py:33
  138.8 3.5 %collective-permute-start.13 = (bf16[72,2048]{1,0:T(8,128)(2,1)S(1)}, bf16[72,2048]{1,0:T(8,128)(2,1)S(1)}, u32[]{:S(2)}, u32[]{:S(2)}) collective-permute-start(bf16[72,2048]{1,0:T(8,128)(2,1)S(1)} %collective-permute-done.11.refs_1_), channel_id=1, source_target_pairs={{0,112},{16,0},{32,16},{48,32},{64,48},{80,64},{96,80},{112,96},{1... | collective-permute-start | bytes 884744 | tf_op jit(solution)/shard_map/ppermute | solution.py:33
  142.3 6.6 %collective-permute-done.17.refs_0_ = bf16[72,2048]{1,0:T(8,128)(2,1)S(1)} collective-permute-done((bf16[72,2048]{1,0:T(8,128)(2,1)S(1)}, bf16[72,2048]{1,0:T(8,128)(2,1)S(1)}, u32[]{:S(2)}, u32[]{:S(2)}) %collective-permute-start.17) | collective-permute-done | bytes 294944 | tf_op jit(solution)/shard_map/ppermute | solution.py:33
  149.1 3.7 %collective-permute-start.18 = (bf16[72,2048]{1,0:T(8,128)(2,1)S(1)}, bf16[72,2048]{1,0:T(8,128)(2,1)S(1)}, u32[]{:S(2)}, u32[]{:S(2)}) collective-permute-start(bf16[72,2048]{1,0:T(8,128)(2,1)S(1)} %collective-permute-done.13.refs_3_), channel_id=1, source_target_pairs={{0,112},{16,0},{32,16},{48,32},{64,48},{80,64},{96,80},{112,96},{1... | collective-permute-start | bytes 884744 | tf_op jit(solution)/shard_map/ppermute | solution.py:33
  152.8 7.1 %collective-permute-done.19.refs_2_ = bf16[72,2048]{1,0:T(8,128)(2,1)S(1)} collective-permute-done((bf16[72,2048]{1,0:T(8,128)(2,1)S(1)}, bf16[72,2048]{1,0:T(8,128)(2,1)S(1)}, u32[]{:S(2)}, u32[]{:S(2)}) %collective-permute-start.19) | collective-permute-done | bytes 294944 | tf_op jit(solution)/shard_map/ppermute | solution.py:33
  159.9 7.9 %collective-permute-done.20.refs_3_ = bf16[72,2048]{1,0:T(8,128)(2,1)S(1)} collective-permute-done((bf16[72,2048]{1,0:T(8,128)(2,1)S(1)}, bf16[72,2048]{1,0:T(8,128)(2,1)S(1)}, u32[]{:S(2)}, u32[]{:S(2)}) %collective-permute-start.20) | collective-permute-done | bytes 294944 | tf_op jit(solution)/shard_map/ppermute | solution.py:33
  167.8 1.9 pack.3
  169.7 7.6 %all-to-all-start.4 = ((bf16[16,24,2048]{2,1,0:T(8,128)(2,1)}), bf16[16,24,2048]{2,1,0:T(8,128)(2,1)}, u32[]{:S(2)}, u32[]{:S(2)}) async-start(bf16[16,24,2048]{2,1,0:T(8,128)(2,1)} %bitcast.31), calls=%async_computation.4 | async-start | bytes 3145728 | tf_op jit(solution)/shard_map/all_to_all | solution.py:714
  178.0 1.9 pack.2
  180.0 12.8 %all-to-all-done.4 = bf16[16,24,2048]{2,1,0:T(8,128)(2,1)} async-done(((bf16[16,24,2048]{2,1,0:T(8,128)(2,1)}), bf16[16,24,2048]{2,1,0:T(8,128)(2,1)}, u32[]{:S(2)}, u32[]{:S(2)}) %all-to-all-start.4) | async-done | bytes 1572896 | tf_op jit(solution)/shard_map/all_to_all | solution.py:714
  192.8 6.5 %all-to-all-start.2 = ((bf16[16,24,2048]{2,1,0:T(8,128)(2,1)}), bf16[16,24,2048]{2,1,0:T(8,128)(2,1)}, u32[]{:S(2)}, u32[]{:S(2)}) async-start(bf16[16,24,2048]{2,1,0:T(8,128)(2,1)} %bitcast.24), calls=%async_computation.2 | async-start | bytes 3145728 | tf_op jit(solution)/shard_map/all_to_all | solution.py:714
  199.2 12.8 %expert_rows.3 = bf16[384,2048]{1,0:T(8,128)(2,1)} custom-call(bf16[384,2048]{1,0:T(8,128)(2,1)} %bitcast.32.rows_ref, bf16[2048,384]{1,0:T(8,128)(2,1)} %bitcast.43, bf16[2048,384]{1,0:T(8,128)(2,1)} %bitcast.47, bf16[2048,384]{1,0:T(8,128)(2,1)} %collective-permute-done.14.refs_2_, bf16[2048,384]{1,0:T(8,128)(2,1)} %collective-permute-done.15.refs_3_, ...), custom_call_target="tpu_custom_call" | custom-call | tf_op jit(solution)/shard_map/expert_rows/pallas_call | solution.py:574
  212.1 2.8 all-to-all-done.2
  214.9 5.7 %all-to-all-start.5 = ((bf16[16,24,2048]{2,1,0:T(8,128)(2,1)}), bf16[16,24,2048]{2,1,0:T(8,128)(2,1)S(1)}, u32[]{:S(2)}, u32[]{:S(2)}) async-start(bf16[16,24,2048]{2,1,0:T(8,128)(2,1)} %bitcast.53), calls=%async_computation.5 | async-start | bytes 3145728 | tf_op jit(solution)/shard_map/all_to_all | solution.py:721
  220.5 12.8 %expert_rows.2 = bf16[384,2048]{1,0:T(8,128)(2,1)} custom-call(bf16[384,2048]{1,0:T(8,128)(2,1)} %bitcast.25.rows_ref, bf16[2048,384]{1,0:T(8,128)(2,1)} %bitcast.44, bf16[2048,384]{1,0:T(8,128)(2,1)} %bitcast.48, bf16[2048,384]{1,0:T(8,128)(2,1)} %collective-permute-done.14.refs_2_, bf16[2048,384]{1,0:T(8,128)(2,1)} %collective-permute-done.15.refs_3_, ...), custom_call_target="tpu_custom_call" | custom-call | tf_op jit(solution)/shard_map/expert_rows/pallas_call | solution.py:574
  233.4 3.6 %all-to-all-done.5 = bf16[16,24,2048]{2,1,0:T(8,128)(2,1)S(1)} async-done(((bf16[16,24,2048]{2,1,0:T(8,128)(2,1)}), bf16[16,24,2048]{2,1,0:T(8,128)(2,1)S(1)}, u32[]{:S(2)}, u32[]{:S(2)}) %all-to-all-start.5) | async-done | bytes 1572896 | tf_op jit(solution)/shard_map/all_to_all | solution.py:721
  237.0 5.6 %all-to-all-start.3 = ((bf16[16,24,2048]{2,1,0:T(8,128)(2,1)}), bf16[16,24,2048]{2,1,0:T(8,128)(2,1)S(1)}, u32[]{:S(2)}, u32[]{:S(2)}) async-start(bf16[16,24,2048]{2,1,0:T(8,128)(2,1)} %bitcast.52), calls=%async_computation.3 | async-start | bytes 3145728 | tf_op jit(solution)/shard_map/all_to_all | solution.py:721
  242.6 0.9 mixed.3
  243.8 3.2 %collective-permute-start.25 = (bf16[64,2048]{1,0:T(8,128)(2,1)S(1)}, bf16[64,2048]{1,0:T(8,128)(2,1)S(1)}, u32[]{:S(2)}, u32[]{:S(2)}) collective-permute-start(bf16[64,2048]{1,0:T(8,128)(2,1)S(1)} %get-tuple-element.23), channel_id=1, source_target_pairs={{0,112},{16,0},{32,16},{48,32},{64,48},{80,64},{96,80},{112,96},{1... | collective-permute-start | bytes 786440 | tf_op jit(solution)/shard_map/ppermute | solution.py:33
  247.1 5.3 %collective-permute-done.21 = bf16[64,2048]{1,0:T(8,128)(2,1)S(1)} collective-permute-done((bf16[64,2048]{1,0:T(8,128)(2,1)S(1)}, bf16[64,2048]{1,0:T(8,128)(2,1)S(1)}, u32[]{:S(2)}, u32[]{:S(2)}) %collective-permute-start.21) | collective-permute-done | bytes 262176 | tf_op jit(solution)/shard_map/ppermute | solution.py:33
  252.5 5.8 %all-to-all-done.3 = bf16[16,24,2048]{2,1,0:T(8,128)(2,1)S(1)} async-done(((bf16[16,24,2048]{2,1,0:T(8,128)(2,1)}), bf16[16,24,2048]{2,1,0:T(8,128)(2,1)S(1)}, u32[]{:S(2)}, u32[]{:S(2)}) %all-to-all-start.3) | async-done | bytes 1572896 | tf_op jit(solution)/shard_map/all_to_all | solution.py:721
  258.4 0.9 mixed.2
  259.4 2.8 %collective-permute-done.22 = bf16[64,2048]{1,0:T(8,128)(2,1)S(1)} collective-permute-done((bf16[64,2048]{1,0:T(8,128)(2,1)S(1)}, bf16[64,2048]{1,0:T(8,128)(2,1)S(1)}, u32[]{:S(2)}, u32[]{:S(2)}) %collective-permute-start.22) | collective-permute-done | bytes 262176 | tf_op jit(solution)/shard_map/ppermute | solution.py:33
  262.4 4.6 %collective-permute-done.26 = bf16[64,2048]{1,0:T(8,128)(2,1)S(1)} collective-permute-done((bf16[64,2048]{1,0:T(8,128)(2,1)S(1)}, bf16[64,2048]{1,0:T(8,128)(2,1)S(1)}, u32[]{:S(2)}, u32[]{:S(2)}) %collective-permute-start.26) | collective-permute-done | bytes 262176 | tf_op jit(solution)/shard_map/ppermute | solution.py:33
  267.0 4.3 %collective-permute-done.23 = bf16[64,2048]{1,0:T(8,128)(2,1)S(1)} collective-permute-done((bf16[64,2048]{1,0:T(8,128)(2,1)S(1)}, bf16[64,2048]{1,0:T(8,128)(2,1)S(1)}, u32[]{:S(2)}, u32[]{:S(2)}) %collective-permute-start.23) | collective-permute-done | bytes 262176 | tf_op jit(solution)/shard_map/ppermute | solution.py:33
  271.5 3.2 %collective-permute-start.27 = (bf16[64,2048]{1,0:T(8,128)(2,1)S(1)}, bf16[64,2048]{1,0:T(8,128)(2,1)S(1)}, u32[]{:S(2)}, u32[]{:S(2)}) collective-permute-start(bf16[64,2048]{1,0:T(8,128)(2,1)S(1)} %get-tuple-element.19), channel_id=1, source_target_pairs={{0,112},{16,0},{32,16},{48,32},{64,48},{80,64},{96,80},{112,96},{1... | collective-permute-start | bytes 786440 | tf_op jit(solution)/shard_map/ppermute | solution.py:33
  274.7 4.3 %collective-permute-done.24 = bf16[64,2048]{1,0:T(8,128)(2,1)S(1)} collective-permute-done((bf16[64,2048]{1,0:T(8,128)(2,1)S(1)}, bf16[64,2048]{1,0:T(8,128)(2,1)S(1)}, u32[]{:S(2)}, u32[]{:S(2)}) %collective-permute-start.24) | collective-permute-done | bytes 262176 | tf_op jit(solution)/shard_map/ppermute | solution.py:33
  (69 shorter events, 4.0 us)
Async XLA Ops:
  0.6 38.9 %collective-permute-start.7 = (bf16[512,2048]{1,0:T(8,128)(2,1)}, bf16[512,2048]{1,0:T(8,128)(2,1)}, u32[]{:S(2)}, u32[]{:S(2)}) collective-permute-start(bf16[512,2048]{1,0:T(8,128)(2,1)} %w_own.1), channel_id=1, source_target_pairs={{0,1},{1,2},{2,3},{3,0},{128,131},{129,128},{130,129},{131,130},{4... | collective-permute-start | bytes 6291464 | tf_op jit(solution)/shard_map/ppermute | solution.py:620
  4.6 79.7 %collective-permute-start.9 = (bf16[256,2048]{1,0:T(8,128)(2,1)}, bf16[256,2048]{1,0:T(8,128)(2,1)S(1)}, u32[]{:S(2)}, u32[]{:S(2)}) collective-permute-start(bf16[256,2048]{1,0:T(8,128)(2,1)} %constant_dynamic-slice_fusion), channel_id=1, source_target_pairs={{0,2},{1,3},{2,0},{3,1},{4,6},{5,7},{6,4},{7,5},{8,10},{9,11},{10,... | collective-permute-start | bytes 3145736 | tf_op jit(solution)/shard_map/ppermute | solution.py:33
  39.5 82.7 %collective-permute-start.8 = (bf16[512,2048]{1,0:T(8,128)(2,1)}, bf16[512,2048]{1,0:T(8,128)(2,1)}, u32[]{:S(2)}, u32[]{:S(2)}) collective-permute-start(bf16[512,2048]{1,0:T(8,128)(2,1)} %collective-permute-done.7.w_near_own), channel_id=1, source_target_pairs={{0,128},{128,0},{1,129},{129,1},{2,130},{130,2},{3,131},{131,3},{4... | collective-permute-start | bytes 6291464 | tf_op jit(solution)/shard_map/ppermute | solution.py:622
  57.4 7.7 %copy-start.4 = (bf16[128,512]{1,0:T(8,128)(2,1)S(1)}, bf16[128,512]{1,0:T(8,128)(2,1)}, u32[]{:S(2)}) copy-start(bf16[128,512]{1,0:T(8,128)(2,1)} %get-tuple-element.11.refs_4_) | copy-start | bytes 393220
  57.4 33.1 %all-to-all-start = ((bf16[4,512,256]{2,1,0:T(8,128)(2,1)}), bf16[4,512,256]{2,1,0:T(8,128)(2,1)S(1)}, u32[]{:S(2)}, u32[]{:S(2)}) async-start(bf16[4,512,256]{2,1,0:T(8,128)(2,1)} %queries_of.1), calls=%async_computation | async-start | bytes 2097152 | tf_op jit(solution)/shard_map/all_to_all | solution.py:662
  65.1 6.8 %collective-permute-start = (bf16[128,512]{1,0:T(8,128)(2,1)S(1)}, bf16[128,512]{1,0:T(8,128)(2,1)S(1)}, u32[]{:S(2)}, u32[]{:S(2)}) collective-permute-start(bf16[128,512]{1,0:T(8,128)(2,1)S(1)} %copy-done.4), channel_id=1, source_target_pairs={{0,16},{16,32},{32,48},{48,64},{64,80},{80,96},{96,112},{112,0},{1... | collective-permute-start | bytes 393224 | tf_op jit(solution)/shard_map/ppermute | solution.py:33
  65.1 6.8 %collective-permute-start.4 = (bf16[128,512]{1,0:T(8,128)(2,1)S(1)}, bf16[128,512]{1,0:T(8,128)(2,1)S(1)}, u32[]{:S(2)}, u32[]{:S(2)}) collective-permute-start(bf16[128,512]{1,0:T(8,128)(2,1)S(1)} %copy-done.4), channel_id=1, source_target_pairs={{0,112},{16,0},{32,16},{48,32},{64,48},{80,64},{96,80},{112,96},{1... | collective-permute-start | bytes 393224 | tf_op jit(solution)/shard_map/ppermute | solution.py:33
  71.9 6.2 %collective-permute-start.1 = (bf16[128,512]{1,0:T(8,128)(2,1)S(1)}, bf16[128,512]{1,0:T(8,128)(2,1)S(1)}, u32[]{:S(2)}, u32[]{:S(2)}) collective-permute-start(bf16[128,512]{1,0:T(8,128)(2,1)S(1)} %collective-permute-done.refs_3_), channel_id=1, source_target_pairs={{0,16},{16,32},{32,48},{48,64},{64,80},{80,96},{96,112},{112,0},{1... | collective-permute-start | bytes 393224 | tf_op jit(solution)/shard_map/ppermute | solution.py:33
  71.9 6.2 %collective-permute-start.5 = (bf16[128,512]{1,0:T(8,128)(2,1)S(1)}, bf16[128,512]{1,0:T(8,128)(2,1)S(1)}, u32[]{:S(2)}, u32[]{:S(2)}) collective-permute-start(bf16[128,512]{1,0:T(8,128)(2,1)S(1)} %collective-permute-done.4.refs_5_), channel_id=1, source_target_pairs={{0,112},{16,0},{32,16},{48,32},{64,48},{80,64},{96,80},{112,96},{1... | collective-permute-start | bytes 393224 | tf_op jit(solution)/shard_map/ppermute | solution.py:33
  78.1 6.2 %collective-permute-start.2 = (bf16[128,512]{1,0:T(8,128)(2,1)S(1)}, bf16[128,512]{1,0:T(8,128)(2,1)S(1)}, u32[]{:S(2)}, u32[]{:S(2)}) collective-permute-start(bf16[128,512]{1,0:T(8,128)(2,1)S(1)} %collective-permute-done.1.refs_2_), channel_id=1, source_target_pairs={{0,16},{16,32},{32,48},{48,64},{64,80},{80,96},{96,112},{112,0},{1... | collective-permute-start | bytes 393224 | tf_op jit(solution)/shard_map/ppermute | solution.py:33
  78.1 6.3 %collective-permute-start.6 = (bf16[128,512]{1,0:T(8,128)(2,1)S(1)}, bf16[128,512]{1,0:T(8,128)(2,1)S(1)}, u32[]{:S(2)}, u32[]{:S(2)}) collective-permute-start(bf16[128,512]{1,0:T(8,128)(2,1)S(1)} %collective-permute-done.5.refs_6_), channel_id=1, source_target_pairs={{0,112},{16,0},{32,16},{48,32},{64,48},{80,64},{96,80},{112,96},{1... | collective-permute-start | bytes 393224 | tf_op jit(solution)/shard_map/ppermute | solution.py:33
  84.3 6.2 %collective-permute-start.3 = (bf16[128,512]{1,0:T(8,128)(2,1)S(1)}, bf16[128,512]{1,0:T(8,128)(2,1)S(1)}, u32[]{:S(2)}, u32[]{:S(2)}) collective-permute-start(bf16[128,512]{1,0:T(8,128)(2,1)S(1)} %collective-permute-done.2.refs_1_), channel_id=1, source_target_pairs={{0,16},{16,32},{32,48},{48,64},{64,80},{80,96},{96,112},{112,0},{1... | collective-permute-start | bytes 393224 | tf_op jit(solution)/shard_map/ppermute | solution.py:33
  84.3 37.9 %collective-permute-start.10 = (bf16[256,2048]{1,0:T(8,128)(2,1)S(1)}, bf16[256,2048]{1,0:T(8,128)(2,1)}, u32[]{:S(2)}, u32[]{:S(2)}) collective-permute-start(bf16[256,2048]{1,0:T(8,128)(2,1)S(1)} %collective-permute-done.9.w_far_own), channel_id=1, source_target_pairs={{0,128},{128,0},{1,129},{129,1},{2,130},{130,2},{3,131},{131,3},{4... | collective-permute-start | bytes 3145736 | tf_op jit(solution)/shard_map/ppermute | solution.py:623
  102.9 7.4 %copy-start.7 = (f32[32,8]{0,1:T(8,128)S(1)}, f32[32,8]{0,1:T(8,128)}, u32[]{:S(2)}) copy-start(f32[32,8]{0,1:T(8,128)} %param.29) | copy-start | bytes 3076
  102.9 7.4 %copy-start.8 = (s32[32,8]{0,1:T(8,128)S(1)}, s32[32,8]{0,1:T(8,128)}, u32[]{:S(2)}) copy-start(s32[32,8]{0,1:T(8,128)} %param.28) | copy-start | bytes 3076
  102.9 19.4 %copy-start = (bf16[128,2048]{1,0:T(8,128)(2,1)S(1)}, bf16[128,2048]{1,0:T(8,128)(2,1)}, u32[]{:S(2)}) copy-start(bf16[128,2048]{1,0:T(8,128)(2,1)} %tokens_ref.3) | copy-start | bytes 1572868
  102.9 19.4 %copy-start.1 = (bf16[128,2048]{1,0:T(8,128)(2,1)S(1)}, bf16[128,2048]{1,0:T(8,128)(2,1)}, u32[]{:S(2)}) copy-start(bf16[128,2048]{1,0:T(8,128)(2,1)} %tangents_ref.3) | copy-start | bytes 1572868
  102.9 19.4 %copy-start.5 = (f32[2048]{0:T(1024)S(1)}, f32[2048]{0:T(1024)}, u32[]{:S(2)}) copy-start(f32[2048]{0:T(1024)} %param.18) | copy-start | bytes 24580
  102.9 19.3 %all-to-all-start.1 = ((bf16[16,136,256]{2,1,0:T(8,128)(2,1)}), bf16[16,136,256]{2,1,0:T(8,128)(2,1)S(1)}, u32[]{:S(2)}, u32[]{:S(2)}) async-start(bf16[16,136,256]{2,1,0:T(8,128)(2,1)} %attend.1), calls=%async_computation.1 | async-start | bytes 2228224 | tf_op jit(solution)/shard_map/all_to_all | solution.py:677
  129.0 0.8 copy-start.2
  129.8 9.0 %collective-permute-start.12 = (bf16[72,2048]{1,0:T(8,128)(2,1)S(1)}, bf16[72,2048]{1,0:T(8,128)(2,1)S(1)}, u32[]{:S(2)}, u32[]{:S(2)}) collective-permute-start(bf16[72,2048]{1,0:T(8,128)(2,1)S(1)} %get-tuple-element.13.refs_0_), channel_id=1, source_target_pairs={{0,16},{16,32},{32,48},{48,64},{64,80},{80,96},{96,112},{112,0},{1... | collective-permute-start | bytes 884744 | tf_op jit(solution)/shard_map/ppermute | solution.py:33
  129.8 9.0 %collective-permute-start.11 = (bf16[72,2048]{1,0:T(8,128)(2,1)S(1)}, bf16[72,2048]{1,0:T(8,128)(2,1)S(1)}, u32[]{:S(2)}, u32[]{:S(2)}) collective-permute-start(bf16[72,2048]{1,0:T(8,128)(2,1)S(1)} %get-tuple-element.13.refs_0_), channel_id=1, source_target_pairs={{0,112},{16,0},{32,16},{48,32},{64,48},{80,64},{96,80},{112,96},{1... | collective-permute-start | bytes 884744 | tf_op jit(solution)/shard_map/ppermute | solution.py:33
  138.8 10.1 %collective-permute-start.17 = (bf16[72,2048]{1,0:T(8,128)(2,1)S(1)}, bf16[72,2048]{1,0:T(8,128)(2,1)S(1)}, u32[]{:S(2)}, u32[]{:S(2)}) collective-permute-start(bf16[72,2048]{1,0:T(8,128)(2,1)S(1)} %collective-permute-done.12.refs_2_), channel_id=1, source_target_pairs={{0,16},{16,32},{32,48},{48,64},{64,80},{80,96},{96,112},{112,0},{1... | collective-permute-start | bytes 884744 | tf_op jit(solution)/shard_map/ppermute | solution.py:33
  138.8 10.2 %collective-permute-start.13 = (bf16[72,2048]{1,0:T(8,128)(2,1)S(1)}, bf16[72,2048]{1,0:T(8,128)(2,1)S(1)}, u32[]{:S(2)}, u32[]{:S(2)}) collective-permute-start(bf16[72,2048]{1,0:T(8,128)(2,1)S(1)} %collective-permute-done.11.refs_1_), channel_id=1, source_target_pairs={{0,112},{16,0},{32,16},{48,32},{64,48},{80,64},{96,80},{112,96},{1... | collective-permute-start | bytes 884744 | tf_op jit(solution)/shard_map/ppermute | solution.py:33
  149.0 10.9 %collective-permute-start.19 = (bf16[72,2048]{1,0:T(8,128)(2,1)S(1)}, bf16[72,2048]{1,0:T(8,128)(2,1)S(1)}, u32[]{:S(2)}, u32[]{:S(2)}) collective-permute-start(bf16[72,2048]{1,0:T(8,128)(2,1)S(1)} %collective-permute-done.17.refs_0_), channel_id=1, source_target_pairs={{0,16},{16,32},{32,48},{48,64},{64,80},{80,96},{96,112},{112,0},{1... | collective-permute-start | bytes 884744 | tf_op jit(solution)/shard_map/ppermute | solution.py:33
  149.1 10.8 %collective-permute-start.18 = (bf16[72,2048]{1,0:T(8,128)(2,1)S(1)}, bf16[72,2048]{1,0:T(8,128)(2,1)S(1)}, u32[]{:S(2)}, u32[]{:S(2)}) collective-permute-start(bf16[72,2048]{1,0:T(8,128)(2,1)S(1)} %collective-permute-done.13.refs_3_), channel_id=1, source_target_pairs={{0,112},{16,0},{32,16},{48,32},{64,48},{80,64},{96,80},{112,96},{1... | collective-permute-start | bytes 884744 | tf_op jit(solution)/shard_map/ppermute | solution.py:33
  159.9 7.9 %collective-permute-start.20 = (bf16[72,2048]{1,0:T(8,128)(2,1)S(1)}, bf16[72,2048]{1,0:T(8,128)(2,1)S(1)}, u32[]{:S(2)}, u32[]{:S(2)}) collective-permute-start(bf16[72,2048]{1,0:T(8,128)(2,1)S(1)} %collective-permute-done.19.refs_2_), channel_id=1, source_target_pairs={{0,16},{16,32},{32,48},{48,64},{64,80},{80,96},{96,112},{112,0},{1... | collective-permute-start | bytes 884744 | tf_op jit(solution)/shard_map/ppermute | solution.py:33
  169.7 7.6 %copy-start.6 = (bf16[1,2048,384]{2,1,0:T(8,128)(2,1)S(1)}, bf16[1,2048,384]{2,1,0:T(8,128)(2,1)}, u32[]{:S(2)}) copy-start(bf16[1,2048,384]{2,1,0:T(8,128)(2,1)} %param.25) | copy-start | bytes 4718596
  169.7 23.0 %all-to-all-start.4 = ((bf16[16,24,2048]{2,1,0:T(8,128)(2,1)}), bf16[16,24,2048]{2,1,0:T(8,128)(2,1)}, u32[]{:S(2)}, u32[]{:S(2)}) async-start(bf16[16,24,2048]{2,1,0:T(8,128)(2,1)} %bitcast.31), calls=%async_computation.4 | async-start | bytes 3145728 | tf_op jit(solution)/shard_map/all_to_all | solution.py:714
  177.3 21.9 %collective-permute-start.14 = (bf16[2048,384]{1,0:T(8,128)(2,1)S(1)}, bf16[2048,384]{1,0:T(8,128)(2,1)}, u32[]{:S(2)}, u32[]{:S(2)}) collective-permute-start(bf16[2048,384]{1,0:T(8,128)(2,1)S(1)} %bitcast.45), channel_id=1, source_target_pairs={{0,128},{128,0},{1,129},{129,1},{2,130},{130,2},{3,131},{131,3},{4... | collective-permute-start | bytes 4718600 | tf_op jit(solution)/shard_map/ppermute | solution.py:627
  177.4 21.8 %collective-permute-start.15 = (bf16[2048,384]{1,0:T(8,128)(2,1)}, bf16[2048,384]{1,0:T(8,128)(2,1)}, u32[]{:S(2)}, u32[]{:S(2)}) collective-permute-start(bf16[2048,384]{1,0:T(8,128)(2,1)} %bitcast.46), channel_id=1, source_target_pairs={{0,128},{128,0},{1,129},{129,1},{2,130},{130,2},{3,131},{131,3},{4... | collective-permute-start | bytes 4718600 | tf_op jit(solution)/shard_map/ppermute | solution.py:627
  177.9 21.3 %collective-permute-start.16 = (bf16[2048,384]{1,0:T(8,128)(2,1)}, bf16[2048,384]{1,0:T(8,128)(2,1)}, u32[]{:S(2)}, u32[]{:S(2)}) collective-permute-start(bf16[2048,384]{1,0:T(8,128)(2,1)} %bitcast.49), channel_id=1, source_target_pairs={{0,128},{128,0},{1,129},{129,1},{2,130},{130,2},{3,131},{131,3},{4... | collective-permute-start | bytes 4718600 | tf_op jit(solution)/shard_map/ppermute | solution.py:627
  192.8 22.1 %all-to-all-start.2 = ((bf16[16,24,2048]{2,1,0:T(8,128)(2,1)}), bf16[16,24,2048]{2,1,0:T(8,128)(2,1)}, u32[]{:S(2)}, u32[]{:S(2)}) async-start(bf16[16,24,2048]{2,1,0:T(8,128)(2,1)} %bitcast.24), calls=%async_computation.2 | async-start | bytes 3145728 | tf_op jit(solution)/shard_map/all_to_all | solution.py:714
  214.9 22.1 %all-to-all-start.5 = ((bf16[16,24,2048]{2,1,0:T(8,128)(2,1)}), bf16[16,24,2048]{2,1,0:T(8,128)(2,1)S(1)}, u32[]{:S(2)}, u32[]{:S(2)}) async-start(bf16[16,24,2048]{2,1,0:T(8,128)(2,1)} %bitcast.53), calls=%async_computation.5 | async-start | bytes 3145728 | tf_op jit(solution)/shard_map/all_to_all | solution.py:721
  237.0 21.4 %all-to-all-start.3 = ((bf16[16,24,2048]{2,1,0:T(8,128)(2,1)}), bf16[16,24,2048]{2,1,0:T(8,128)(2,1)S(1)}, u32[]{:S(2)}, u32[]{:S(2)}) async-start(bf16[16,24,2048]{2,1,0:T(8,128)(2,1)} %bitcast.52), calls=%async_computation.3 | async-start | bytes 3145728 | tf_op jit(solution)/shard_map/all_to_all | solution.py:721
  243.7 8.6 %collective-permute-start.21 = (bf16[64,2048]{1,0:T(8,128)(2,1)S(1)}, bf16[64,2048]{1,0:T(8,128)(2,1)S(1)}, u32[]{:S(2)}, u32[]{:S(2)}) collective-permute-start(bf16[64,2048]{1,0:T(8,128)(2,1)S(1)} %get-tuple-element.22), channel_id=1, source_target_pairs={{0,16},{16,32},{32,48},{48,64},{64,80},{80,96},{96,112},{112,0},{1... | collective-permute-start | bytes 786440 | tf_op jit(solution)/shard_map/ppermute | solution.py:33
  243.8 8.5 %collective-permute-start.25 = (bf16[64,2048]{1,0:T(8,128)(2,1)S(1)}, bf16[64,2048]{1,0:T(8,128)(2,1)S(1)}, u32[]{:S(2)}, u32[]{:S(2)}) collective-permute-start(bf16[64,2048]{1,0:T(8,128)(2,1)S(1)} %get-tuple-element.23), channel_id=1, source_target_pairs={{0,112},{16,0},{32,16},{48,32},{64,48},{80,64},{96,80},{112,96},{1... | collective-permute-start | bytes 786440 | tf_op jit(solution)/shard_map/ppermute | solution.py:33
  252.5 9.8 %collective-permute-start.22 = (bf16[64,2048]{1,0:T(8,128)(2,1)S(1)}, bf16[64,2048]{1,0:T(8,128)(2,1)S(1)}, u32[]{:S(2)}, u32[]{:S(2)}) collective-permute-start(bf16[64,2048]{1,0:T(8,128)(2,1)S(1)} %get-tuple-element.20), channel_id=1, source_target_pairs={{0,16},{16,32},{32,48},{48,64},{64,80},{80,96},{96,112},{112,0},{1... | collective-permute-start | bytes 786440 | tf_op jit(solution)/shard_map/ppermute | solution.py:33
  259.3 19.7 %copy-start.3 = (f32[64,2048]{1,0:T(8,128)S(1)}, f32[64,2048]{1,0:T(8,128)}, u32[]{:S(2)}) copy-start(f32[64,2048]{1,0:T(8,128)} %copy-done.2) | copy-start | bytes 1572868
  259.3 7.7 %collective-permute-start.26 = (bf16[64,2048]{1,0:T(8,128)(2,1)S(1)}, bf16[64,2048]{1,0:T(8,128)(2,1)S(1)}, u32[]{:S(2)}, u32[]{:S(2)}) collective-permute-start(bf16[64,2048]{1,0:T(8,128)(2,1)S(1)} %get-tuple-element.21), channel_id=1, source_target_pairs={{0,112},{16,0},{32,16},{48,32},{64,48},{80,64},{96,80},{112,96},{1... | collective-permute-start | bytes 786440 | tf_op jit(solution)/shard_map/ppermute | solution.py:33
  262.3 9.0 %collective-permute-start.23 = (bf16[64,2048]{1,0:T(8,128)(2,1)S(1)}, bf16[64,2048]{1,0:T(8,128)(2,1)S(1)}, u32[]{:S(2)}, u32[]{:S(2)}) collective-permute-start(bf16[64,2048]{1,0:T(8,128)(2,1)S(1)} %fusion.3), channel_id=1, source_target_pairs={{0,16},{16,32},{32,48},{48,64},{64,80},{80,96},{96,112},{112,0},{1... | collective-permute-start | bytes 786440 | tf_op jit(solution)/shard_map/ppermute | solution.py:33
  271.4 7.7 %collective-permute-start.24 = (bf16[64,2048]{1,0:T(8,128)(2,1)S(1)}, bf16[64,2048]{1,0:T(8,128)(2,1)S(1)}, u32[]{:S(2)}, u32[]{:S(2)}) collective-permute-start(bf16[64,2048]{1,0:T(8,128)(2,1)S(1)} %get-tuple-element.18), channel_id=1, source_target_pairs={{0,16},{16,32},{32,48},{48,64},{64,80},{80,96},{96,112},{112,0},{1... | collective-permute-start | bytes 786440 | tf_op jit(solution)/shard_map/ppermute | solution.py:33
  271.5 7.6 %collective-permute-start.27 = (bf16[64,2048]{1,0:T(8,128)(2,1)S(1)}, bf16[64,2048]{1,0:T(8,128)(2,1)S(1)}, u32[]{:S(2)}, u32[]{:S(2)}) collective-permute-start(bf16[64,2048]{1,0:T(8,128)(2,1)S(1)} %get-tuple-element.19), channel_id=1, source_target_pairs={{0,112},{16,0},{32,16},{48,32},{64,48},{80,64},{96,80},{112,96},{1... | collective-permute-start | bytes 786440 | tf_op jit(solution)/shard_map/ppermute | solution.py:33

commit v2 on v1

--- a/solution.py
+++ b/solution.py
@@ -55,8 +55,12 @@
     return jnp.where(row == 0, high, jnp.where(row == 1, middle, jnp.where(row == 2, low, 0.0)))
 
 
-def attend_kernel(scale, group_rows, moe_rows, span_ref, joint_ref, *refs):
-    blocks, (out_ref, held_ref, score_ref) = refs[:-3], refs[-3:]
+def attend_kernel(scale, group_rows, moe_rows, first, count, span_ref, joint_ref, *refs):
+    blocks, refs = refs[:count], refs[count:]
+    if first:
+        sums_ref, figures_ref, held_ref, score_ref = refs
+    else:
+        old_sums_ref, old_figures_ref, out_ref, held_ref, score_ref = refs
     rows, width = joint_ref.shape[0], joint_ref.shape[1] // 2
     keys = blocks[0].shape[0]
     chunk = held_ref.shape[1]
@@ -81,12 +85,15 @@
         score = lax.dot_general(
             query, held_ref[number, :, :width], contract, preferred_element_type=jnp.float32
         )
-        first = number * each_chunk
-        span = jnp.where(lane < keys, span_ref[first], span_ref[first + 1])
+        lead = number * each_chunk
+        span = jnp.where(lane < keys, span_ref[lead], span_ref[lead + 1])
         score = jnp.where(span <= own, score * scale, masked_score)
         score_ref[number] = score
         top = jnp.maximum(top, score)
     top = jnp.max(top, axis=1, keepdims=True)
+    if not first:
+        old_top = old_figures_ref[:, :1]
+        top = jnp.maximum(top, old_top)
     total = jnp.zeros(shape, jnp.float32)
     slope = jnp.zeros(shape, jnp.float32)
     sums = jnp.zeros((rows, 2 * width), jnp.float32)
@@ -112,14 +119,24 @@
         )
     total = jnp.sum(total, axis=1, keepdims=True)
     slope = jnp.sum(slope, axis=1, keepdims=True)
+    lane = lax.broadcasted_iota(jnp.int32, (rows, width), 1)
+    if first:
+        sums_ref[:, :width] = sums[:, :width]
+        sums_ref[:, width:] = sums[:, width:] + tilted
+        figures_ref[...] = jnp.where(lane == 0, top, jnp.where(lane == 1, total, slope))
+        return
+    fade = jnp.exp(old_top - top)
+    total = total + fade * old_figures_ref[:, 1:2]
+    slope = slope + fade * old_figures_ref[:, 2:3]
+    primal = sums[:, :width] + fade * old_sums_ref[:, :width]
+    tangent = sums[:, width:] + tilted + fade * old_sums_ref[:, width:]
     some = total > 0.0
     share = jnp.where(some, 1.0 / jnp.where(some, total, 1.0), 0.0)
-    output = sums[:, :width] * share
+    output = primal * share
     mean_slope = slope * share
-    d_output = (sums[:, width:] + tilted) * share - mean_slope * output
+    d_output = tangent * share - mean_slope * output
     level = jnp.where(some, top + jnp.log(jnp.where(some, total, 1.0)), masked_score)
     both = jnp.concatenate([output, d_output], axis=1).astype(jnp.bfloat16)
-    lane = lax.broadcasted_iota(jnp.int32, (rows, width), 1)
     figures = jnp.where(lane < width // 2, level, mean_slope)
     each = out_ref.shape[1] - 8
     for number in range(out_ref.shape[0]):
@@ -131,28 +148,42 @@
         out_ref[number, each:] = stats.astype(jnp.bfloat16)
 
 
-def attend(spans, joint_query, blocks, receivers, rows_each, group_rows, moe_rows):
+def attend(spans, joint_query, blocks, state, receivers, rows_each, group_rows, moe_rows):
     width = joint_query.shape[1]
     count = 2
     rows = count * rows_each
     whole = pl.BlockSpec(blocks[0].shape, lambda i: (0, 0))
+    row_block = pl.BlockSpec((rows, width), lambda i: (i, 0))
+    half_block = pl.BlockSpec((rows, width // 2), lambda i: (i, 0))
+    first = not state
+    if first:
+        out_specs = (row_block, half_block)
+        out_shape = (
+            jax.ShapeDtypeStruct((joint_query.shape[0], width), jnp.float32),
+            jax.ShapeDtypeStruct((joint_query.shape[0], width // 2), jnp.float32),
+        )
+    else:
+        out_specs = pl.BlockSpec((count, rows_each + 8, width), lambda i: (i, 0, 0))
+        out_shape = jax.ShapeDtypeStruct((receivers, rows_each + 8, width), jnp.bfloat16)
+    scale = (width // 2) ** (-0.5)
     return pl.pallas_call(
-        functools.partial(attend_kernel, (width // 2) ** (-0.5), group_rows, moe_rows),
+        functools.partial(attend_kernel, scale, group_rows, moe_rows, first, len(blocks)),
         grid=(receivers // count,),
         in_specs=[
             pl.BlockSpec(memory_space=pltpu.SMEM),
-            pl.BlockSpec((rows, width), lambda i: (i, 0)),
+            row_block,
             *[whole] * len(blocks),
+            *([] if first else [row_block, half_block]),
         ],
-        out_specs=pl.BlockSpec((count, rows_each + 8, width), lambda i: (i, 0, 0)),
-        out_shape=jax.ShapeDtypeStruct((receivers, rows_each + 8, width), jnp.bfloat16),
+        out_specs=out_specs,
+        out_shape=out_shape,
         scratch_shapes=[
             pltpu.VMEM((len(blocks) // 2, 2 * blocks[0].shape[0], blocks[0].shape[1]), jnp.bfloat16),
             pltpu.VMEM((len(blocks) // 2, rows, 2 * blocks[0].shape[0]), jnp.float32),
         ],
         compiler_params=pltpu.CompilerParams(vmem_limit_bytes=40 << 20),
         name="attend",
-    )(spans, joint_query, *blocks)
+    )(spans, joint_query, *blocks, *state)
 
 
 def merge_kernel(
@@ -490,16 +521,18 @@
 
 
 def expert_kernel(rows_ref, *refs):
-    sources, out_ref, held, (sum_ref, hidden_ref, sems) = refs[:6], refs[6], refs[7:13], refs[13:]
-    down_a, down_b = held[4:]
+    sources, out_ref, held, (sum_ref, hidden_ref, sems) = refs[:6], refs[6], refs[7:10], refs[10:]
     count, depth = rows_ref.shape
-    units = held[0].shape[1]
+    units = sources[0].shape[1]
     step = depth // 4
 
     def copy(number, k):
         part = pl.ds(pl.multiple_of(k * step, step), step)
+        side = number % 2 * units
         return pltpu.make_async_copy(
-            sources[number].at[part], held[number].at[part], sems.at[number, k]
+            sources[number].at[part],
+            held[number // 2].at[part, side : side + units],
+            sems.at[number, k],
         )
 
     for numbers in (range(4), range(4, 6)):
@@ -510,8 +543,9 @@
 
     def contract(k, carry):
         part = pl.ds(pl.multiple_of(k * step, step), step)
-        for number in range(4):
-            copy(number, k).wait()
+        for number in range(2):
+            copy(2 * number, k).wait()
+            copy(2 * number + 1, k).wait()
             sum_ref[number] += jnp.dot(
                 rows_ref[:, part], held[number][part], preferred_element_type=jnp.float32
             )
@@ -526,13 +560,12 @@
         primal = active * up_value
         return primal, active_slope * gate_tangent * up_value + active * up_tangent
 
-    groups = 48 if count % 96 else 96
+    groups = 48
 
     def activate(number, carry):
-        half = number // (count // groups)
-        part = pl.ds(pl.multiple_of(number % (count // groups) * groups, groups), groups)
-        gate = sum_ref[2 * half, part].reshape(groups // 24, 3, 8, units)
-        up = sum_ref[2 * half + 1, part].reshape(groups // 24, 3, 8, units)
+        part = pl.ds(pl.multiple_of(number * groups, groups), groups)
+        gate = sum_ref[0, part].reshape(groups // 24, 3, 8, 2 * units)
+        up = sum_ref[1, part].reshape(groups // 24, 3, 8, 2 * units)
         primal, tangent = pair(gate[:, 0], gate[:, 1], up[:, 0], up[:, 1])
         mixed_gate, mixed_up = gate[:, 2], up[:, 2]
         turned_gate = pltpu.roll(mixed_gate, 4, 1)
@@ -545,11 +578,11 @@
             jnp.where(first, turned_up, mixed_up),
         )
         last = jnp.where(first, last_primal, last_tangent)
-        hidden = jnp.stack([primal, tangent, last], 1).reshape(groups, units)
-        hidden_ref[half, part] = hidden.astype(jnp.bfloat16)
+        hidden = jnp.stack([primal, tangent, last], 1).reshape(groups, 2 * units)
+        hidden_ref[part] = hidden.astype(jnp.bfloat16)
         return carry
 
-    lax.fori_loop(0, 2 * (count // groups), activate, 0)
+    lax.fori_loop(0, count // groups, activate, 0)
 
     def produce(n, carry):
         part = pl.ds(pl.multiple_of(n * step, step), step)
@@ -557,9 +590,7 @@
         copy(5, n).wait()
         across = (((1,), (1,)), ((), ()))
         result = lax.dot_general(
-            hidden_ref[0], down_a[part], across, preferred_element_type=jnp.float32
-        ) + lax.dot_general(
-            hidden_ref[1], down_b[part], across, preferred_element_type=jnp.float32
+            hidden_ref[...], held[2][part], across, preferred_element_type=jnp.float32
         )
         out_ref[:, part] = result.astype(out_ref.dtype)
         return carry
@@ -577,14 +608,14 @@
         out_specs=vmem,
         out_shape=jax.ShapeDtypeStruct(rows.shape, jnp.bfloat16),
         scratch_shapes=[
-            *[pltpu.VMEM((depth, units), jnp.bfloat16)] * 6,
-            pltpu.VMEM((4, count, units), jnp.float32),
-            pltpu.VMEM((2, count, units), jnp.bfloat16),
+            *[pltpu.VMEM((depth, 2 * units), jnp.bfloat16)] * 3,
+            pltpu.VMEM((2, count, 2 * units), jnp.float32),
+            pltpu.VMEM((count, 2 * units), jnp.bfloat16),
             pltpu.SemaphoreType.DMA((6, 4)),
         ],
         compiler_params=pltpu.CompilerParams(vmem_limit_bytes=56 << 20),
         name="expert_rows",
-    )(rows, gate, up, gate_other, up_other, down, down_other)
+    )(rows, gate, gate_other, up, up_other, down, down_other)
 
 
 def layer(
@@ -661,19 +692,26 @@
     own_rows = copies.shape[1]
     joint_query = lax.all_to_all(copies, "seq_1", 0, 0, tiled=True)
     joint_query = joint_query.reshape(row_groups * own_rows, 2 * head_width)
-    order = sorted(blocks)
-    spans = jnp.stack(
-        [
+    receivers = row_groups * head_count
+    rows_each = heads_here * moe_rows
+    state = ()
+    for order in ((0, -1, 1, -2), (2, -3, 3, -4)):
+        spans = [
             (lax.rem(plane + k + plane_count, plane_count) - plane) * plane_rows
             + row_in_plane * tok_count
             for k in order
         ]
-    ).astype(jnp.int32)
-    receivers = row_groups * head_count
-    rows_each = heads_here * moe_rows
-    sent = attend(
-        spans, joint_query, [blocks[k] for k in order], receivers, rows_each, own_rows, moe_rows
-    )
+        state = attend(
+            jnp.stack(spans).astype(jnp.int32),
+            joint_query,
+            [blocks[k] for k in order],
+            state,
+            receivers,
+            rows_each,
+            own_rows,
+            moe_rows,
+        )
+    sent = state
     arrived = lax.all_to_all(sent, ("seq_1", "head"), 0, 0, tiled=True)
     here = lax.axis_index("head")
     side = 1 - 2 * core

time: 281 us -> 289 us (1.028)
  waiting for transfers between devices: 133 us -> 137 us
    ppermute x22, waiting for transfers between devices: 64.4 us -> 53.4 us  [shifted(): lax.ppermute(array, axis, [(i, (i + offset) % size) for i in range(size)])]
    all_to_all x2, waiting for transfers between devices: 15.6 us -> 23.1 us  [layer(): received = lax.all_to_all(outgoing, ('seq_1', 'head'), 0, 0, tiled=True)]
    all_to_all x1, waiting for transfers between devices: 11.8 us -> 17.3 us  [layer(): arrived = lax.all_to_all(sent, ('seq_1', 'head'), 0, 0, tiled=True)]
    pallas_call x2, Pallas kernels: 25.6 us -> 22.1 us  [expert_rows(): pl.pallas_call(expert_kernel, in_specs=[vmem] + [hbm] * 6, out_specs=vmem...]
    pallas_call x1 -> x2, Pallas kernels: 12.4 us -> 15.7 us  [attend(): pl.pallas_call(functools.partial(attend_kernel, scale, group_rows, moe_ro...]
  transfers between devices with their start and end apart: 34 -> 34, of which waited for: 20 -> 18; matrix products, arithmetic and copies ran while one was open for 1% -> 1% of each run, Pallas kernels for 18% -> 17%
where the time goes in v2:
time: 289 us; the launch traced here: 286 us
  waiting for transfers between devices  137 us (47%)
  starting transfers between devices  83.5 us (29%)
  Pallas kernels  57.8 us (20%)
  local copies, waits for them, and re-layouts  4.12 us (1%)
    ppermute x22, waiting for transfers between devices, shifted(): lax.ppermute(array, axis, [(i, (i + offset) % size) for i in range(size)])  53.4 us
    ppermute x1, waiting for transfers between devices, layer(): near_own = lax.ppermute(w_out, ('dp', 'head'), sides)  32.2 us
    ppermute x22, starting transfers between devices, shifted(): lax.ppermute(array, axis, [(i, (i + offset) % size) for i in range(size)])  30.9 us
    all_to_all x2, waiting for transfers between devices, layer(): received = lax.all_to_all(outgoing, ('seq_1', 'head'), 0, 0, tiled=True)  23.1 us
    pallas_call x2, Pallas kernels, expert_rows(): pl.pallas_call(expert_kernel, in_specs=[vmem] + [hbm] * 6, out_specs=vmem...  22.1 us
    all_to_all x1, waiting for transfers between devices, layer(): arrived = lax.all_to_all(sent, ('seq_1', 'head'), 0, 0, tiled=True)  17.3 us
    pallas_call x2, Pallas kernels, attend(): pl.pallas_call(functools.partial(attend_kernel, scale, group_rows, moe_ro...  15.7 us
    all_to_all x2, starting transfers between devices, layer(): received = lax.all_to_all(outgoing, ('seq_1', 'head'), 0, 0, tiled=True)  14.8 us
  transfers between devices with their start and end apart: 34, of which 18 were waited for; matrix products, arithmetic and copies ran while one was open for 1% of the time, Pallas kernels for 17%

profile of v2, /device:TPU:8, one launch (start us, length us, event | category | flops | bytes accessed | tf_op | source)
XLA Modules:
  0.0 285.7 jit_solution(5036085799587545807)
XLA Ops:
  0.6 1.6 collective-permute-start.7
  2.2 2.4 constant_dynamic-slice_fusion
  4.6 2.7 collective-permute-start.9
  7.3 32.2 %collective-permute-done.7.w_near_own = bf16[512,2048]{1,0:T(8,128)(2,1)} collective-permute-done((bf16[512,2048]{1,0:T(8,128)(2,1)}, bf16[512,2048]{1,0:T(8,128)(2,1)}, u32[]{:S(2)}, u32[]{:S(2)}) %collective-permute-start.7) | collective-permute-done | bytes 2097184 | tf_op jit(solution)/shard_map/ppermute | solution.py:651
  39.5 9.3 %collective-permute-start.8 = (bf16[512,2048]{1,0:T(8,128)(2,1)}, bf16[512,2048]{1,0:T(8,128)(2,1)}, u32[]{:S(2)}, u32[]{:S(2)}) collective-permute-start(bf16[512,2048]{1,0:T(8,128)(2,1)} %collective-permute-done.7.w_near_own), channel_id=1, source_target_pairs={{0,128},{128,0},{1,129},{129,1},{2,130},{130,2},{3,131},{131,3},{4... | collective-permute-start | bytes 6291464 | tf_op jit(solution)/shard_map/ppermute | solution.py:653
  49.9 3.6 %keys_of.1 = (bf16[256,2048]{1,0:T(8,128)(2,1)}, bf16[128,512]{1,0:T(8,128)(2,1)}) custom-call(s32[1]{0:T(128)} %bitcast.9.head_ref, bf16[128,2048]{1,0:T(8,128)(2,1)} %tokens_ref.3, bf16[128,2048]{1,0:T(8,128)(2,1)} %tangents_ref.3, f32[1,2048]{1,0:T(1,128)} %bitcast.55, bf16[2048,256]{1,0:T(8,128)(2,1)} %w_key_ref.1, bf16[2048,256]{1,0:T(8,128)(2,1)} %w_value_ref.1, ...), custom_call_target="tpu_custom_call" | custom-call | tf_op jit(solution)/shard_map/keys_of/pallas_call | solution.py:368
  53.5 3.9 %queries_of.1 = bf16[4,512,256]{2,1,0:T(8,128)(2,1)} custom-call(bf16[256,2048]{1,0:T(8,128)(2,1)} %get-tuple-element.12.stacked_ref, bf16[2048,512]{1,0:T(8,128)(2,1)} %weight_ref.1, f32[1,128]{1,0:T(1,128)} %bitcast.57, f32[128,128]{1,0:T(8,128)} %get-tuple-element.33.cosine_ref, f32[128,128]{1,0:T(8,128)} %get-tuple-element.34.sine_ref), custom_call_target="tpu_custom_call" | custom-call | tf_op jit(solution)/shard_map/queries_of/pallas_call | solution.py:418
  57.4 7.7 %all-to-all-start = ((bf16[4,512,256]{2,1,0:T(8,128)(2,1)}), bf16[4,512,256]{2,1,0:T(8,128)(2,1)S(1)}, u32[]{:S(2)}, u32[]{:S(2)}) async-start(bf16[4,512,256]{2,1,0:T(8,128)(2,1)} %queries_of.1), calls=%async_computation | async-start | bytes 2097152 | tf_op jit(solution)/shard_map/all_to_all | solution.py:693
  65.1 3.2 %collective-permute-start = (bf16[128,512]{1,0:T(8,128)(2,1)S(1)}, bf16[128,512]{1,0:T(8,128)(2,1)S(1)}, u32[]{:S(2)}, u32[]{:S(2)}) collective-permute-start(bf16[128,512]{1,0:T(8,128)(2,1)S(1)} %copy-done.4), channel_id=1, source_target_pairs={{0,112},{16,0},{32,16},{48,32},{64,48},{80,64},{96,80},{112,96},{1... | collective-permute-start | bytes 393224 | tf_op jit(solution)/shard_map/ppermute | solution.py:33
  68.3 3.6 %collective-permute-done.2.refs_1_ = bf16[128,512]{1,0:T(8,128)(2,1)S(1)} collective-permute-done((bf16[128,512]{1,0:T(8,128)(2,1)S(1)}, bf16[128,512]{1,0:T(8,128)(2,1)S(1)}, u32[]{:S(2)}, u32[]{:S(2)}) %collective-permute-start.2) | collective-permute-done | bytes 131104 | tf_op jit(solution)/shard_map/ppermute | solution.py:33
  71.9 3.2 %collective-permute-start.1 = (bf16[128,512]{1,0:T(8,128)(2,1)S(1)}, bf16[128,512]{1,0:T(8,128)(2,1)S(1)}, u32[]{:S(2)}, u32[]{:S(2)}) collective-permute-start(bf16[128,512]{1,0:T(8,128)(2,1)S(1)} %collective-permute-done.refs_2_), channel_id=1, source_target_pairs={{0,112},{16,0},{32,16},{48,32},{64,48},{80,64},{96,80},{112,96},{1... | collective-permute-start | bytes 393224 | tf_op jit(solution)/shard_map/ppermute | solution.py:33
  75.2 2.9 %collective-permute-done.3.refs_3_ = bf16[128,512]{1,0:T(8,128)(2,1)S(1)} collective-permute-done((bf16[128,512]{1,0:T(8,128)(2,1)S(1)}, bf16[128,512]{1,0:T(8,128)(2,1)S(1)}, u32[]{:S(2)}, u32[]{:S(2)}) %collective-permute-start.3) | collective-permute-done | bytes 131104 | tf_op jit(solution)/shard_map/ppermute | solution.py:33
  78.1 3.2 %collective-permute-start.5 = (bf16[128,512]{1,0:T(8,128)(2,1)S(1)}, bf16[128,512]{1,0:T(8,128)(2,1)S(1)}, u32[]{:S(2)}, u32[]{:S(2)}) collective-permute-start(bf16[128,512]{1,0:T(8,128)(2,1)S(1)} %collective-permute-done.1.refs_0_), channel_id=1, source_target_pairs={{0,112},{16,0},{32,16},{48,32},{64,48},{80,64},{96,80},{112,96},{1... | collective-permute-start | bytes 393224 | tf_op jit(solution)/shard_map/ppermute | solution.py:33
  81.3 2.9 %collective-permute-done.4.refs_1_ = bf16[128,512]{1,0:T(8,128)(2,1)S(1)} collective-permute-done((bf16[128,512]{1,0:T(8,128)(2,1)S(1)}, bf16[128,512]{1,0:T(8,128)(2,1)S(1)}, u32[]{:S(2)}, u32[]{:S(2)}) %collective-permute-start.4) | collective-permute-done | bytes 131104 | tf_op jit(solution)/shard_map/ppermute | solution.py:33
  84.5 6.9 %attend.2 = (f32[2048,256]{1,0:T(8,128)S(1)}, f32[2048,128]{1,0:T(8,128)S(1)}) custom-call(s32[4]{0:T(128)S(1)} %pad_add_fusion.1.span_ref, bf16[2048,256]{1,0:T(8,128)(2,1)S(1)} %bitcast.39, bf16[128,512]{1,0:T(8,128)(2,1)S(1)} %copy-done.4, bf16[128,512]{1,0:T(8,128)(2,1)S(1)} %collective-permute-done.2.refs_1_, ...), custom_call_target="tpu_custom_call" | custom-call | tf_op jit(solution)/shard_map/attend/pallas_call | solution.py:169
  91.4 8.8 %attend.3 = bf16[16,136,256]{2,1,0:T(8,128)(2,1)} custom-call(s32[4]{0:T(128)S(1)} %pad_add_fusion.span_ref, bf16[2048,256]{1,0:T(8,128)(2,1)S(1)} %bitcast.40, bf16[128,512]{1,0:T(8,128)(2,1)S(1)} %collective-permute-done.1.refs_0_, bf16[128,512]{1,0:T(8,128)(2,1)S(1)} %collective-permute-done.4.refs_1_, ...), custom_call_target="tpu_custom_call" | custom-call | tf_op jit(solution)/shard_map/attend/pallas_call | solution.py:169
  100.3 7.3 %all-to-all-start.1 = ((bf16[16,136,256]{2,1,0:T(8,128)(2,1)}), bf16[16,136,256]{2,1,0:T(8,128)(2,1)S(1)}, u32[]{:S(2)}, u32[]{:S(2)}) async-start(bf16[16,136,256]{2,1,0:T(8,128)(2,1)} %attend.3), calls=%async_computation.1 | async-start | bytes 2228224 | tf_op jit(solution)/shard_map/all_to_all | solution.py:715
  107.8 17.3 %all-to-all-done.1.arrived_ref = bf16[16,136,256]{2,1,0:T(8,128)(2,1)S(1)} async-done(((bf16[16,136,256]{2,1,0:T(8,128)(2,1)}), bf16[16,136,256]{2,1,0:T(8,128)(2,1)S(1)}, u32[]{:S(2)}, u32[]{:S(2)}) %all-to-all-start.1) | async-done | bytes 1114144 | tf_op jit(solution)/shard_map/all_to_all | solution.py:715
  125.2 6.8 %merge.1 = (f32[64,2048]{1,0:T(8,128)S(1)}, bf16[72,2048]{1,0:T(8,128)(2,1)S(1)}) custom-call(s32[5]{0:T(128)S(1)} %stack.62.place_ref, bf16[16,136,256]{2,1,0:T(8,128)(2,1)S(1)} %all-to-all-done.1.arrived_ref, bf16[128,2048]{1,0:T(8,128)(2,1)S(1)} %copy-done, bf16[128,2048]{1,0:T(8,128)(2,1)S(1)} %copy-done.1, f32[1,2048]{1,0:T(1,128)S(1)} %bitcast.43, ...), custom_call_target="tpu_custom_call" | custom-call | tf_op jit(solution)/shard_map/merge/pallas_call | solution.py:293
  132.8 3.2 %collective-permute-start.11 = (bf16[72,2048]{1,0:T(8,128)(2,1)S(1)}, bf16[72,2048]{1,0:T(8,128)(2,1)S(1)}, u32[]{:S(2)}, u32[]{:S(2)}) collective-permute-start(bf16[72,2048]{1,0:T(8,128)(2,1)S(1)} %get-tuple-element.17.refs_0_), channel_id=1, source_target_pairs={{0,112},{16,0},{32,16},{48,32},{64,48},{80,64},{96,80},{112,96},{1... | collective-permute-start | bytes 884744 | tf_op jit(solution)/shard_map/ppermute | solution.py:33
  136.0 6.1 %collective-permute-done.12.refs_2_ = bf16[72,2048]{1,0:T(8,128)(2,1)S(1)} collective-permute-done((bf16[72,2048]{1,0:T(8,128)(2,1)S(1)}, bf16[72,2048]{1,0:T(8,128)(2,1)S(1)}, u32[]{:S(2)}, u32[]{:S(2)}) %collective-permute-start.12) | collective-permute-done | bytes 294944 | tf_op jit(solution)/shard_map/ppermute | solution.py:33
  142.1 3.2 %collective-permute-start.13 = (bf16[72,2048]{1,0:T(8,128)(2,1)S(1)}, bf16[72,2048]{1,0:T(8,128)(2,1)S(1)}, u32[]{:S(2)}, u32[]{:S(2)}) collective-permute-start(bf16[72,2048]{1,0:T(8,128)(2,1)S(1)} %collective-permute-done.11.refs_1_), channel_id=1, source_target_pairs={{0,112},{16,0},{32,16},{48,32},{64,48},{80,64},{96,80},{112,96},{1... | collective-permute-start | bytes 884744 | tf_op jit(solution)/shard_map/ppermute | solution.py:33
  145.3 5.2 %collective-permute-done.17.refs_0_ = bf16[72,2048]{1,0:T(8,128)(2,1)S(1)} collective-permute-done((bf16[72,2048]{1,0:T(8,128)(2,1)S(1)}, bf16[72,2048]{1,0:T(8,128)(2,1)S(1)}, u32[]{:S(2)}, u32[]{:S(2)}) %collective-permute-start.17) | collective-permute-done | bytes 294944 | tf_op jit(solution)/shard_map/ppermute | solution.py:33
  150.5 3.2 %collective-permute-start.18 = (bf16[72,2048]{1,0:T(8,128)(2,1)S(1)}, bf16[72,2048]{1,0:T(8,128)(2,1)S(1)}, u32[]{:S(2)}, u32[]{:S(2)}) collective-permute-start(bf16[72,2048]{1,0:T(8,128)(2,1)S(1)} %collective-permute-done.13.refs_3_), channel_id=1, source_target_pairs={{0,112},{16,0},{32,16},{48,32},{64,48},{80,64},{96,80},{112,96},{1... | collective-permute-start | bytes 884744 | tf_op jit(solution)/shard_map/ppermute | solution.py:33
  153.8 4.7 %collective-permute-done.19.refs_2_ = bf16[72,2048]{1,0:T(8,128)(2,1)S(1)} collective-permute-done((bf16[72,2048]{1,0:T(8,128)(2,1)S(1)}, bf16[72,2048]{1,0:T(8,128)(2,1)S(1)}, u32[]{:S(2)}, u32[]{:S(2)}) %collective-permute-start.19) | collective-permute-done | bytes 294944 | tf_op jit(solution)/shard_map/ppermute | solution.py:33
  158.5 7.9 %collective-permute-done.20.refs_3_ = bf16[72,2048]{1,0:T(8,128)(2,1)S(1)} collective-permute-done((bf16[72,2048]{1,0:T(8,128)(2,1)S(1)}, bf16[72,2048]{1,0:T(8,128)(2,1)S(1)}, u32[]{:S(2)}, u32[]{:S(2)}) %collective-permute-start.20) | collective-permute-done | bytes 294944 | tf_op jit(solution)/shard_map/ppermute | solution.py:33
  166.4 2.0 pack.3
  168.3 8.1 %all-to-all-start.4 = ((bf16[16,24,2048]{2,1,0:T(8,128)(2,1)}), bf16[16,24,2048]{2,1,0:T(8,128)(2,1)}, u32[]{:S(2)}, u32[]{:S(2)}) async-start(bf16[16,24,2048]{2,1,0:T(8,128)(2,1)} %bitcast.31), calls=%async_computation.4 | async-start | bytes 3145728 | tf_op jit(solution)/shard_map/all_to_all | solution.py:752
  177.1 1.9 pack.2
  179.0 15.8 %all-to-all-done.4 = bf16[16,24,2048]{2,1,0:T(8,128)(2,1)} async-done(((bf16[16,24,2048]{2,1,0:T(8,128)(2,1)}), bf16[16,24,2048]{2,1,0:T(8,128)(2,1)}, u32[]{:S(2)}, u32[]{:S(2)}) %all-to-all-start.4) | async-done | bytes 1572896 | tf_op jit(solution)/shard_map/all_to_all | solution.py:752
  194.9 6.7 %all-to-all-start.2 = ((bf16[16,24,2048]{2,1,0:T(8,128)(2,1)}), bf16[16,24,2048]{2,1,0:T(8,128)(2,1)}, u32[]{:S(2)}, u32[]{:S(2)}) async-start(bf16[16,24,2048]{2,1,0:T(8,128)(2,1)} %bitcast.24), calls=%async_computation.2 | async-start | bytes 3145728 | tf_op jit(solution)/shard_map/all_to_all | solution.py:752
  201.6 11.1 %expert_rows.3 = bf16[384,2048]{1,0:T(8,128)(2,1)} custom-call(bf16[384,2048]{1,0:T(8,128)(2,1)} %bitcast.32.rows_ref, bf16[2048,384]{1,0:T(8,128)(2,1)} %bitcast.44, bf16[2048,384]{1,0:T(8,128)(2,1)} %collective-permute-done.14.refs_1_, bf16[2048,384]{1,0:T(8,128)(2,1)} %bitcast.48, bf16[2048,384]{1,0:T(8,128)(2,1)} %collective-permute-done.15.refs_3_, ...), custom_call_target="tpu_custom_call" | custom-call | tf_op jit(solution)/shard_map/expert_rows/pallas_call | solution.py:605
  212.6 7.3 %all-to-all-done.2 = bf16[16,24,2048]{2,1,0:T(8,128)(2,1)} async-done(((bf16[16,24,2048]{2,1,0:T(8,128)(2,1)}), bf16[16,24,2048]{2,1,0:T(8,128)(2,1)}, u32[]{:S(2)}, u32[]{:S(2)}) %all-to-all-start.2) | async-done | bytes 1572896 | tf_op jit(solution)/shard_map/all_to_all | solution.py:752
  219.9 5.5 %all-to-all-start.5 = ((bf16[16,24,2048]{2,1,0:T(8,128)(2,1)}), bf16[16,24,2048]{2,1,0:T(8,128)(2,1)S(1)}, u32[]{:S(2)}, u32[]{:S(2)}) async-start(bf16[16,24,2048]{2,1,0:T(8,128)(2,1)} %bitcast.54), calls=%async_computation.5 | async-start | bytes 3145728 | tf_op jit(solution)/shard_map/all_to_all | solution.py:759
  225.4 11.1 %expert_rows.2 = bf16[384,2048]{1,0:T(8,128)(2,1)} custom-call(bf16[384,2048]{1,0:T(8,128)(2,1)} %bitcast.25.rows_ref, bf16[2048,384]{1,0:T(8,128)(2,1)} %bitcast.45, bf16[2048,384]{1,0:T(8,128)(2,1)} %collective-permute-done.14.refs_1_, bf16[2048,384]{1,0:T(8,128)(2,1)} %bitcast.49, bf16[2048,384]{1,0:T(8,128)(2,1)} %collective-permute-done.15.refs_3_, ...), custom_call_target="tpu_custom_call" | custom-call | tf_op jit(solution)/shard_map/expert_rows/pallas_call | solution.py:605
  236.5 6.4 %all-to-all-done.5 = bf16[16,24,2048]{2,1,0:T(8,128)(2,1)S(1)} async-done(((bf16[16,24,2048]{2,1,0:T(8,128)(2,1)}), bf16[16,24,2048]{2,1,0:T(8,128)(2,1)S(1)}, u32[]{:S(2)}, u32[]{:S(2)}) %all-to-all-start.5) | async-done | bytes 1572896 | tf_op jit(solution)/shard_map/all_to_all | solution.py:759
  242.9 5.7 %all-to-all-start.3 = ((bf16[16,24,2048]{2,1,0:T(8,128)(2,1)}), bf16[16,24,2048]{2,1,0:T(8,128)(2,1)S(1)}, u32[]{:S(2)}, u32[]{:S(2)}) async-start(bf16[16,24,2048]{2,1,0:T(8,128)(2,1)} %bitcast.53), calls=%async_computation.3 | async-start | bytes 3145728 | tf_op jit(solution)/shard_map/all_to_all | solution.py:759
  249.7 1.4 collective-permute-start.21
  251.1 1.9 collective-permute-start.25
  253.1 6.6 %collective-permute-done.21 = bf16[64,2048]{1,0:T(8,128)(2,1)S(1)} collective-permute-done((bf16[64,2048]{1,0:T(8,128)(2,1)S(1)}, bf16[64,2048]{1,0:T(8,128)(2,1)S(1)}, u32[]{:S(2)}, u32[]{:S(2)}) %collective-permute-start.21) | collective-permute-done | bytes 262176 | tf_op jit(solution)/shard_map/ppermute | solution.py:33
  259.9 5.1 %all-to-all-done.3 = bf16[16,24,2048]{2,1,0:T(8,128)(2,1)S(1)} async-done(((bf16[16,24,2048]{2,1,0:T(8,128)(2,1)}), bf16[16,24,2048]{2,1,0:T(8,128)(2,1)S(1)}, u32[]{:S(2)}, u32[]{:S(2)}) %all-to-all-start.3) | async-done | bytes 1572896 | tf_op jit(solution)/shard_map/all_to_all | solution.py:759
  265.0 0.9 mixed.2
  266.3 1.2 collective-permute-done.22
  267.5 1.5 collective-permute-start.23
  269.0 4.2 %collective-permute-done.26 = bf16[64,2048]{1,0:T(8,128)(2,1)S(1)} collective-permute-done((bf16[64,2048]{1,0:T(8,128)(2,1)S(1)}, bf16[64,2048]{1,0:T(8,128)(2,1)S(1)}, u32[]{:S(2)}, u32[]{:S(2)}) %collective-permute-start.26) | collective-permute-done | bytes 262176 | tf_op jit(solution)/shard_map/ppermute | solution.py:33
  273.2 3.8 %collective-permute-done.23 = bf16[64,2048]{1,0:T(8,128)(2,1)S(1)} collective-permute-done((bf16[64,2048]{1,0:T(8,128)(2,1)S(1)}, bf16[64,2048]{1,0:T(8,128)(2,1)S(1)}, u32[]{:S(2)}, u32[]{:S(2)}) %collective-permute-start.23) | collective-permute-done | bytes 262176 | tf_op jit(solution)/shard_map/ppermute | solution.py:33
  277.7 2.9 collective-permute-start.27
  280.6 4.3 %collective-permute-done.24 = bf16[64,2048]{1,0:T(8,128)(2,1)S(1)} collective-permute-done((bf16[64,2048]{1,0:T(8,128)(2,1)S(1)}, bf16[64,2048]{1,0:T(8,128)(2,1)S(1)}, u32[]{:S(2)}, u32[]{:S(2)}) %collective-permute-start.24) | collective-permute-done | bytes 262176 | tf_op jit(solution)/shard_map/ppermute | solution.py:33
  (71 shorter events, 6.5 us)
Async XLA Ops:
  0.6 38.9 %collective-permute-start.7 = (bf16[512,2048]{1,0:T(8,128)(2,1)}, bf16[512,2048]{1,0:T(8,128)(2,1)}, u32[]{:S(2)}, u32[]{:S(2)}) collective-permute-start(bf16[512,2048]{1,0:T(8,128)(2,1)} %w_own.1), channel_id=1, source_target_pairs={{0,1},{1,2},{2,3},{3,0},{128,131},{129,128},{130,129},{131,130},{4... | collective-permute-start | bytes 6291464 | tf_op jit(solution)/shard_map/ppermute | solution.py:651
  4.6 79.8 %collective-permute-start.9 = (bf16[256,2048]{1,0:T(8,128)(2,1)}, bf16[256,2048]{1,0:T(8,128)(2,1)S(1)}, u32[]{:S(2)}, u32[]{:S(2)}) collective-permute-start(bf16[256,2048]{1,0:T(8,128)(2,1)} %constant_dynamic-slice_fusion), channel_id=1, source_target_pairs={{0,2},{1,3},{2,0},{3,1},{4,6},{5,7},{6,4},{7,5},{8,10},{9,11},{10,... | collective-permute-start | bytes 3145736 | tf_op jit(solution)/shard_map/ppermute | solution.py:33
  39.5 85.7 %collective-permute-start.8 = (bf16[512,2048]{1,0:T(8,128)(2,1)}, bf16[512,2048]{1,0:T(8,128)(2,1)}, u32[]{:S(2)}, u32[]{:S(2)}) collective-permute-start(bf16[512,2048]{1,0:T(8,128)(2,1)} %collective-permute-done.7.w_near_own), channel_id=1, source_target_pairs={{0,128},{128,0},{1,129},{129,1},{2,130},{130,2},{3,131},{131,3},{4... | collective-permute-start | bytes 6291464 | tf_op jit(solution)/shard_map/ppermute | solution.py:653
  57.4 7.7 %copy-start.4 = (bf16[128,512]{1,0:T(8,128)(2,1)S(1)}, bf16[128,512]{1,0:T(8,128)(2,1)}, u32[]{:S(2)}) copy-start(bf16[128,512]{1,0:T(8,128)(2,1)} %get-tuple-element.13.refs_0_) | copy-start | bytes 393220
  57.4 27.1 %all-to-all-start = ((bf16[4,512,256]{2,1,0:T(8,128)(2,1)}), bf16[4,512,256]{2,1,0:T(8,128)(2,1)S(1)}, u32[]{:S(2)}, u32[]{:S(2)}) async-start(bf16[4,512,256]{2,1,0:T(8,128)(2,1)} %queries_of.1), calls=%async_computation | async-start | bytes 2097152 | tf_op jit(solution)/shard_map/all_to_all | solution.py:693
  65.1 6.8 %collective-permute-start.2 = (bf16[128,512]{1,0:T(8,128)(2,1)S(1)}, bf16[128,512]{1,0:T(8,128)(2,1)S(1)}, u32[]{:S(2)}, u32[]{:S(2)}) collective-permute-start(bf16[128,512]{1,0:T(8,128)(2,1)S(1)} %copy-done.4), channel_id=1, source_target_pairs={{0,16},{16,32},{32,48},{48,64},{64,80},{80,96},{96,112},{112,0},{1... | collective-permute-start | bytes 393224 | tf_op jit(solution)/shard_map/ppermute | solution.py:33
  65.1 6.8 %collective-permute-start = (bf16[128,512]{1,0:T(8,128)(2,1)S(1)}, bf16[128,512]{1,0:T(8,128)(2,1)S(1)}, u32[]{:S(2)}, u32[]{:S(2)}) collective-permute-start(bf16[128,512]{1,0:T(8,128)(2,1)S(1)} %copy-done.4), channel_id=1, source_target_pairs={{0,112},{16,0},{32,16},{48,32},{64,48},{80,64},{96,80},{112,96},{1... | collective-permute-start | bytes 393224 | tf_op jit(solution)/shard_map/ppermute | solution.py:33
  71.9 6.2 %collective-permute-start.3 = (bf16[128,512]{1,0:T(8,128)(2,1)S(1)}, bf16[128,512]{1,0:T(8,128)(2,1)S(1)}, u32[]{:S(2)}, u32[]{:S(2)}) collective-permute-start(bf16[128,512]{1,0:T(8,128)(2,1)S(1)} %collective-permute-done.2.refs_1_), channel_id=1, source_target_pairs={{0,16},{16,32},{32,48},{48,64},{64,80},{80,96},{96,112},{112,0},{1... | collective-permute-start | bytes 393224 | tf_op jit(solution)/shard_map/ppermute | solution.py:33
  71.9 6.2 %collective-permute-start.1 = (bf16[128,512]{1,0:T(8,128)(2,1)S(1)}, bf16[128,512]{1,0:T(8,128)(2,1)S(1)}, u32[]{:S(2)}, u32[]{:S(2)}) collective-permute-start(bf16[128,512]{1,0:T(8,128)(2,1)S(1)} %collective-permute-done.refs_2_), channel_id=1, source_target_pairs={{0,112},{16,0},{32,16},{48,32},{64,48},{80,64},{96,80},{112,96},{1... | collective-permute-start | bytes 393224 | tf_op jit(solution)/shard_map/ppermute | solution.py:33
  78.1 6.2 %collective-permute-start.4 = (bf16[128,512]{1,0:T(8,128)(2,1)S(1)}, bf16[128,512]{1,0:T(8,128)(2,1)S(1)}, u32[]{:S(2)}, u32[]{:S(2)}) collective-permute-start(bf16[128,512]{1,0:T(8,128)(2,1)S(1)} %collective-permute-done.3.refs_3_), channel_id=1, source_target_pairs={{0,16},{16,32},{32,48},{48,64},{64,80},{80,96},{96,112},{112,0},{1... | collective-permute-start | bytes 393224 | tf_op jit(solution)/shard_map/ppermute | solution.py:33
  78.1 13.3 %collective-permute-start.5 = (bf16[128,512]{1,0:T(8,128)(2,1)S(1)}, bf16[128,512]{1,0:T(8,128)(2,1)S(1)}, u32[]{:S(2)}, u32[]{:S(2)}) collective-permute-start(bf16[128,512]{1,0:T(8,128)(2,1)S(1)} %collective-permute-done.1.refs_0_), channel_id=1, source_target_pairs={{0,112},{16,0},{32,16},{48,32},{64,48},{80,64},{96,80},{112,96},{1... | collective-permute-start | bytes 393224 | tf_op jit(solution)/shard_map/ppermute | solution.py:33
  84.3 7.1 %collective-permute-start.6 = (bf16[128,512]{1,0:T(8,128)(2,1)S(1)}, bf16[128,512]{1,0:T(8,128)(2,1)S(1)}, u32[]{:S(2)}, u32[]{:S(2)}) collective-permute-start(bf16[128,512]{1,0:T(8,128)(2,1)S(1)} %collective-permute-done.4.refs_1_), channel_id=1, source_target_pairs={{0,16},{16,32},{32,48},{48,64},{64,80},{80,96},{96,112},{112,0},{1... | collective-permute-start | bytes 393224 | tf_op jit(solution)/shard_map/ppermute | solution.py:33
  84.4 40.8 %collective-permute-start.10 = (bf16[256,2048]{1,0:T(8,128)(2,1)S(1)}, bf16[256,2048]{1,0:T(8,128)(2,1)}, u32[]{:S(2)}, u32[]{:S(2)}) collective-permute-start(bf16[256,2048]{1,0:T(8,128)(2,1)S(1)} %collective-permute-done.9.w_far_own), channel_id=1, source_target_pairs={{0,128},{128,0},{1,129},{129,1},{2,130},{130,2},{3,131},{131,3},{4... | collective-permute-start | bytes 3145736 | tf_op jit(solution)/shard_map/ppermute | solution.py:654
  100.2 7.4 %copy-start.7 = (f32[32,8]{0,1:T(8,128)S(1)}, f32[32,8]{0,1:T(8,128)}, u32[]{:S(2)}) copy-start(f32[32,8]{0,1:T(8,128)} %param.29) | copy-start | bytes 3076
  100.2 7.4 %copy-start.8 = (s32[32,8]{0,1:T(8,128)S(1)}, s32[32,8]{0,1:T(8,128)}, u32[]{:S(2)}) copy-start(s32[32,8]{0,1:T(8,128)} %param.28) | copy-start | bytes 3076
  100.2 24.9 %copy-start = (bf16[128,2048]{1,0:T(8,128)(2,1)S(1)}, bf16[128,2048]{1,0:T(8,128)(2,1)}, u32[]{:S(2)}) copy-start(bf16[128,2048]{1,0:T(8,128)(2,1)} %tokens_ref.3) | copy-start | bytes 1572868
  100.2 24.9 %copy-start.1 = (bf16[128,2048]{1,0:T(8,128)(2,1)S(1)}, bf16[128,2048]{1,0:T(8,128)(2,1)}, u32[]{:S(2)}) copy-start(bf16[128,2048]{1,0:T(8,128)(2,1)} %tangents_ref.3) | copy-start | bytes 1572868
  100.2 24.9 %copy-start.5 = (f32[2048]{0:T(1024)S(1)}, f32[2048]{0:T(1024)}, u32[]{:S(2)}) copy-start(f32[2048]{0:T(1024)} %param.18) | copy-start | bytes 24580
  100.3 24.9 %all-to-all-start.1 = ((bf16[16,136,256]{2,1,0:T(8,128)(2,1)}), bf16[16,136,256]{2,1,0:T(8,128)(2,1)S(1)}, u32[]{:S(2)}, u32[]{:S(2)}) async-start(bf16[16,136,256]{2,1,0:T(8,128)(2,1)} %attend.3), calls=%async_computation.1 | async-start | bytes 2228224 | tf_op jit(solution)/shard_map/all_to_all | solution.py:715
  132.0 0.8 copy-start.2
  132.8 9.3 %collective-permute-start.12 = (bf16[72,2048]{1,0:T(8,128)(2,1)S(1)}, bf16[72,2048]{1,0:T(8,128)(2,1)S(1)}, u32[]{:S(2)}, u32[]{:S(2)}) collective-permute-start(bf16[72,2048]{1,0:T(8,128)(2,1)S(1)} %get-tuple-element.17.refs_0_), channel_id=1, source_target_pairs={{0,16},{16,32},{32,48},{48,64},{64,80},{80,96},{96,112},{112,0},{1... | collective-permute-start | bytes 884744 | tf_op jit(solution)/shard_map/ppermute | solution.py:33
  132.8 9.3 %collective-permute-start.11 = (bf16[72,2048]{1,0:T(8,128)(2,1)S(1)}, bf16[72,2048]{1,0:T(8,128)(2,1)S(1)}, u32[]{:S(2)}, u32[]{:S(2)}) collective-permute-start(bf16[72,2048]{1,0:T(8,128)(2,1)S(1)} %get-tuple-element.17.refs_0_), channel_id=1, source_target_pairs={{0,112},{16,0},{32,16},{48,32},{64,48},{80,64},{96,80},{112,96},{1... | collective-permute-start | bytes 884744 | tf_op jit(solution)/shard_map/ppermute | solution.py:33
  142.1 8.4 %collective-permute-start.17 = (bf16[72,2048]{1,0:T(8,128)(2,1)S(1)}, bf16[72,2048]{1,0:T(8,128)(2,1)S(1)}, u32[]{:S(2)}, u32[]{:S(2)}) collective-permute-start(bf16[72,2048]{1,0:T(8,128)(2,1)S(1)} %collective-permute-done.12.refs_2_), channel_id=1, source_target_pairs={{0,16},{16,32},{32,48},{48,64},{64,80},{80,96},{96,112},{112,0},{1... | collective-permute-start | bytes 884744 | tf_op jit(solution)/shard_map/ppermute | solution.py:33
  142.1 8.4 %collective-permute-start.13 = (bf16[72,2048]{1,0:T(8,128)(2,1)S(1)}, bf16[72,2048]{1,0:T(8,128)(2,1)S(1)}, u32[]{:S(2)}, u32[]{:S(2)}) collective-permute-start(bf16[72,2048]{1,0:T(8,128)(2,1)S(1)} %collective-permute-done.11.refs_1_), channel_id=1, source_target_pairs={{0,112},{16,0},{32,16},{48,32},{64,48},{80,64},{96,80},{112,96},{1... | collective-permute-start | bytes 884744 | tf_op jit(solution)/shard_map/ppermute | solution.py:33
  150.5 7.9 %collective-permute-start.19 = (bf16[72,2048]{1,0:T(8,128)(2,1)S(1)}, bf16[72,2048]{1,0:T(8,128)(2,1)S(1)}, u32[]{:S(2)}, u32[]{:S(2)}) collective-permute-start(bf16[72,2048]{1,0:T(8,128)(2,1)S(1)} %collective-permute-done.17.refs_0_), channel_id=1, source_target_pairs={{0,16},{16,32},{32,48},{48,64},{64,80},{80,96},{96,112},{112,0},{1... | collective-permute-start | bytes 884744 | tf_op jit(solution)/shard_map/ppermute | solution.py:33
  150.5 7.9 %collective-permute-start.18 = (bf16[72,2048]{1,0:T(8,128)(2,1)S(1)}, bf16[72,2048]{1,0:T(8,128)(2,1)S(1)}, u32[]{:S(2)}, u32[]{:S(2)}) collective-permute-start(bf16[72,2048]{1,0:T(8,128)(2,1)S(1)} %collective-permute-done.13.refs_3_), channel_id=1, source_target_pairs={{0,112},{16,0},{32,16},{48,32},{64,48},{80,64},{96,80},{112,96},{1... | collective-permute-start | bytes 884744 | tf_op jit(solution)/shard_map/ppermute | solution.py:33
  158.4 7.9 %collective-permute-start.20 = (bf16[72,2048]{1,0:T(8,128)(2,1)S(1)}, bf16[72,2048]{1,0:T(8,128)(2,1)S(1)}, u32[]{:S(2)}, u32[]{:S(2)}) collective-permute-start(bf16[72,2048]{1,0:T(8,128)(2,1)S(1)} %collective-permute-done.19.refs_2_), channel_id=1, source_target_pairs={{0,16},{16,32},{32,48},{48,64},{64,80},{80,96},{96,112},{112,0},{1... | collective-permute-start | bytes 884744 | tf_op jit(solution)/shard_map/ppermute | solution.py:33
  168.3 8.1 %copy-start.6 = (bf16[1,2048,384]{2,1,0:T(8,128)(2,1)S(1)}, bf16[1,2048,384]{2,1,0:T(8,128)(2,1)}, u32[]{:S(2)}) copy-start(bf16[1,2048,384]{2,1,0:T(8,128)(2,1)} %param.25) | copy-start | bytes 4718596
  168.3 26.5 %all-to-all-start.4 = ((bf16[16,24,2048]{2,1,0:T(8,128)(2,1)}), bf16[16,24,2048]{2,1,0:T(8,128)(2,1)}, u32[]{:S(2)}, u32[]{:S(2)}) async-start(bf16[16,24,2048]{2,1,0:T(8,128)(2,1)} %bitcast.31), calls=%async_computation.4 | async-start | bytes 3145728 | tf_op jit(solution)/shard_map/all_to_all | solution.py:752
  176.4 25.1 %collective-permute-start.14 = (bf16[2048,384]{1,0:T(8,128)(2,1)S(1)}, bf16[2048,384]{1,0:T(8,128)(2,1)}, u32[]{:S(2)}, u32[]{:S(2)}) collective-permute-start(bf16[2048,384]{1,0:T(8,128)(2,1)S(1)} %bitcast.46), channel_id=1, source_target_pairs={{0,128},{128,0},{1,129},{129,1},{2,130},{130,2},{3,131},{131,3},{4... | collective-permute-start | bytes 4718600 | tf_op jit(solution)/shard_map/ppermute | solution.py:658
  176.5 25.0 %collective-permute-start.15 = (bf16[2048,384]{1,0:T(8,128)(2,1)}, bf16[2048,384]{1,0:T(8,128)(2,1)}, u32[]{:S(2)}, u32[]{:S(2)}) collective-permute-start(bf16[2048,384]{1,0:T(8,128)(2,1)} %bitcast.47), channel_id=1, source_target_pairs={{0,128},{128,0},{1,129},{129,1},{2,130},{130,2},{3,131},{131,3},{4... | collective-permute-start | bytes 4718600 | tf_op jit(solution)/shard_map/ppermute | solution.py:658
  177.0 24.5 %collective-permute-start.16 = (bf16[2048,384]{1,0:T(8,128)(2,1)}, bf16[2048,384]{1,0:T(8,128)(2,1)}, u32[]{:S(2)}, u32[]{:S(2)}) collective-permute-start(bf16[2048,384]{1,0:T(8,128)(2,1)} %bitcast.50), channel_id=1, source_target_pairs={{0,128},{128,0},{1,129},{129,1},{2,130},{130,2},{3,131},{131,3},{4... | collective-permute-start | bytes 4718600 | tf_op jit(solution)/shard_map/ppermute | solution.py:658
  194.9 25.1 %all-to-all-start.2 = ((bf16[16,24,2048]{2,1,0:T(8,128)(2,1)}), bf16[16,24,2048]{2,1,0:T(8,128)(2,1)}, u32[]{:S(2)}, u32[]{:S(2)}) async-start(bf16[16,24,2048]{2,1,0:T(8,128)(2,1)} %bitcast.24), calls=%async_computation.2 | async-start | bytes 3145728 | tf_op jit(solution)/shard_map/all_to_all | solution.py:752
  219.9 23.0 %all-to-all-start.5 = ((bf16[16,24,2048]{2,1,0:T(8,128)(2,1)}), bf16[16,24,2048]{2,1,0:T(8,128)(2,1)S(1)}, u32[]{:S(2)}, u32[]{:S(2)}) async-start(bf16[16,24,2048]{2,1,0:T(8,128)(2,1)} %bitcast.54), calls=%async_computation.5 | async-start | bytes 3145728 | tf_op jit(solution)/shard_map/all_to_all | solution.py:759
  242.9 22.0 %all-to-all-start.3 = ((bf16[16,24,2048]{2,1,0:T(8,128)(2,1)}), bf16[16,24,2048]{2,1,0:T(8,128)(2,1)S(1)}, u32[]{:S(2)}, u32[]{:S(2)}) async-start(bf16[16,24,2048]{2,1,0:T(8,128)(2,1)} %bitcast.53), calls=%async_computation.3 | async-start | bytes 3145728 | tf_op jit(solution)/shard_map/all_to_all | solution.py:759
  249.7 9.9 %collective-permute-start.21 = (bf16[64,2048]{1,0:T(8,128)(2,1)S(1)}, bf16[64,2048]{1,0:T(8,128)(2,1)S(1)}, u32[]{:S(2)}, u32[]{:S(2)}) collective-permute-start(bf16[64,2048]{1,0:T(8,128)(2,1)S(1)} %get-tuple-element.26), channel_id=1, source_target_pairs={{0,16},{16,32},{32,48},{48,64},{64,80},{80,96},{96,112},{112,0},{1... | collective-permute-start | bytes 786440 | tf_op jit(solution)/shard_map/ppermute | solution.py:33
  251.1 8.5 %collective-permute-start.25 = (bf16[64,2048]{1,0:T(8,128)(2,1)S(1)}, bf16[64,2048]{1,0:T(8,128)(2,1)S(1)}, u32[]{:S(2)}, u32[]{:S(2)}) collective-permute-start(bf16[64,2048]{1,0:T(8,128)(2,1)S(1)} %get-tuple-element.27), channel_id=1, source_target_pairs={{0,112},{16,0},{32,16},{48,32},{64,48},{80,64},{96,80},{112,96},{1... | collective-permute-start | bytes 786440 | tf_op jit(solution)/shard_map/ppermute | solution.py:33
  259.8 7.7 %collective-permute-start.22 = (bf16[64,2048]{1,0:T(8,128)(2,1)S(1)}, bf16[64,2048]{1,0:T(8,128)(2,1)S(1)}, u32[]{:S(2)}, u32[]{:S(2)}) collective-permute-start(bf16[64,2048]{1,0:T(8,128)(2,1)S(1)} %get-tuple-element.24), channel_id=1, source_target_pairs={{0,16},{16,32},{32,48},{48,64},{64,80},{80,96},{96,112},{112,0},{1... | collective-permute-start | bytes 786440 | tf_op jit(solution)/shard_map/ppermute | solution.py:33
  265.9 18.9 %copy-start.3 = (f32[64,2048]{1,0:T(8,128)S(1)}, f32[64,2048]{1,0:T(8,128)}, u32[]{:S(2)}) copy-start(f32[64,2048]{1,0:T(8,128)} %copy-done.2) | copy-start | bytes 1572868
  265.9 7.3 %collective-permute-start.26 = (bf16[64,2048]{1,0:T(8,128)(2,1)S(1)}, bf16[64,2048]{1,0:T(8,128)(2,1)S(1)}, u32[]{:S(2)}, u32[]{:S(2)}) collective-permute-start(bf16[64,2048]{1,0:T(8,128)(2,1)S(1)} %get-tuple-element.25), channel_id=1, source_target_pairs={{0,112},{16,0},{32,16},{48,32},{64,48},{80,64},{96,80},{112,96},{1... | collective-permute-start | bytes 786440 | tf_op jit(solution)/shard_map/ppermute | solution.py:33
  267.5 9.5 %collective-permute-start.23 = (bf16[64,2048]{1,0:T(8,128)(2,1)S(1)}, bf16[64,2048]{1,0:T(8,128)(2,1)S(1)}, u32[]{:S(2)}, u32[]{:S(2)}) collective-permute-start(bf16[64,2048]{1,0:T(8,128)(2,1)S(1)} %fusion.3), channel_id=1, source_target_pairs={{0,16},{16,32},{32,48},{48,64},{64,80},{80,96},{96,112},{112,0},{1... | collective-permute-start | bytes 786440 | tf_op jit(solution)/shard_map/ppermute | solution.py:33
  277.1 7.7 %collective-permute-start.24 = (bf16[64,2048]{1,0:T(8,128)(2,1)S(1)}, bf16[64,2048]{1,0:T(8,128)(2,1)S(1)}, u32[]{:S(2)}, u32[]{:S(2)}) collective-permute-start(bf16[64,2048]{1,0:T(8,128)(2,1)S(1)} %get-tuple-element.22), channel_id=1, source_target_pairs={{0,16},{16,32},{32,48},{48,64},{64,80},{80,96},{96,112},{112,0},{1... | collective-permute-start | bytes 786440 | tf_op jit(solution)/shard_map/ppermute | solution.py:33
  277.7 7.1 %collective-permute-start.27 = (bf16[64,2048]{1,0:T(8,128)(2,1)S(1)}, bf16[64,2048]{1,0:T(8,128)(2,1)S(1)}, u32[]{:S(2)}, u32[]{:S(2)}) collective-permute-start(bf16[64,2048]{1,0:T(8,128)(2,1)S(1)} %get-tuple-element.23), channel_id=1, source_target_pairs={{0,112},{16,0},{32,16},{48,32},{64,48},{80,64},{96,80},{112,96},{1... | collective-permute-start | bytes 786440 | tf_op jit(solution)/shard_map/ppermute | solution.py:33

commit v3 on v2

--- a/solution.py
+++ b/solution.py
@@ -150,7 +150,7 @@
 
 def attend(spans, joint_query, blocks, state, receivers, rows_each, group_rows, moe_rows):
     width = joint_query.shape[1]
-    count = 2
+    count = 4 if state else 2
     rows = count * rows_each
     whole = pl.BlockSpec(blocks[0].shape, lambda i: (0, 0))
     row_block = pl.BlockSpec((rows, width), lambda i: (i, 0))
@@ -393,7 +393,23 @@
     )(head, tokens, tangents, gain, w_key, w_value, key_gain, cosine, sine)
 
 
-def queries_kernel(moe_rows, stacked_ref, weight_ref, gain_ref, cosine_ref, sine_ref, out_ref):
+def queries_kernel(
+    moe_rows,
+    core_ref,
+    stacked_ref,
+    weight_ref,
+    gain_ref,
+    cosine_ref,
+    sine_ref,
+    w_out_ref,
+    out_ref,
+    far_ref,
+    sem,
+):
+    half_rows = far_ref.shape[0]
+    start = pl.multiple_of(core_ref[0] * half_rows, half_rows)
+    far_copy = pltpu.make_async_copy(w_out_ref.at[pl.ds(start, half_rows)], far_ref, sem)
+    far_copy.start()
     count = stacked_ref.shape[0] // 2
     width = gain_ref.shape[1]
     heads = weight_ref.shape[1] // width
@@ -410,16 +426,24 @@
                 out_ref[copy, start : start + moe_rows] = joint[
                     receiver * moe_rows : (receiver + 1) * moe_rows
                 ]
-
-
-def queries_of(stacked, weight, gain, cosine, sine, copies, moe_rows):
+    far_copy.wait()
+
+
+def queries_of(core, stacked, weight, gain, cosine, sine, w_out, copies, moe_rows):
     width = gain.shape[1]
     rows = stacked.shape[0] // 2 * (weight.shape[1] // width)
+    vmem, hbm = (pl.BlockSpec(memory_space=space) for space in (pltpu.VMEM, pl.ANY))
     return pl.pallas_call(
         functools.partial(queries_kernel, moe_rows),
-        out_shape=jax.ShapeDtypeStruct((copies, rows, 2 * width), jnp.bfloat16),
+        in_specs=[pl.BlockSpec(memory_space=pltpu.SMEM)] + [vmem] * 5 + [hbm],
+        out_specs=(vmem, vmem),
+        out_shape=(
+            jax.ShapeDtypeStruct((copies, rows, 2 * width), jnp.bfloat16),
+            jax.ShapeDtypeStruct((w_out.shape[0] // 2, w_out.shape[1]), w_out.dtype),
+        ),
+        scratch_shapes=[pltpu.SemaphoreType.DMA],
         name="queries_of",
-    )(stacked, weight, gain, cosine, sine)
+    )(core, stacked, weight, gain, cosine, sine, w_out)
 
 
 def table_of(refs, rows, number):
@@ -643,17 +667,6 @@
     core = lax.axis_index("dp")
     other_core = [(0, 1), (1, 0)]
 
-    half_rows = w_out.shape[0] // 2
-    ring = range(head_count)
-    sides = [(i, (i + 1) % head_count) for i in ring]
-    sides += [(head_count + i, head_count + (i - 1) % head_count) for i in ring]
-    far_rows = lax.dynamic_slice_in_dim(w_out, core * half_rows, half_rows, 0)
-    near_own = lax.ppermute(w_out, ("dp", "head"), sides)
-    far_own = shifted(far_rows, "head", head_count // 2)
-    near_other = lax.ppermute(near_own, "dp", other_core)
-    far_other = lax.ppermute(far_own, "dp", other_core)
-    out_pieces = (w_out, near_own, near_other, far_own, far_other)
-
     own_halves = [expert_gate[0], expert_up[0], expert_down[0]]
     expert_halves = own_halves + [lax.ppermute(half, "dp", other_core) for half in own_halves]
 
@@ -688,14 +701,33 @@
     tables = jnp.pad(tables, ((0, 0), (0, model_width - tables.shape[1])))
 
     row_groups = lax.axis_size("seq_1")
-    copies = queries_of(stacked, w_query, query_gain[None], cosine, sine, row_groups, moe_rows)
+    copies, far_rows = queries_of(
+        core.astype(jnp.int32)[None],
+        stacked,
+        w_query,
+        query_gain[None],
+        cosine,
+        sine,
+        w_out,
+        row_groups,
+        moe_rows,
+    )
+
+    ring = range(head_count)
+    sides = [(i, (i + 1) % head_count) for i in ring]
+    sides += [(head_count + i, head_count + (i - 1) % head_count) for i in ring]
+    near_own = lax.ppermute(w_out, ("dp", "head"), sides)
+    far_own = shifted(far_rows, "head", head_count // 2)
+    near_other = lax.ppermute(near_own, "dp", other_core)
+    far_other = lax.ppermute(far_own, "dp", other_core)
+    out_pieces = (w_out, near_own, near_other, far_own, far_other)
     own_rows = copies.shape[1]
     joint_query = lax.all_to_all(copies, "seq_1", 0, 0, tiled=True)
     joint_query = joint_query.reshape(row_groups * own_rows, 2 * head_width)
     receivers = row_groups * head_count
     rows_each = heads_here * moe_rows
     state = ()
-    for order in ((0, -1, 1, -2), (2, -3, 3, -4)):
+    for order in ((0, -1, 1, -2, 2, -3), (3, -4)):
         spans = [
             (lax.rem(plane + k + plane_count, plane_count) - plane) * plane_rows
             + row_in_plane * tok_count

time: 289 us -> 283 us (0.979)
  waiting for transfers between devices: 137 us -> 130 us
  Pallas kernels: 57.8 us -> 61.2 us
    ppermute x1, waiting for transfers between devices: 32.2 us -> 25.3 us  [layer(): near_own = lax.ppermute(w_out, ('dp', 'head'), sides)]
  transfers between devices with their start and end apart: 34 -> 34, of which waited for: 18 -> 19; matrix products, arithmetic and copies ran while one was open for 1% -> 1% of each run, Pallas kernels for 17% -> 19%
where the time goes in v3:
time: 283 us; the launch traced here: 280 us
  waiting for transfers between devices  130 us (46%)
  starting transfers between devices  84.6 us (30%)
  Pallas kernels  61.2 us (22%)
    ppermute x22, waiting for transfers between devices, shifted(): lax.ppermute(array, axis, [(i, (i + offset) % size) for i in range(size)])  52.6 us
    ppermute x22, starting transfers between devices, shifted(): lax.ppermute(array, axis, [(i, (i + offset) % size) for i in range(size)])  32.6 us
    ppermute x1, waiting for transfers between devices, layer(): near_own = lax.ppermute(w_out, ('dp', 'head'), sides)  25.3 us
    all_to_all x2, waiting for transfers between devices, layer(): received = lax.all_to_all(outgoing, ('seq_1', 'head'), 0, 0, tiled=True)  23.3 us
    pallas_call x2, Pallas kernels, expert_rows(): pl.pallas_call(expert_kernel, in_specs=[vmem] + [hbm] * 6, out_specs=vmem...  22.2 us
    pallas_call x2, Pallas kernels, attend(): pl.pallas_call(functools.partial(attend_kernel, scale, group_rows, moe_ro...  18.4 us
    all_to_all x1, waiting for transfers between devices, layer(): arrived = lax.all_to_all(sent, ('seq_1', 'head'), 0, 0, tiled=True)  17.3 us
    all_to_all x2, starting transfers between devices, layer(): received = lax.all_to_all(outgoing, ('seq_1', 'head'), 0, 0, tiled=True)  14.6 us
  transfers between devices with their start and end apart: 34, of which 19 were waited for; matrix products, arithmetic and copies ran while one was open for 1% of the time, Pallas kernels for 19%

profile of v3, /device:TPU:8, one launch (start us, length us, event | category | flops | bytes accessed | tf_op | source)
XLA Modules:
  0.0 280.0 jit_solution(4443700315995668003)
XLA Ops:
  0.6 1.6 collective-permute-start.7
  3.3 3.6 %keys_of.1 = (bf16[256,2048]{1,0:T(8,128)(2,1)}, bf16[128,512]{1,0:T(8,128)(2,1)}) custom-call(s32[1]{0:T(128)} %bitcast.7.head_ref, bf16[128,2048]{1,0:T(8,128)(2,1)} %tokens_ref.3, bf16[128,2048]{1,0:T(8,128)(2,1)} %tangents_ref.3, f32[1,2048]{1,0:T(1,128)} %bitcast.55, bf16[2048,256]{1,0:T(8,128)(2,1)} %w_key_ref.1, bf16[2048,256]{1,0:T(8,128)(2,1)} %w_value_ref.1, ...), custom_call_target="tpu_custom_call" | custom-call | tf_op jit(solution)/shard_map/keys_of/pallas_call | solution.py:368
  6.9 4.5 %queries_of.1 = (bf16[4,512,256]{2,1,0:T(8,128)(2,1)}, bf16[256,2048]{1,0:T(8,128)(2,1)}) custom-call(s32[1]{0:T(128)} %bitcast.4.core_ref, bf16[256,2048]{1,0:T(8,128)(2,1)} %get-tuple-element.14.stacked_ref, bf16[2048,512]{1,0:T(8,128)(2,1)} %weight_ref.1, f32[1,128]{1,0:T(1,128)} %bitcast.57, f32[128,128]{1,0:T(8,128)} %get-tuple-element.37.cosine_ref, ...), custom_call_target="tpu_custom_call" | custom-call | tf_op jit(solution)/shard_map/queries_of/pallas_call | solution.py:436
  11.4 2.8 %collective-permute-start.9 = (bf16[256,2048]{1,0:T(8,128)(2,1)}, bf16[256,2048]{1,0:T(8,128)(2,1)S(1)}, u32[]{:S(2)}, u32[]{:S(2)}) collective-permute-start(bf16[256,2048]{1,0:T(8,128)(2,1)} %get-tuple-element.19), channel_id=1, source_target_pairs={{0,2},{1,3},{2,0},{3,1},{4,6},{5,7},{6,4},{7,5},{8,10},{9,11},{10,... | collective-permute-start | bytes 3145736 | tf_op jit(solution)/shard_map/ppermute | solution.py:33
  14.2 25.3 %collective-permute-done.7.w_near_own = bf16[512,2048]{1,0:T(8,128)(2,1)} collective-permute-done((bf16[512,2048]{1,0:T(8,128)(2,1)}, bf16[512,2048]{1,0:T(8,128)(2,1)}, u32[]{:S(2)}, u32[]{:S(2)}) %collective-permute-start.7) | collective-permute-done | bytes 2097184 | tf_op jit(solution)/shard_map/ppermute | solution.py:719
  39.5 9.3 %collective-permute-start.8 = (bf16[512,2048]{1,0:T(8,128)(2,1)}, bf16[512,2048]{1,0:T(8,128)(2,1)}, u32[]{:S(2)}, u32[]{:S(2)}) collective-permute-start(bf16[512,2048]{1,0:T(8,128)(2,1)} %collective-permute-done.7.w_near_own), channel_id=1, source_target_pairs={{0,128},{128,0},{1,129},{129,1},{2,130},{130,2},{3,131},{131,3},{4... | collective-permute-start | bytes 6291464 | tf_op jit(solution)/shard_map/ppermute | solution.py:721
  48.8 7.6 %all-to-all-start = ((bf16[4,512,256]{2,1,0:T(8,128)(2,1)}), bf16[4,512,256]{2,1,0:T(8,128)(2,1)S(1)}, u32[]{:S(2)}, u32[]{:S(2)}) async-start(bf16[4,512,256]{2,1,0:T(8,128)(2,1)} %get-tuple-element.15), calls=%async_computation | async-start | bytes 2097152 | tf_op jit(solution)/shard_map/all_to_all | solution.py:725
  56.4 3.2 %collective-permute-start = (bf16[128,512]{1,0:T(8,128)(2,1)S(1)}, bf16[128,512]{1,0:T(8,128)(2,1)S(1)}, u32[]{:S(2)}, u32[]{:S(2)}) collective-permute-start(bf16[128,512]{1,0:T(8,128)(2,1)S(1)} %copy-done.4), channel_id=1, source_target_pairs={{0,112},{16,0},{32,16},{48,32},{64,48},{80,64},{96,80},{112,96},{1... | collective-permute-start | bytes 393224 | tf_op jit(solution)/shard_map/ppermute | solution.py:33
  59.6 3.6 %collective-permute-done.3.refs_1_ = bf16[128,512]{1,0:T(8,128)(2,1)S(1)} collective-permute-done((bf16[128,512]{1,0:T(8,128)(2,1)S(1)}, bf16[128,512]{1,0:T(8,128)(2,1)S(1)}, u32[]{:S(2)}, u32[]{:S(2)}) %collective-permute-start.3) | collective-permute-done | bytes 131104 | tf_op jit(solution)/shard_map/ppermute | solution.py:33
  63.2 3.2 %collective-permute-start.1 = (bf16[128,512]{1,0:T(8,128)(2,1)S(1)}, bf16[128,512]{1,0:T(8,128)(2,1)S(1)}, u32[]{:S(2)}, u32[]{:S(2)}) collective-permute-start(bf16[128,512]{1,0:T(8,128)(2,1)S(1)} %collective-permute-done.refs_2_), channel_id=1, source_target_pairs={{0,112},{16,0},{32,16},{48,32},{64,48},{80,64},{96,80},{112,96},{1... | collective-permute-start | bytes 393224 | tf_op jit(solution)/shard_map/ppermute | solution.py:33
  66.5 2.9 %collective-permute-done.4.refs_3_ = bf16[128,512]{1,0:T(8,128)(2,1)S(1)} collective-permute-done((bf16[128,512]{1,0:T(8,128)(2,1)S(1)}, bf16[128,512]{1,0:T(8,128)(2,1)S(1)}, u32[]{:S(2)}, u32[]{:S(2)}) %collective-permute-start.4) | collective-permute-done | bytes 131104 | tf_op jit(solution)/shard_map/ppermute | solution.py:33
  69.4 3.2 %collective-permute-start.2 = (bf16[128,512]{1,0:T(8,128)(2,1)S(1)}, bf16[128,512]{1,0:T(8,128)(2,1)S(1)}, u32[]{:S(2)}, u32[]{:S(2)}) collective-permute-start(bf16[128,512]{1,0:T(8,128)(2,1)S(1)} %collective-permute-done.1.refs_4_), channel_id=1, source_target_pairs={{0,112},{16,0},{32,16},{48,32},{64,48},{80,64},{96,80},{112,96},{1... | collective-permute-start | bytes 393224 | tf_op jit(solution)/shard_map/ppermute | solution.py:33
  72.6 2.9 %collective-permute-done.5.refs_5_ = bf16[128,512]{1,0:T(8,128)(2,1)S(1)} collective-permute-done((bf16[128,512]{1,0:T(8,128)(2,1)S(1)}, bf16[128,512]{1,0:T(8,128)(2,1)S(1)}, u32[]{:S(2)}, u32[]{:S(2)}) %collective-permute-start.5) | collective-permute-done | bytes 131104 | tf_op jit(solution)/shard_map/ppermute | solution.py:33
  75.8 9.6 %attend.2 = (f32[2048,256]{1,0:T(8,128)S(1)}, f32[2048,128]{1,0:T(8,128)S(1)}) custom-call(s32[6]{0:T(128)S(1)} %stack.72.span_ref, bf16[2048,256]{1,0:T(8,128)(2,1)S(1)} %bitcast.39, bf16[128,512]{1,0:T(8,128)(2,1)S(1)} %copy-done.4, bf16[128,512]{1,0:T(8,128)(2,1)S(1)} %collective-permute-done.3.refs_1_, ...), custom_call_target="tpu_custom_call" | custom-call | tf_op jit(solution)/shard_map/attend/pallas_call | solution.py:169
  85.4 8.8 %attend.3 = bf16[16,136,256]{2,1,0:T(8,128)(2,1)} custom-call(s32[2]{0:T(128)S(1)} %pad_add_fusion.span_ref, bf16[2048,256]{1,0:T(8,128)(2,1)S(1)} %bitcast.40, bf16[128,512]{1,0:T(8,128)(2,1)S(1)} %collective-permute-done.2.refs_0_, bf16[128,512]{1,0:T(8,128)(2,1)S(1)} %collective-permute-done.6.refs_1_, f32[2048,256]{1,0:T(8,128)S(1)} %get-tuple-element.17.refs_2_, ...), custom_call_target="tpu_custom_call" | custom-call | tf_op jit(solution)/shard_map/attend/pallas_call | solution.py:169
  94.2 7.2 %all-to-all-start.1 = ((bf16[16,136,256]{2,1,0:T(8,128)(2,1)}), bf16[16,136,256]{2,1,0:T(8,128)(2,1)S(1)}, u32[]{:S(2)}, u32[]{:S(2)}) async-start(bf16[16,136,256]{2,1,0:T(8,128)(2,1)} %attend.3), calls=%async_computation.1 | async-start | bytes 2228224 | tf_op jit(solution)/shard_map/all_to_all | solution.py:747
  101.7 17.3 %all-to-all-done.1.arrived_ref = bf16[16,136,256]{2,1,0:T(8,128)(2,1)S(1)} async-done(((bf16[16,136,256]{2,1,0:T(8,128)(2,1)}), bf16[16,136,256]{2,1,0:T(8,128)(2,1)S(1)}, u32[]{:S(2)}, u32[]{:S(2)}) %all-to-all-start.1) | async-done | bytes 1114144 | tf_op jit(solution)/shard_map/all_to_all | solution.py:747
  119.1 6.8 %merge.1 = (f32[64,2048]{1,0:T(8,128)S(1)}, bf16[72,2048]{1,0:T(8,128)(2,1)S(1)}) custom-call(s32[5]{0:T(128)S(1)} %stack.62.place_ref, bf16[16,136,256]{2,1,0:T(8,128)(2,1)S(1)} %all-to-all-done.1.arrived_ref, bf16[128,2048]{1,0:T(8,128)(2,1)S(1)} %copy-done, bf16[128,2048]{1,0:T(8,128)(2,1)S(1)} %copy-done.1, f32[1,2048]{1,0:T(1,128)S(1)} %bitcast.43, ...), custom_call_target="tpu_custom_call" | custom-call | tf_op jit(solution)/shard_map/merge/pallas_call | solution.py:293
  126.7 3.2 %collective-permute-start.11 = (bf16[72,2048]{1,0:T(8,128)(2,1)S(1)}, bf16[72,2048]{1,0:T(8,128)(2,1)S(1)}, u32[]{:S(2)}, u32[]{:S(2)}) collective-permute-start(bf16[72,2048]{1,0:T(8,128)(2,1)S(1)} %get-tuple-element.21.refs_0_), channel_id=1, source_target_pairs={{0,112},{16,0},{32,16},{48,32},{64,48},{80,64},{96,80},{112,96},{1... | collective-permute-start | bytes 884744 | tf_op jit(solution)/shard_map/ppermute | solution.py:33
  129.9 6.2 %collective-permute-done.12.refs_2_ = bf16[72,2048]{1,0:T(8,128)(2,1)S(1)} collective-permute-done((bf16[72,2048]{1,0:T(8,128)(2,1)S(1)}, bf16[72,2048]{1,0:T(8,128)(2,1)S(1)}, u32[]{:S(2)}, u32[]{:S(2)}) %collective-permute-start.12) | collective-permute-done | bytes 294944 | tf_op jit(solution)/shard_map/ppermute | solution.py:33
  136.1 3.2 %collective-permute-start.13 = (bf16[72,2048]{1,0:T(8,128)(2,1)S(1)}, bf16[72,2048]{1,0:T(8,128)(2,1)S(1)}, u32[]{:S(2)}, u32[]{:S(2)}) collective-permute-start(bf16[72,2048]{1,0:T(8,128)(2,1)S(1)} %collective-permute-done.11.refs_1_), channel_id=1, source_target_pairs={{0,112},{16,0},{32,16},{48,32},{64,48},{80,64},{96,80},{112,96},{1... | collective-permute-start | bytes 884744 | tf_op jit(solution)/shard_map/ppermute | solution.py:33
  139.4 5.4 %collective-permute-done.17.refs_0_ = bf16[72,2048]{1,0:T(8,128)(2,1)S(1)} collective-permute-done((bf16[72,2048]{1,0:T(8,128)(2,1)S(1)}, bf16[72,2048]{1,0:T(8,128)(2,1)S(1)}, u32[]{:S(2)}, u32[]{:S(2)}) %collective-permute-start.17) | collective-permute-done | bytes 294944 | tf_op jit(solution)/shard_map/ppermute | solution.py:33
  145.0 3.0 %collective-permute-start.18 = (bf16[72,2048]{1,0:T(8,128)(2,1)S(1)}, bf16[72,2048]{1,0:T(8,128)(2,1)S(1)}, u32[]{:S(2)}, u32[]{:S(2)}) collective-permute-start(bf16[72,2048]{1,0:T(8,128)(2,1)S(1)} %collective-permute-done.13.refs_3_), channel_id=1, source_target_pairs={{0,112},{16,0},{32,16},{48,32},{64,48},{80,64},{96,80},{112,96},{1... | collective-permute-start | bytes 884744 | tf_op jit(solution)/shard_map/ppermute | solution.py:33
  148.0 4.7 %collective-permute-done.19.refs_2_ = bf16[72,2048]{1,0:T(8,128)(2,1)S(1)} collective-permute-done((bf16[72,2048]{1,0:T(8,128)(2,1)S(1)}, bf16[72,2048]{1,0:T(8,128)(2,1)S(1)}, u32[]{:S(2)}, u32[]{:S(2)}) %collective-permute-start.19) | collective-permute-done | bytes 294944 | tf_op jit(solution)/shard_map/ppermute | solution.py:33
  152.7 7.9 %collective-permute-done.20.refs_3_ = bf16[72,2048]{1,0:T(8,128)(2,1)S(1)} collective-permute-done((bf16[72,2048]{1,0:T(8,128)(2,1)S(1)}, bf16[72,2048]{1,0:T(8,128)(2,1)S(1)}, u32[]{:S(2)}, u32[]{:S(2)}) %collective-permute-start.20) | collective-permute-done | bytes 294944 | tf_op jit(solution)/shard_map/ppermute | solution.py:33
  160.6 2.0 pack.3
  162.6 7.9 %all-to-all-start.4 = ((bf16[16,24,2048]{2,1,0:T(8,128)(2,1)}), bf16[16,24,2048]{2,1,0:T(8,128)(2,1)}, u32[]{:S(2)}, u32[]{:S(2)}) async-start(bf16[16,24,2048]{2,1,0:T(8,128)(2,1)} %bitcast.31), calls=%async_computation.4 | async-start | bytes 3145728 | tf_op jit(solution)/shard_map/all_to_all | solution.py:784
  171.1 1.9 pack.2
  173.1 15.8 %all-to-all-done.4 = bf16[16,24,2048]{2,1,0:T(8,128)(2,1)} async-done(((bf16[16,24,2048]{2,1,0:T(8,128)(2,1)}), bf16[16,24,2048]{2,1,0:T(8,128)(2,1)}, u32[]{:S(2)}, u32[]{:S(2)}) %all-to-all-start.4) | async-done | bytes 1572896 | tf_op jit(solution)/shard_map/all_to_all | solution.py:784
  188.9 6.7 %all-to-all-start.2 = ((bf16[16,24,2048]{2,1,0:T(8,128)(2,1)}), bf16[16,24,2048]{2,1,0:T(8,128)(2,1)}, u32[]{:S(2)}, u32[]{:S(2)}) async-start(bf16[16,24,2048]{2,1,0:T(8,128)(2,1)} %bitcast.24), calls=%async_computation.2 | async-start | bytes 3145728 | tf_op jit(solution)/shard_map/all_to_all | solution.py:784
  195.6 11.1 %expert_rows.3 = bf16[384,2048]{1,0:T(8,128)(2,1)} custom-call(bf16[384,2048]{1,0:T(8,128)(2,1)} %bitcast.32.rows_ref, bf16[2048,384]{1,0:T(8,128)(2,1)} %bitcast.44, bf16[2048,384]{1,0:T(8,128)(2,1)} %collective-permute-done.14.refs_1_, bf16[2048,384]{1,0:T(8,128)(2,1)} %bitcast.48, bf16[2048,384]{1,0:T(8,128)(2,1)} %collective-permute-done.15.refs_3_, ...), custom_call_target="tpu_custom_call" | custom-call | tf_op jit(solution)/shard_map/expert_rows/pallas_call | solution.py:629
  206.7 7.4 %all-to-all-done.2 = bf16[16,24,2048]{2,1,0:T(8,128)(2,1)} async-done(((bf16[16,24,2048]{2,1,0:T(8,128)(2,1)}), bf16[16,24,2048]{2,1,0:T(8,128)(2,1)}, u32[]{:S(2)}, u32[]{:S(2)}) %all-to-all-start.2) | async-done | bytes 1572896 | tf_op jit(solution)/shard_map/all_to_all | solution.py:784
  214.1 5.4 %all-to-all-start.5 = ((bf16[16,24,2048]{2,1,0:T(8,128)(2,1)}), bf16[16,24,2048]{2,1,0:T(8,128)(2,1)S(1)}, u32[]{:S(2)}, u32[]{:S(2)}) async-start(bf16[16,24,2048]{2,1,0:T(8,128)(2,1)} %bitcast.54), calls=%async_computation.5 | async-start | bytes 3145728 | tf_op jit(solution)/shard_map/all_to_all | solution.py:791
  219.5 11.1 %expert_rows.2 = bf16[384,2048]{1,0:T(8,128)(2,1)} custom-call(bf16[384,2048]{1,0:T(8,128)(2,1)} %bitcast.25.rows_ref, bf16[2048,384]{1,0:T(8,128)(2,1)} %bitcast.45, bf16[2048,384]{1,0:T(8,128)(2,1)} %collective-permute-done.14.refs_1_, bf16[2048,384]{1,0:T(8,128)(2,1)} %bitcast.49, bf16[2048,384]{1,0:T(8,128)(2,1)} %collective-permute-done.15.refs_3_, ...), custom_call_target="tpu_custom_call" | custom-call | tf_op jit(solution)/shard_map/expert_rows/pallas_call | solution.py:629
  230.6 6.5 %all-to-all-done.5 = bf16[16,24,2048]{2,1,0:T(8,128)(2,1)S(1)} async-done(((bf16[16,24,2048]{2,1,0:T(8,128)(2,1)}), bf16[16,24,2048]{2,1,0:T(8,128)(2,1)S(1)}, u32[]{:S(2)}, u32[]{:S(2)}) %all-to-all-start.5) | async-done | bytes 1572896 | tf_op jit(solution)/shard_map/all_to_all | solution.py:791
  237.1 5.6 %all-to-all-start.3 = ((bf16[16,24,2048]{2,1,0:T(8,128)(2,1)}), bf16[16,24,2048]{2,1,0:T(8,128)(2,1)S(1)}, u32[]{:S(2)}, u32[]{:S(2)}) async-start(bf16[16,24,2048]{2,1,0:T(8,128)(2,1)} %bitcast.53), calls=%async_computation.3 | async-start | bytes 3145728 | tf_op jit(solution)/shard_map/all_to_all | solution.py:791
  242.7 0.9 mixed.3
  243.9 1.4 collective-permute-start.21
  245.3 1.9 collective-permute-start.25
  247.2 6.2 %collective-permute-done.21 = bf16[64,2048]{1,0:T(8,128)(2,1)S(1)} collective-permute-done((bf16[64,2048]{1,0:T(8,128)(2,1)S(1)}, bf16[64,2048]{1,0:T(8,128)(2,1)S(1)}, u32[]{:S(2)}, u32[]{:S(2)}) %collective-permute-start.21) | collective-permute-done | bytes 262176 | tf_op jit(solution)/shard_map/ppermute | solution.py:33
  254.4 4.8 %all-to-all-done.3 = bf16[16,24,2048]{2,1,0:T(8,128)(2,1)S(1)} async-done(((bf16[16,24,2048]{2,1,0:T(8,128)(2,1)}), bf16[16,24,2048]{2,1,0:T(8,128)(2,1)S(1)}, u32[]{:S(2)}, u32[]{:S(2)}) %all-to-all-start.3) | async-done | bytes 1572896 | tf_op jit(solution)/shard_map/all_to_all | solution.py:791
  259.2 0.9 mixed.2
  261.2 2.5 collective-permute-start.23
  263.7 4.2 %collective-permute-done.26 = bf16[64,2048]{1,0:T(8,128)(2,1)S(1)} collective-permute-done((bf16[64,2048]{1,0:T(8,128)(2,1)S(1)}, bf16[64,2048]{1,0:T(8,128)(2,1)S(1)}, u32[]{:S(2)}, u32[]{:S(2)}) %collective-permute-start.26) | collective-permute-done | bytes 262176 | tf_op jit(solution)/shard_map/ppermute | solution.py:33
  267.9 3.2 %collective-permute-done.23 = bf16[64,2048]{1,0:T(8,128)(2,1)S(1)} collective-permute-done((bf16[64,2048]{1,0:T(8,128)(2,1)S(1)}, bf16[64,2048]{1,0:T(8,128)(2,1)S(1)}, u32[]{:S(2)}, u32[]{:S(2)}) %collective-permute-start.23) | collective-permute-done | bytes 262176 | tf_op jit(solution)/shard_map/ppermute | solution.py:33
  271.2 1.1 collective-permute-start.24
  272.3 2.6 collective-permute-start.27
  274.9 4.3 %collective-permute-done.24 = bf16[64,2048]{1,0:T(8,128)(2,1)S(1)} collective-permute-done((bf16[64,2048]{1,0:T(8,128)(2,1)S(1)}, bf16[64,2048]{1,0:T(8,128)(2,1)S(1)}, u32[]{:S(2)}, u32[]{:S(2)}) %collective-permute-start.24) | collective-permute-done | bytes 262176 | tf_op jit(solution)/shard_map/ppermute | solution.py:33
  (70 shorter events, 6.5 us)
Async XLA Ops:
  0.6 38.9 %collective-permute-start.7 = (bf16[512,2048]{1,0:T(8,128)(2,1)}, bf16[512,2048]{1,0:T(8,128)(2,1)}, u32[]{:S(2)}, u32[]{:S(2)}) collective-permute-start(bf16[512,2048]{1,0:T(8,128)(2,1)} %w_own.1), channel_id=1, source_target_pairs={{0,1},{1,2},{2,3},{3,0},{128,131},{129,128},{130,129},{131,130},{4... | collective-permute-start | bytes 6291464 | tf_op jit(solution)/shard_map/ppermute | solution.py:719
  11.4 45.0 %copy-start.4 = (bf16[128,512]{1,0:T(8,128)(2,1)S(1)}, bf16[128,512]{1,0:T(8,128)(2,1)}, u32[]{:S(2)}) copy-start(bf16[128,512]{1,0:T(8,128)(2,1)} %get-tuple-element.16.refs_0_) | copy-start | bytes 393220
  11.4 64.2 %collective-permute-start.9 = (bf16[256,2048]{1,0:T(8,128)(2,1)}, bf16[256,2048]{1,0:T(8,128)(2,1)S(1)}, u32[]{:S(2)}, u32[]{:S(2)}) collective-permute-start(bf16[256,2048]{1,0:T(8,128)(2,1)} %get-tuple-element.19), channel_id=1, source_target_pairs={{0,2},{1,3},{2,0},{3,1},{4,6},{5,7},{6,4},{7,5},{8,10},{9,11},{10,... | collective-permute-start | bytes 3145736 | tf_op jit(solution)/shard_map/ppermute | solution.py:33
  39.5 79.6 %collective-permute-start.8 = (bf16[512,2048]{1,0:T(8,128)(2,1)}, bf16[512,2048]{1,0:T(8,128)(2,1)}, u32[]{:S(2)}, u32[]{:S(2)}) collective-permute-start(bf16[512,2048]{1,0:T(8,128)(2,1)} %collective-permute-done.7.w_near_own), channel_id=1, source_target_pairs={{0,128},{128,0},{1,129},{129,1},{2,130},{130,2},{3,131},{131,3},{4... | collective-permute-start | bytes 6291464 | tf_op jit(solution)/shard_map/ppermute | solution.py:721
  48.8 26.9 %all-to-all-start = ((bf16[4,512,256]{2,1,0:T(8,128)(2,1)}), bf16[4,512,256]{2,1,0:T(8,128)(2,1)S(1)}, u32[]{:S(2)}, u32[]{:S(2)}) async-start(bf16[4,512,256]{2,1,0:T(8,128)(2,1)} %get-tuple-element.15), calls=%async_computation | async-start | bytes 2097152 | tf_op jit(solution)/shard_map/all_to_all | solution.py:725
  56.4 6.8 %collective-permute-start.3 = (bf16[128,512]{1,0:T(8,128)(2,1)S(1)}, bf16[128,512]{1,0:T(8,128)(2,1)S(1)}, u32[]{:S(2)}, u32[]{:S(2)}) collective-permute-start(bf16[128,512]{1,0:T(8,128)(2,1)S(1)} %copy-done.4), channel_id=1, source_target_pairs={{0,16},{16,32},{32,48},{48,64},{64,80},{80,96},{96,112},{112,0},{1... | collective-permute-start | bytes 393224 | tf_op jit(solution)/shard_map/ppermute | solution.py:33
  56.4 6.8 %collective-permute-start = (bf16[128,512]{1,0:T(8,128)(2,1)S(1)}, bf16[128,512]{1,0:T(8,128)(2,1)S(1)}, u32[]{:S(2)}, u32[]{:S(2)}) collective-permute-start(bf16[128,512]{1,0:T(8,128)(2,1)S(1)} %copy-done.4), channel_id=1, source_target_pairs={{0,112},{16,0},{32,16},{48,32},{64,48},{80,64},{96,80},{112,96},{1... | collective-permute-start | bytes 393224 | tf_op jit(solution)/shard_map/ppermute | solution.py:33
  63.2 6.2 %collective-permute-start.4 = (bf16[128,512]{1,0:T(8,128)(2,1)S(1)}, bf16[128,512]{1,0:T(8,128)(2,1)S(1)}, u32[]{:S(2)}, u32[]{:S(2)}) collective-permute-start(bf16[128,512]{1,0:T(8,128)(2,1)S(1)} %collective-permute-done.3.refs_1_), channel_id=1, source_target_pairs={{0,16},{16,32},{32,48},{48,64},{64,80},{80,96},{96,112},{112,0},{1... | collective-permute-start | bytes 393224 | tf_op jit(solution)/shard_map/ppermute | solution.py:33
  63.2 6.2 %collective-permute-start.1 = (bf16[128,512]{1,0:T(8,128)(2,1)S(1)}, bf16[128,512]{1,0:T(8,128)(2,1)S(1)}, u32[]{:S(2)}, u32[]{:S(2)}) collective-permute-start(bf16[128,512]{1,0:T(8,128)(2,1)S(1)} %collective-permute-done.refs_2_), channel_id=1, source_target_pairs={{0,112},{16,0},{32,16},{48,32},{64,48},{80,64},{96,80},{112,96},{1... | collective-permute-start | bytes 393224 | tf_op jit(solution)/shard_map/ppermute | solution.py:33
  69.4 6.2 %collective-permute-start.5 = (bf16[128,512]{1,0:T(8,128)(2,1)S(1)}, bf16[128,512]{1,0:T(8,128)(2,1)S(1)}, u32[]{:S(2)}, u32[]{:S(2)}) collective-permute-start(bf16[128,512]{1,0:T(8,128)(2,1)S(1)} %collective-permute-done.4.refs_3_), channel_id=1, source_target_pairs={{0,16},{16,32},{32,48},{48,64},{64,80},{80,96},{96,112},{112,0},{1... | collective-permute-start | bytes 393224 | tf_op jit(solution)/shard_map/ppermute | solution.py:33
  69.4 16.0 %collective-permute-start.2 = (bf16[128,512]{1,0:T(8,128)(2,1)S(1)}, bf16[128,512]{1,0:T(8,128)(2,1)S(1)}, u32[]{:S(2)}, u32[]{:S(2)}) collective-permute-start(bf16[128,512]{1,0:T(8,128)(2,1)S(1)} %collective-permute-done.1.refs_4_), channel_id=1, source_target_pairs={{0,112},{16,0},{32,16},{48,32},{64,48},{80,64},{96,80},{112,96},{1... | collective-permute-start | bytes 393224 | tf_op jit(solution)/shard_map/ppermute | solution.py:33
  75.6 9.8 %collective-permute-start.6 = (bf16[128,512]{1,0:T(8,128)(2,1)S(1)}, bf16[128,512]{1,0:T(8,128)(2,1)S(1)}, u32[]{:S(2)}, u32[]{:S(2)}) collective-permute-start(bf16[128,512]{1,0:T(8,128)(2,1)S(1)} %collective-permute-done.5.refs_5_), channel_id=1, source_target_pairs={{0,16},{16,32},{32,48},{48,64},{64,80},{80,96},{96,112},{112,0},{1... | collective-permute-start | bytes 393224 | tf_op jit(solution)/shard_map/ppermute | solution.py:33
  75.6 43.5 %collective-permute-start.10 = (bf16[256,2048]{1,0:T(8,128)(2,1)S(1)}, bf16[256,2048]{1,0:T(8,128)(2,1)}, u32[]{:S(2)}, u32[]{:S(2)}) collective-permute-start(bf16[256,2048]{1,0:T(8,128)(2,1)S(1)} %collective-permute-done.9.w_far_own), channel_id=1, source_target_pairs={{0,128},{128,0},{1,129},{129,1},{2,130},{130,2},{3,131},{131,3},{4... | collective-permute-start | bytes 3145736 | tf_op jit(solution)/shard_map/ppermute | solution.py:722
  94.2 7.3 %copy-start.7 = (f32[32,8]{0,1:T(8,128)S(1)}, f32[32,8]{0,1:T(8,128)}, u32[]{:S(2)}) copy-start(f32[32,8]{0,1:T(8,128)} %param.29) | copy-start | bytes 3076
  94.2 7.3 %copy-start.8 = (s32[32,8]{0,1:T(8,128)S(1)}, s32[32,8]{0,1:T(8,128)}, u32[]{:S(2)}) copy-start(s32[32,8]{0,1:T(8,128)} %param.28) | copy-start | bytes 3076
  94.2 24.9 %copy-start = (bf16[128,2048]{1,0:T(8,128)(2,1)S(1)}, bf16[128,2048]{1,0:T(8,128)(2,1)}, u32[]{:S(2)}) copy-start(bf16[128,2048]{1,0:T(8,128)(2,1)} %tokens_ref.3) | copy-start | bytes 1572868
  94.2 24.9 %copy-start.1 = (bf16[128,2048]{1,0:T(8,128)(2,1)S(1)}, bf16[128,2048]{1,0:T(8,128)(2,1)}, u32[]{:S(2)}) copy-start(bf16[128,2048]{1,0:T(8,128)(2,1)} %tangents_ref.3) | copy-start | bytes 1572868
  94.2 24.9 %copy-start.5 = (f32[2048]{0:T(1024)S(1)}, f32[2048]{0:T(1024)}, u32[]{:S(2)}) copy-start(f32[2048]{0:T(1024)} %param.18) | copy-start | bytes 24580
  94.2 24.9 %all-to-all-start.1 = ((bf16[16,136,256]{2,1,0:T(8,128)(2,1)}), bf16[16,136,256]{2,1,0:T(8,128)(2,1)S(1)}, u32[]{:S(2)}, u32[]{:S(2)}) async-start(bf16[16,136,256]{2,1,0:T(8,128)(2,1)} %attend.3), calls=%async_computation.1 | async-start | bytes 2228224 | tf_op jit(solution)/shard_map/all_to_all | solution.py:747
  125.9 0.8 copy-start.2
  126.7 9.5 %collective-permute-start.12 = (bf16[72,2048]{1,0:T(8,128)(2,1)S(1)}, bf16[72,2048]{1,0:T(8,128)(2,1)S(1)}, u32[]{:S(2)}, u32[]{:S(2)}) collective-permute-start(bf16[72,2048]{1,0:T(8,128)(2,1)S(1)} %get-tuple-element.21.refs_0_), channel_id=1, source_target_pairs={{0,16},{16,32},{32,48},{48,64},{64,80},{80,96},{96,112},{112,0},{1... | collective-permute-start | bytes 884744 | tf_op jit(solution)/shard_map/ppermute | solution.py:33
  126.7 9.5 %collective-permute-start.11 = (bf16[72,2048]{1,0:T(8,128)(2,1)S(1)}, bf16[72,2048]{1,0:T(8,128)(2,1)S(1)}, u32[]{:S(2)}, u32[]{:S(2)}) collective-permute-start(bf16[72,2048]{1,0:T(8,128)(2,1)S(1)} %get-tuple-element.21.refs_0_), channel_id=1, source_target_pairs={{0,112},{16,0},{32,16},{48,32},{64,48},{80,64},{96,80},{112,96},{1... | collective-permute-start | bytes 884744 | tf_op jit(solution)/shard_map/ppermute | solution.py:33
  136.1 8.6 %collective-permute-start.17 = (bf16[72,2048]{1,0:T(8,128)(2,1)S(1)}, bf16[72,2048]{1,0:T(8,128)(2,1)S(1)}, u32[]{:S(2)}, u32[]{:S(2)}) collective-permute-start(bf16[72,2048]{1,0:T(8,128)(2,1)S(1)} %collective-permute-done.12.refs_2_), channel_id=1, source_target_pairs={{0,16},{16,32},{32,48},{48,64},{64,80},{80,96},{96,112},{112,0},{1... | collective-permute-start | bytes 884744 | tf_op jit(solution)/shard_map/ppermute | solution.py:33
  136.1 8.8 %collective-permute-start.13 = (bf16[72,2048]{1,0:T(8,128)(2,1)S(1)}, bf16[72,2048]{1,0:T(8,128)(2,1)S(1)}, u32[]{:S(2)}, u32[]{:S(2)}) collective-permute-start(bf16[72,2048]{1,0:T(8,128)(2,1)S(1)} %collective-permute-done.11.refs_1_), channel_id=1, source_target_pairs={{0,112},{16,0},{32,16},{48,32},{64,48},{80,64},{96,80},{112,96},{1... | collective-permute-start | bytes 884744 | tf_op jit(solution)/shard_map/ppermute | solution.py:33
  144.7 7.9 %collective-permute-start.19 = (bf16[72,2048]{1,0:T(8,128)(2,1)S(1)}, bf16[72,2048]{1,0:T(8,128)(2,1)S(1)}, u32[]{:S(2)}, u32[]{:S(2)}) collective-permute-start(bf16[72,2048]{1,0:T(8,128)(2,1)S(1)} %collective-permute-done.17.refs_0_), channel_id=1, source_target_pairs={{0,16},{16,32},{32,48},{48,64},{64,80},{80,96},{96,112},{112,0},{1... | collective-permute-start | bytes 884744 | tf_op jit(solution)/shard_map/ppermute | solution.py:33
  145.0 7.7 %collective-permute-start.18 = (bf16[72,2048]{1,0:T(8,128)(2,1)S(1)}, bf16[72,2048]{1,0:T(8,128)(2,1)S(1)}, u32[]{:S(2)}, u32[]{:S(2)}) collective-permute-start(bf16[72,2048]{1,0:T(8,128)(2,1)S(1)} %collective-permute-done.13.refs_3_), channel_id=1, source_target_pairs={{0,112},{16,0},{32,16},{48,32},{64,48},{80,64},{96,80},{112,96},{1... | collective-permute-start | bytes 884744 | tf_op jit(solution)/shard_map/ppermute | solution.py:33
  152.7 7.9 %collective-permute-start.20 = (bf16[72,2048]{1,0:T(8,128)(2,1)S(1)}, bf16[72,2048]{1,0:T(8,128)(2,1)S(1)}, u32[]{:S(2)}, u32[]{:S(2)}) collective-permute-start(bf16[72,2048]{1,0:T(8,128)(2,1)S(1)} %collective-permute-done.19.refs_2_), channel_id=1, source_target_pairs={{0,16},{16,32},{32,48},{48,64},{64,80},{80,96},{96,112},{112,0},{1... | collective-permute-start | bytes 884744 | tf_op jit(solution)/shard_map/ppermute | solution.py:33
  162.6 7.9 %copy-start.6 = (bf16[1,2048,384]{2,1,0:T(8,128)(2,1)S(1)}, bf16[1,2048,384]{2,1,0:T(8,128)(2,1)}, u32[]{:S(2)}) copy-start(bf16[1,2048,384]{2,1,0:T(8,128)(2,1)} %param.25) | copy-start | bytes 4718596
  162.6 26.3 %all-to-all-start.4 = ((bf16[16,24,2048]{2,1,0:T(8,128)(2,1)}), bf16[16,24,2048]{2,1,0:T(8,128)(2,1)}, u32[]{:S(2)}, u32[]{:S(2)}) async-start(bf16[16,24,2048]{2,1,0:T(8,128)(2,1)} %bitcast.31), calls=%async_computation.4 | async-start | bytes 3145728 | tf_op jit(solution)/shard_map/all_to_all | solution.py:784
  170.4 25.1 %collective-permute-start.14 = (bf16[2048,384]{1,0:T(8,128)(2,1)S(1)}, bf16[2048,384]{1,0:T(8,128)(2,1)}, u32[]{:S(2)}, u32[]{:S(2)}) collective-permute-start(bf16[2048,384]{1,0:T(8,128)(2,1)S(1)} %bitcast.46), channel_id=1, source_target_pairs={{0,128},{128,0},{1,129},{129,1},{2,130},{130,2},{3,131},{131,3},{4... | collective-permute-start | bytes 4718600 | tf_op jit(solution)/shard_map/ppermute | solution.py:671
  170.5 25.0 %collective-permute-start.15 = (bf16[2048,384]{1,0:T(8,128)(2,1)}, bf16[2048,384]{1,0:T(8,128)(2,1)}, u32[]{:S(2)}, u32[]{:S(2)}) collective-permute-start(bf16[2048,384]{1,0:T(8,128)(2,1)} %bitcast.47), channel_id=1, source_target_pairs={{0,128},{128,0},{1,129},{129,1},{2,130},{130,2},{3,131},{131,3},{4... | collective-permute-start | bytes 4718600 | tf_op jit(solution)/shard_map/ppermute | solution.py:671
  171.0 24.6 %collective-permute-start.16 = (bf16[2048,384]{1,0:T(8,128)(2,1)}, bf16[2048,384]{1,0:T(8,128)(2,1)}, u32[]{:S(2)}, u32[]{:S(2)}) collective-permute-start(bf16[2048,384]{1,0:T(8,128)(2,1)} %bitcast.50), channel_id=1, source_target_pairs={{0,128},{128,0},{1,129},{129,1},{2,130},{130,2},{3,131},{131,3},{4... | collective-permute-start | bytes 4718600 | tf_op jit(solution)/shard_map/ppermute | solution.py:671
  188.9 25.3 %all-to-all-start.2 = ((bf16[16,24,2048]{2,1,0:T(8,128)(2,1)}), bf16[16,24,2048]{2,1,0:T(8,128)(2,1)}, u32[]{:S(2)}, u32[]{:S(2)}) async-start(bf16[16,24,2048]{2,1,0:T(8,128)(2,1)} %bitcast.24), calls=%async_computation.2 | async-start | bytes 3145728 | tf_op jit(solution)/shard_map/all_to_all | solution.py:784
  214.1 23.0 %all-to-all-start.5 = ((bf16[16,24,2048]{2,1,0:T(8,128)(2,1)}), bf16[16,24,2048]{2,1,0:T(8,128)(2,1)S(1)}, u32[]{:S(2)}, u32[]{:S(2)}) async-start(bf16[16,24,2048]{2,1,0:T(8,128)(2,1)} %bitcast.54), calls=%async_computation.5 | async-start | bytes 3145728 | tf_op jit(solution)/shard_map/all_to_all | solution.py:791
  237.1 22.1 %all-to-all-start.3 = ((bf16[16,24,2048]{2,1,0:T(8,128)(2,1)}), bf16[16,24,2048]{2,1,0:T(8,128)(2,1)S(1)}, u32[]{:S(2)}, u32[]{:S(2)}) async-start(bf16[16,24,2048]{2,1,0:T(8,128)(2,1)} %bitcast.53), calls=%async_computation.3 | async-start | bytes 3145728 | tf_op jit(solution)/shard_map/all_to_all | solution.py:791
  243.9 9.5 %collective-permute-start.21 = (bf16[64,2048]{1,0:T(8,128)(2,1)S(1)}, bf16[64,2048]{1,0:T(8,128)(2,1)S(1)}, u32[]{:S(2)}, u32[]{:S(2)}) collective-permute-start(bf16[64,2048]{1,0:T(8,128)(2,1)S(1)} %get-tuple-element.30), channel_id=1, source_target_pairs={{0,16},{16,32},{32,48},{48,64},{64,80},{80,96},{96,112},{112,0},{1... | collective-permute-start | bytes 786440 | tf_op jit(solution)/shard_map/ppermute | solution.py:33
  245.3 8.1 %collective-permute-start.25 = (bf16[64,2048]{1,0:T(8,128)(2,1)S(1)}, bf16[64,2048]{1,0:T(8,128)(2,1)S(1)}, u32[]{:S(2)}, u32[]{:S(2)}) collective-permute-start(bf16[64,2048]{1,0:T(8,128)(2,1)S(1)} %get-tuple-element.31), channel_id=1, source_target_pairs={{0,112},{16,0},{32,16},{48,32},{64,48},{80,64},{96,80},{112,96},{1... | collective-permute-start | bytes 786440 | tf_op jit(solution)/shard_map/ppermute | solution.py:33
  253.5 7.7 %collective-permute-start.22 = (bf16[64,2048]{1,0:T(8,128)(2,1)S(1)}, bf16[64,2048]{1,0:T(8,128)(2,1)S(1)}, u32[]{:S(2)}, u32[]{:S(2)}) collective-permute-start(bf16[64,2048]{1,0:T(8,128)(2,1)S(1)} %get-tuple-element.28), channel_id=1, source_target_pairs={{0,16},{16,32},{32,48},{48,64},{64,80},{80,96},{96,112},{112,0},{1... | collective-permute-start | bytes 786440 | tf_op jit(solution)/shard_map/ppermute | solution.py:33
  260.1 19.1 %copy-start.3 = (f32[64,2048]{1,0:T(8,128)S(1)}, f32[64,2048]{1,0:T(8,128)}, u32[]{:S(2)}) copy-start(f32[64,2048]{1,0:T(8,128)} %copy-done.2) | copy-start | bytes 1572868
  260.1 7.8 %collective-permute-start.26 = (bf16[64,2048]{1,0:T(8,128)(2,1)S(1)}, bf16[64,2048]{1,0:T(8,128)(2,1)S(1)}, u32[]{:S(2)}, u32[]{:S(2)}) collective-permute-start(bf16[64,2048]{1,0:T(8,128)(2,1)S(1)} %get-tuple-element.29), channel_id=1, source_target_pairs={{0,112},{16,0},{32,16},{48,32},{64,48},{80,64},{96,80},{112,96},{1... | collective-permute-start | bytes 786440 | tf_op jit(solution)/shard_map/ppermute | solution.py:33
  261.2 9.9 %collective-permute-start.23 = (bf16[64,2048]{1,0:T(8,128)(2,1)S(1)}, bf16[64,2048]{1,0:T(8,128)(2,1)S(1)}, u32[]{:S(2)}, u32[]{:S(2)}) collective-permute-start(bf16[64,2048]{1,0:T(8,128)(2,1)S(1)} %fusion.3), channel_id=1, source_target_pairs={{0,16},{16,32},{32,48},{48,64},{64,80},{80,96},{96,112},{112,0},{1... | collective-permute-start | bytes 786440 | tf_op jit(solution)/shard_map/ppermute | solution.py:33
  271.2 7.9 %collective-permute-start.24 = (bf16[64,2048]{1,0:T(8,128)(2,1)S(1)}, bf16[64,2048]{1,0:T(8,128)(2,1)S(1)}, u32[]{:S(2)}, u32[]{:S(2)}) collective-permute-start(bf16[64,2048]{1,0:T(8,128)(2,1)S(1)} %get-tuple-element.26), channel_id=1, source_target_pairs={{0,16},{16,32},{32,48},{48,64},{64,80},{80,96},{96,112},{112,0},{1... | collective-permute-start | bytes 786440 | tf_op jit(solution)/shard_map/ppermute | solution.py:33
  272.3 6.9 %collective-permute-start.27 = (bf16[64,2048]{1,0:T(8,128)(2,1)S(1)}, bf16[64,2048]{1,0:T(8,128)(2,1)S(1)}, u32[]{:S(2)}, u32[]{:S(2)}) collective-permute-start(bf16[64,2048]{1,0:T(8,128)(2,1)S(1)} %get-tuple-element.27), channel_id=1, source_target_pairs={{0,112},{16,0},{32,16},{48,32},{64,48},{80,64},{96,80},{112,96},{1... | collective-permute-start | bytes 786440 | tf_op jit(solution)/shard_map/ppermute | solution.py:33

commit v4 on v3

--- a/solution.py
+++ b/solution.py
@@ -59,6 +59,8 @@
     blocks, refs = refs[:count], refs[count:]
     if first:
         sums_ref, figures_ref, held_ref, score_ref = refs
+    elif first is None:
+        out_ref, held_ref, score_ref = refs
     else:
         old_sums_ref, old_figures_ref, out_ref, held_ref, score_ref = refs
     rows, width = joint_ref.shape[0], joint_ref.shape[1] // 2
@@ -91,7 +93,7 @@
         score_ref[number] = score
         top = jnp.maximum(top, score)
     top = jnp.max(top, axis=1, keepdims=True)
-    if not first:
+    if first is False:
         old_top = old_figures_ref[:, :1]
         top = jnp.maximum(top, old_top)
     total = jnp.zeros(shape, jnp.float32)
@@ -125,11 +127,14 @@
         sums_ref[:, width:] = sums[:, width:] + tilted
         figures_ref[...] = jnp.where(lane == 0, top, jnp.where(lane == 1, total, slope))
         return
-    fade = jnp.exp(old_top - top)
-    total = total + fade * old_figures_ref[:, 1:2]
-    slope = slope + fade * old_figures_ref[:, 2:3]
-    primal = sums[:, :width] + fade * old_sums_ref[:, :width]
-    tangent = sums[:, width:] + tilted + fade * old_sums_ref[:, width:]
+    primal = sums[:, :width]
+    tangent = sums[:, width:] + tilted
+    if first is False:
+        fade = jnp.exp(old_top - top)
+        total = total + fade * old_figures_ref[:, 1:2]
+        slope = slope + fade * old_figures_ref[:, 2:3]
+        primal = primal + fade * old_sums_ref[:, :width]
+        tangent = tangent + fade * old_sums_ref[:, width:]
     some = total > 0.0
     share = jnp.where(some, 1.0 / jnp.where(some, total, 1.0), 0.0)
     output = primal * share
@@ -155,7 +160,7 @@
     whole = pl.BlockSpec(blocks[0].shape, lambda i: (0, 0))
     row_block = pl.BlockSpec((rows, width), lambda i: (i, 0))
     half_block = pl.BlockSpec((rows, width // 2), lambda i: (i, 0))
-    first = not state
+    first = None if state is None else not state
     if first:
         out_specs = (row_block, half_block)
         out_shape = (
@@ -173,7 +178,7 @@
             pl.BlockSpec(memory_space=pltpu.SMEM),
             row_block,
             *[whole] * len(blocks),
-            *([] if first else [row_block, half_block]),
+            *([row_block, half_block] if state else []),
         ],
         out_specs=out_specs,
         out_shape=out_shape,
@@ -183,7 +188,7 @@
         ],
         compiler_params=pltpu.CompilerParams(vmem_limit_bytes=40 << 20),
         name="attend",
-    )(spans, joint_query, *blocks, *state)
+    )(spans, joint_query, *blocks, *(state or ()))
 
 
 def merge_kernel(
@@ -726,8 +731,8 @@
     joint_query = joint_query.reshape(row_groups * own_rows, 2 * head_width)
     receivers = row_groups * head_count
     rows_each = heads_here * moe_rows
-    state = ()
-    for order in ((0, -1, 1, -2, 2, -3), (3, -4)):
+    state = None
+    for order in ((0, -1, 1, -2, 2, -3, 3, -4),):
         spans = [
             (lax.rem(plane + k + plane_count, plane_count) - plane) * plane_rows
             + row_in_plane * tok_count

time: 283 us -> 273 us (0.965)
  Pallas kernels: 61.2 us -> 55.1 us
  starting transfers between devices: 84.6 us -> 81.6 us
    ppermute x22, waiting for transfers between devices: 52.6 us -> 64.4 us  [shifted(): lax.ppermute(array, axis, [(i, (i + offset) % size) for i in range(size)])]
    pallas_call x2 -> x1, Pallas kernels: 18.4 us -> 12.4 us  [attend(): pl.pallas_call(functools.partial(attend_kernel, scale, group_rows, moe_ro...]
    all_to_all x2, waiting for transfers between devices: 23.3 us -> 17.3 us  [layer(): received = lax.all_to_all(outgoing, ('seq_1', 'head'), 0, 0, tiled=True)]
    all_to_all x1, waiting for transfers between devices: 17.3 us -> 11.8 us  [layer(): arrived = lax.all_to_all(sent, ('seq_1', 'head'), 0, 0, tiled=True)]
  transfers between devices with their start and end apart: 34 -> 34, of which waited for: 19 -> 20; matrix products, arithmetic and copies ran while one was open for 1% -> 1% of each run, Pallas kernels for 19% -> 17%
where the time goes in v4:
time: 273 us; the launch traced here: 271 us
  waiting for transfers between devices  130 us (48%)
  starting transfers between devices  81.6 us (30%)
  Pallas kernels  55.1 us (20%)
    ppermute x22, waiting for transfers between devices, shifted(): lax.ppermute(array, axis, [(i, (i + offset) % size) for i in range(size)])  64.4 us
    ppermute x22, starting transfers between devices, shifted(): lax.ppermute(array, axis, [(i, (i + offset) % size) for i in range(size)])  29.8 us
    ppermute x1, waiting for transfers between devices, layer(): near_own = lax.ppermute(w_out, ('dp', 'head'), sides)  25.3 us
    pallas_call x2, Pallas kernels, expert_rows(): pl.pallas_call(expert_kernel, in_specs=[vmem] + [hbm] * 6, out_specs=vmem...  22.1 us
    all_to_all x2, waiting for transfers between devices, layer(): received = lax.all_to_all(outgoing, ('seq_1', 'head'), 0, 0, tiled=True)  17.3 us
    all_to_all x2, starting transfers between devices, layer(): received = lax.all_to_all(outgoing, ('seq_1', 'head'), 0, 0, tiled=True)  14.1 us
    pallas_call x1, Pallas kernels, attend(): pl.pallas_call(functools.partial(attend_kernel, scale, group_rows, moe_ro...  12.4 us
    all_to_all x1, waiting for transfers between devices, layer(): arrived = lax.all_to_all(sent, ('seq_1', 'head'), 0, 0, tiled=True)  11.8 us
  transfers between devices with their start and end apart: 34, of which 20 were waited for; matrix products, arithmetic and copies ran while one was open for 1% of the time, Pallas kernels for 17%

profile of v4, /device:TPU:8, one launch (start us, length us, event | category | flops | bytes accessed | tf_op | source)
XLA Modules:
  0.0 271.2 jit_solution(6078700600882627077)
XLA Ops:
  0.6 1.6 collective-permute-start.7
  2.5 0.7 pad_maximum_fusion
  3.3 3.6 %keys_of.1 = (bf16[256,2048]{1,0:T(8,128)(2,1)}, bf16[128,512]{1,0:T(8,128)(2,1)}) custom-call(s32[1]{0:T(128)} %bitcast.13.head_ref, bf16[128,2048]{1,0:T(8,128)(2,1)} %tokens_ref.3, bf16[128,2048]{1,0:T(8,128)(2,1)} %tangents_ref.3, f32[1,2048]{1,0:T(1,128)} %bitcast.54, bf16[2048,256]{1,0:T(8,128)(2,1)} %w_key_ref.1, bf16[2048,256]{1,0:T(8,128)(2,1)} %w_value_ref.1, ...), custom_call_target="tpu_custom_call" | custom-call | tf_op jit(solution)/shard_map/keys_of/pallas_call | solution.py:373
  6.9 4.5 %queries_of.1 = (bf16[4,512,256]{2,1,0:T(8,128)(2,1)}, bf16[256,2048]{1,0:T(8,128)(2,1)}) custom-call(s32[1]{0:T(128)} %bitcast.4.core_ref, bf16[256,2048]{1,0:T(8,128)(2,1)} %get-tuple-element.12.stacked_ref, bf16[2048,512]{1,0:T(8,128)(2,1)} %weight_ref.1, f32[1,128]{1,0:T(1,128)} %bitcast.56, f32[128,128]{1,0:T(8,128)} %get-tuple-element.33.cosine_ref, ...), custom_call_target="tpu_custom_call" | custom-call | tf_op jit(solution)/shard_map/queries_of/pallas_call | solution.py:441
  11.4 2.8 %collective-permute-start.9 = (bf16[256,2048]{1,0:T(8,128)(2,1)}, bf16[256,2048]{1,0:T(8,128)(2,1)S(1)}, u32[]{:S(2)}, u32[]{:S(2)}) collective-permute-start(bf16[256,2048]{1,0:T(8,128)(2,1)} %get-tuple-element.15), channel_id=1, source_target_pairs={{0,2},{1,3},{2,0},{3,1},{4,6},{5,7},{6,4},{7,5},{8,10},{9,11},{10,... | collective-permute-start | bytes 3145736 | tf_op jit(solution)/shard_map/ppermute | solution.py:33
  14.2 25.3 %collective-permute-done.7.w_near_own = bf16[512,2048]{1,0:T(8,128)(2,1)} collective-permute-done((bf16[512,2048]{1,0:T(8,128)(2,1)}, bf16[512,2048]{1,0:T(8,128)(2,1)}, u32[]{:S(2)}, u32[]{:S(2)}) %collective-permute-start.7) | collective-permute-done | bytes 2097184 | tf_op jit(solution)/shard_map/ppermute | solution.py:724
  39.5 9.3 %collective-permute-start.8 = (bf16[512,2048]{1,0:T(8,128)(2,1)}, bf16[512,2048]{1,0:T(8,128)(2,1)}, u32[]{:S(2)}, u32[]{:S(2)}) collective-permute-start(bf16[512,2048]{1,0:T(8,128)(2,1)} %collective-permute-done.7.w_near_own), channel_id=1, source_target_pairs={{0,128},{128,0},{1,129},{129,1},{2,130},{130,2},{3,131},{131,3},{4... | collective-permute-start | bytes 6291464 | tf_op jit(solution)/shard_map/ppermute | solution.py:726
  48.8 7.6 %all-to-all-start = ((bf16[4,512,256]{2,1,0:T(8,128)(2,1)}), bf16[4,512,256]{2,1,0:T(8,128)(2,1)S(1)}, u32[]{:S(2)}, u32[]{:S(2)}) async-start(bf16[4,512,256]{2,1,0:T(8,128)(2,1)} %get-tuple-element.13), calls=%async_computation | async-start | bytes 2097152 | tf_op jit(solution)/shard_map/all_to_all | solution.py:730
  56.4 3.2 %collective-permute-start.1 = (bf16[128,512]{1,0:T(8,128)(2,1)S(1)}, bf16[128,512]{1,0:T(8,128)(2,1)S(1)}, u32[]{:S(2)}, u32[]{:S(2)}) collective-permute-start(bf16[128,512]{1,0:T(8,128)(2,1)S(1)} %copy-done.4), channel_id=1, source_target_pairs={{0,112},{16,0},{32,16},{48,32},{64,48},{80,64},{96,80},{112,96},{1... | collective-permute-start | bytes 393224 | tf_op jit(solution)/shard_map/ppermute | solution.py:33
  59.6 3.6 %collective-permute-done.refs_1_ = bf16[128,512]{1,0:T(8,128)(2,1)S(1)} collective-permute-done((bf16[128,512]{1,0:T(8,128)(2,1)S(1)}, bf16[128,512]{1,0:T(8,128)(2,1)S(1)}, u32[]{:S(2)}, u32[]{:S(2)}) %collective-permute-start) | collective-permute-done | bytes 131104 | tf_op jit(solution)/shard_map/ppermute | solution.py:33
  63.2 3.2 %collective-permute-start.3 = (bf16[128,512]{1,0:T(8,128)(2,1)S(1)}, bf16[128,512]{1,0:T(8,128)(2,1)S(1)}, u32[]{:S(2)}, u32[]{:S(2)}) collective-permute-start(bf16[128,512]{1,0:T(8,128)(2,1)S(1)} %collective-permute-done.1.refs_2_), channel_id=1, source_target_pairs={{0,112},{16,0},{32,16},{48,32},{64,48},{80,64},{96,80},{112,96},{1... | collective-permute-start | bytes 393224 | tf_op jit(solution)/shard_map/ppermute | solution.py:33
  66.5 2.9 %collective-permute-done.2.refs_3_ = bf16[128,512]{1,0:T(8,128)(2,1)S(1)} collective-permute-done((bf16[128,512]{1,0:T(8,128)(2,1)S(1)}, bf16[128,512]{1,0:T(8,128)(2,1)S(1)}, u32[]{:S(2)}, u32[]{:S(2)}) %collective-permute-start.2) | collective-permute-done | bytes 131104 | tf_op jit(solution)/shard_map/ppermute | solution.py:33
  69.4 3.2 %collective-permute-start.5 = (bf16[128,512]{1,0:T(8,128)(2,1)S(1)}, bf16[128,512]{1,0:T(8,128)(2,1)S(1)}, u32[]{:S(2)}, u32[]{:S(2)}) collective-permute-start(bf16[128,512]{1,0:T(8,128)(2,1)S(1)} %collective-permute-done.3.refs_4_), channel_id=1, source_target_pairs={{0,112},{16,0},{32,16},{48,32},{64,48},{80,64},{96,80},{112,96},{1... | collective-permute-start | bytes 393224 | tf_op jit(solution)/shard_map/ppermute | solution.py:33
  72.6 2.9 %collective-permute-done.4.refs_5_ = bf16[128,512]{1,0:T(8,128)(2,1)S(1)} collective-permute-done((bf16[128,512]{1,0:T(8,128)(2,1)S(1)}, bf16[128,512]{1,0:T(8,128)(2,1)S(1)}, u32[]{:S(2)}, u32[]{:S(2)}) %collective-permute-start.4) | collective-permute-done | bytes 131104 | tf_op jit(solution)/shard_map/ppermute | solution.py:33
  75.7 6.0 %collective-permute-done.6.refs_7_ = bf16[128,512]{1,0:T(8,128)(2,1)S(1)} collective-permute-done((bf16[128,512]{1,0:T(8,128)(2,1)S(1)}, bf16[128,512]{1,0:T(8,128)(2,1)S(1)}, u32[]{:S(2)}, u32[]{:S(2)}) %collective-permute-start.6) | collective-permute-done | bytes 131104 | tf_op jit(solution)/shard_map/ppermute | solution.py:33
  81.8 12.4 %attend.1 = bf16[16,136,256]{2,1,0:T(8,128)(2,1)} custom-call(s32[8]{0:T(128)S(1)} %stack.68.span_ref, bf16[2048,256]{1,0:T(8,128)(2,1)S(1)} %bitcast.41, bf16[128,512]{1,0:T(8,128)(2,1)S(1)} %copy-done.4, bf16[128,512]{1,0:T(8,128)(2,1)S(1)} %collective-permute-done.refs_1_, bf16[128,512]{1,0:T(8,128)(2,1)S(1)} %collective-permute-done.1.refs_2_, ...), custom_call_target="tpu_custom_call" | custom-call | tf_op jit(solution)/shard_map/attend/pallas_call | solution.py:174
  94.2 7.2 %all-to-all-start.1 = ((bf16[16,136,256]{2,1,0:T(8,128)(2,1)}), bf16[16,136,256]{2,1,0:T(8,128)(2,1)S(1)}, u32[]{:S(2)}, u32[]{:S(2)}) async-start(bf16[16,136,256]{2,1,0:T(8,128)(2,1)} %attend.1), calls=%async_computation.1 | async-start | bytes 2228224 | tf_op jit(solution)/shard_map/all_to_all | solution.py:752
  101.7 11.8 %all-to-all-done.1.arrived_ref = bf16[16,136,256]{2,1,0:T(8,128)(2,1)S(1)} async-done(((bf16[16,136,256]{2,1,0:T(8,128)(2,1)}), bf16[16,136,256]{2,1,0:T(8,128)(2,1)S(1)}, u32[]{:S(2)}, u32[]{:S(2)}) %all-to-all-start.1) | async-done | bytes 1114144 | tf_op jit(solution)/shard_map/all_to_all | solution.py:752
  113.5 6.8 %merge.1 = (f32[64,2048]{1,0:T(8,128)S(1)}, bf16[72,2048]{1,0:T(8,128)(2,1)S(1)}) custom-call(s32[5]{0:T(128)S(1)} %stack.59.place_ref, bf16[16,136,256]{2,1,0:T(8,128)(2,1)S(1)} %all-to-all-done.1.arrived_ref, bf16[128,2048]{1,0:T(8,128)(2,1)S(1)} %copy-done, bf16[128,2048]{1,0:T(8,128)(2,1)S(1)} %copy-done.1, f32[1,2048]{1,0:T(1,128)S(1)} %bitcast.42, ...), custom_call_target="tpu_custom_call" | custom-call | tf_op jit(solution)/shard_map/merge/pallas_call | solution.py:298
  120.3 0.8 copy-done.2
  121.1 3.2 %collective-permute-start.11 = (bf16[72,2048]{1,0:T(8,128)(2,1)S(1)}, bf16[72,2048]{1,0:T(8,128)(2,1)S(1)}, u32[]{:S(2)}, u32[]{:S(2)}) collective-permute-start(bf16[72,2048]{1,0:T(8,128)(2,1)S(1)} %get-tuple-element.17.refs_0_), channel_id=1, source_target_pairs={{0,112},{16,0},{32,16},{48,32},{64,48},{80,64},{96,80},{112,96},{1... | collective-permute-start | bytes 884744 | tf_op jit(solution)/shard_map/ppermute | solution.py:33
  124.3 5.8 %collective-permute-done.12.refs_2_ = bf16[72,2048]{1,0:T(8,128)(2,1)S(1)} collective-permute-done((bf16[72,2048]{1,0:T(8,128)(2,1)S(1)}, bf16[72,2048]{1,0:T(8,128)(2,1)S(1)}, u32[]{:S(2)}, u32[]{:S(2)}) %collective-permute-start.12) | collective-permute-done | bytes 294944 | tf_op jit(solution)/shard_map/ppermute | solution.py:33
  130.1 3.5 %collective-permute-start.13 = (bf16[72,2048]{1,0:T(8,128)(2,1)S(1)}, bf16[72,2048]{1,0:T(8,128)(2,1)S(1)}, u32[]{:S(2)}, u32[]{:S(2)}) collective-permute-start(bf16[72,2048]{1,0:T(8,128)(2,1)S(1)} %collective-permute-done.11.refs_1_), channel_id=1, source_target_pairs={{0,112},{16,0},{32,16},{48,32},{64,48},{80,64},{96,80},{112,96},{1... | collective-permute-start | bytes 884744 | tf_op jit(solution)/shard_map/ppermute | solution.py:33
  133.6 6.7 %collective-permute-done.17.refs_0_ = bf16[72,2048]{1,0:T(8,128)(2,1)S(1)} collective-permute-done((bf16[72,2048]{1,0:T(8,128)(2,1)S(1)}, bf16[72,2048]{1,0:T(8,128)(2,1)S(1)}, u32[]{:S(2)}, u32[]{:S(2)}) %collective-permute-start.17) | collective-permute-done | bytes 294944 | tf_op jit(solution)/shard_map/ppermute | solution.py:33
  140.4 3.7 %collective-permute-start.18 = (bf16[72,2048]{1,0:T(8,128)(2,1)S(1)}, bf16[72,2048]{1,0:T(8,128)(2,1)S(1)}, u32[]{:S(2)}, u32[]{:S(2)}) collective-permute-start(bf16[72,2048]{1,0:T(8,128)(2,1)S(1)} %collective-permute-done.13.refs_3_), channel_id=1, source_target_pairs={{0,112},{16,0},{32,16},{48,32},{64,48},{80,64},{96,80},{112,96},{1... | collective-permute-start | bytes 884744 | tf_op jit(solution)/shard_map/ppermute | solution.py:33
  144.1 7.1 %collective-permute-done.19.refs_2_ = bf16[72,2048]{1,0:T(8,128)(2,1)S(1)} collective-permute-done((bf16[72,2048]{1,0:T(8,128)(2,1)S(1)}, bf16[72,2048]{1,0:T(8,128)(2,1)S(1)}, u32[]{:S(2)}, u32[]{:S(2)}) %collective-permute-start.19) | collective-permute-done | bytes 294944 | tf_op jit(solution)/shard_map/ppermute | solution.py:33
  151.2 7.9 %collective-permute-done.20.refs_3_ = bf16[72,2048]{1,0:T(8,128)(2,1)S(1)} collective-permute-done((bf16[72,2048]{1,0:T(8,128)(2,1)S(1)}, bf16[72,2048]{1,0:T(8,128)(2,1)S(1)}, u32[]{:S(2)}, u32[]{:S(2)}) %collective-permute-start.20) | collective-permute-done | bytes 294944 | tf_op jit(solution)/shard_map/ppermute | solution.py:33
  159.1 2.0 pack.3
  161.0 7.6 %all-to-all-start.4 = ((bf16[16,24,2048]{2,1,0:T(8,128)(2,1)}), bf16[16,24,2048]{2,1,0:T(8,128)(2,1)}, u32[]{:S(2)}, u32[]{:S(2)}) async-start(bf16[16,24,2048]{2,1,0:T(8,128)(2,1)} %bitcast.31), calls=%async_computation.4 | async-start | bytes 3145728 | tf_op jit(solution)/shard_map/all_to_all | solution.py:789
  169.4 1.9 pack.2
  171.3 12.8 %all-to-all-done.4 = bf16[16,24,2048]{2,1,0:T(8,128)(2,1)} async-done(((bf16[16,24,2048]{2,1,0:T(8,128)(2,1)}), bf16[16,24,2048]{2,1,0:T(8,128)(2,1)}, u32[]{:S(2)}, u32[]{:S(2)}) %all-to-all-start.4) | async-done | bytes 1572896 | tf_op jit(solution)/shard_map/all_to_all | solution.py:789
  184.1 6.5 %all-to-all-start.2 = ((bf16[16,24,2048]{2,1,0:T(8,128)(2,1)}), bf16[16,24,2048]{2,1,0:T(8,128)(2,1)}, u32[]{:S(2)}, u32[]{:S(2)}) async-start(bf16[16,24,2048]{2,1,0:T(8,128)(2,1)} %bitcast.24), calls=%async_computation.2 | async-start | bytes 3145728 | tf_op jit(solution)/shard_map/all_to_all | solution.py:789
  190.6 11.0 %expert_rows.3 = bf16[384,2048]{1,0:T(8,128)(2,1)} custom-call(bf16[384,2048]{1,0:T(8,128)(2,1)} %bitcast.32.rows_ref, bf16[2048,384]{1,0:T(8,128)(2,1)} %bitcast.43, bf16[2048,384]{1,0:T(8,128)(2,1)} %collective-permute-done.14.refs_1_, bf16[2048,384]{1,0:T(8,128)(2,1)} %bitcast.47, bf16[2048,384]{1,0:T(8,128)(2,1)} %collective-permute-done.15.refs_3_, ...), custom_call_target="tpu_custom_call" | custom-call | tf_op jit(solution)/shard_map/expert_rows/pallas_call | solution.py:634
  201.6 4.6 %all-to-all-done.2 = bf16[16,24,2048]{2,1,0:T(8,128)(2,1)} async-done(((bf16[16,24,2048]{2,1,0:T(8,128)(2,1)}), bf16[16,24,2048]{2,1,0:T(8,128)(2,1)}, u32[]{:S(2)}, u32[]{:S(2)}) %all-to-all-start.2) | async-done | bytes 1572896 | tf_op jit(solution)/shard_map/all_to_all | solution.py:789
  206.2 5.7 %all-to-all-start.5 = ((bf16[16,24,2048]{2,1,0:T(8,128)(2,1)}), bf16[16,24,2048]{2,1,0:T(8,128)(2,1)S(1)}, u32[]{:S(2)}, u32[]{:S(2)}) async-start(bf16[16,24,2048]{2,1,0:T(8,128)(2,1)} %bitcast.53), calls=%async_computation.5 | async-start | bytes 3145728 | tf_op jit(solution)/shard_map/all_to_all | solution.py:796
  211.9 11.1 %expert_rows.2 = bf16[384,2048]{1,0:T(8,128)(2,1)} custom-call(bf16[384,2048]{1,0:T(8,128)(2,1)} %bitcast.25.rows_ref, bf16[2048,384]{1,0:T(8,128)(2,1)} %bitcast.44, bf16[2048,384]{1,0:T(8,128)(2,1)} %collective-permute-done.14.refs_1_, bf16[2048,384]{1,0:T(8,128)(2,1)} %bitcast.48, bf16[2048,384]{1,0:T(8,128)(2,1)} %collective-permute-done.15.refs_3_, ...), custom_call_target="tpu_custom_call" | custom-call | tf_op jit(solution)/shard_map/expert_rows/pallas_call | solution.py:634
  223.0 5.3 %all-to-all-done.5 = bf16[16,24,2048]{2,1,0:T(8,128)(2,1)S(1)} async-done(((bf16[16,24,2048]{2,1,0:T(8,128)(2,1)}), bf16[16,24,2048]{2,1,0:T(8,128)(2,1)S(1)}, u32[]{:S(2)}, u32[]{:S(2)}) %all-to-all-start.5) | async-done | bytes 1572896 | tf_op jit(solution)/shard_map/all_to_all | solution.py:796
  228.3 5.6 %all-to-all-start.3 = ((bf16[16,24,2048]{2,1,0:T(8,128)(2,1)}), bf16[16,24,2048]{2,1,0:T(8,128)(2,1)S(1)}, u32[]{:S(2)}, u32[]{:S(2)}) async-start(bf16[16,24,2048]{2,1,0:T(8,128)(2,1)} %bitcast.52), calls=%async_computation.3 | async-start | bytes 3145728 | tf_op jit(solution)/shard_map/all_to_all | solution.py:796
  233.9 0.9 mixed.3
  235.2 3.2 %collective-permute-start.25 = (bf16[64,2048]{1,0:T(8,128)(2,1)S(1)}, bf16[64,2048]{1,0:T(8,128)(2,1)S(1)}, u32[]{:S(2)}, u32[]{:S(2)}) collective-permute-start(bf16[64,2048]{1,0:T(8,128)(2,1)S(1)} %get-tuple-element.27), channel_id=1, source_target_pairs={{0,112},{16,0},{32,16},{48,32},{64,48},{80,64},{96,80},{112,96},{1... | collective-permute-start | bytes 786440 | tf_op jit(solution)/shard_map/ppermute | solution.py:33
  238.4 5.2 %collective-permute-done.21 = bf16[64,2048]{1,0:T(8,128)(2,1)S(1)} collective-permute-done((bf16[64,2048]{1,0:T(8,128)(2,1)S(1)}, bf16[64,2048]{1,0:T(8,128)(2,1)S(1)}, u32[]{:S(2)}, u32[]{:S(2)}) %collective-permute-start.21) | collective-permute-done | bytes 262176 | tf_op jit(solution)/shard_map/ppermute | solution.py:33
  243.8 5.9 %all-to-all-done.3 = bf16[16,24,2048]{2,1,0:T(8,128)(2,1)S(1)} async-done(((bf16[16,24,2048]{2,1,0:T(8,128)(2,1)}), bf16[16,24,2048]{2,1,0:T(8,128)(2,1)S(1)}, u32[]{:S(2)}, u32[]{:S(2)}) %all-to-all-start.3) | async-done | bytes 1572896 | tf_op jit(solution)/shard_map/all_to_all | solution.py:796
  249.7 0.9 mixed.2
  250.8 2.8 %collective-permute-done.22 = bf16[64,2048]{1,0:T(8,128)(2,1)S(1)} collective-permute-done((bf16[64,2048]{1,0:T(8,128)(2,1)S(1)}, bf16[64,2048]{1,0:T(8,128)(2,1)S(1)}, u32[]{:S(2)}, u32[]{:S(2)}) %collective-permute-start.22) | collective-permute-done | bytes 262176 | tf_op jit(solution)/shard_map/ppermute | solution.py:33
  253.7 4.6 %collective-permute-done.26 = bf16[64,2048]{1,0:T(8,128)(2,1)S(1)} collective-permute-done((bf16[64,2048]{1,0:T(8,128)(2,1)S(1)}, bf16[64,2048]{1,0:T(8,128)(2,1)S(1)}, u32[]{:S(2)}, u32[]{:S(2)}) %collective-permute-start.26) | collective-permute-done | bytes 262176 | tf_op jit(solution)/shard_map/ppermute | solution.py:33
  258.3 4.3 %collective-permute-done.23 = bf16[64,2048]{1,0:T(8,128)(2,1)S(1)} collective-permute-done((bf16[64,2048]{1,0:T(8,128)(2,1)S(1)}, bf16[64,2048]{1,0:T(8,128)(2,1)S(1)}, u32[]{:S(2)}, u32[]{:S(2)}) %collective-permute-start.23) | collective-permute-done | bytes 262176 | tf_op jit(solution)/shard_map/ppermute | solution.py:33
  262.8 3.2 %collective-permute-start.27 = (bf16[64,2048]{1,0:T(8,128)(2,1)S(1)}, bf16[64,2048]{1,0:T(8,128)(2,1)S(1)}, u32[]{:S(2)}, u32[]{:S(2)}) collective-permute-start(bf16[64,2048]{1,0:T(8,128)(2,1)S(1)} %get-tuple-element.23), channel_id=1, source_target_pairs={{0,112},{16,0},{32,16},{48,32},{64,48},{80,64},{96,80},{112,96},{1... | collective-permute-start | bytes 786440 | tf_op jit(solution)/shard_map/ppermute | solution.py:33
  266.1 4.3 %collective-permute-done.24 = bf16[64,2048]{1,0:T(8,128)(2,1)S(1)} collective-permute-done((bf16[64,2048]{1,0:T(8,128)(2,1)S(1)}, bf16[64,2048]{1,0:T(8,128)(2,1)S(1)}, u32[]{:S(2)}, u32[]{:S(2)}) %collective-permute-start.24) | collective-permute-done | bytes 262176 | tf_op jit(solution)/shard_map/ppermute | solution.py:33
  (68 shorter events, 3.2 us)
Async XLA Ops:
  0.6 38.9 %collective-permute-start.7 = (bf16[512,2048]{1,0:T(8,128)(2,1)}, bf16[512,2048]{1,0:T(8,128)(2,1)}, u32[]{:S(2)}, u32[]{:S(2)}) collective-permute-start(bf16[512,2048]{1,0:T(8,128)(2,1)} %w_own.1), channel_id=1, source_target_pairs={{0,1},{1,2},{2,3},{3,0},{128,131},{129,128},{130,129},{131,130},{4... | collective-permute-start | bytes 6291464 | tf_op jit(solution)/shard_map/ppermute | solution.py:724
  11.4 45.0 %copy-start.4 = (bf16[128,512]{1,0:T(8,128)(2,1)S(1)}, bf16[128,512]{1,0:T(8,128)(2,1)}, u32[]{:S(2)}) copy-start(bf16[128,512]{1,0:T(8,128)(2,1)} %get-tuple-element.14.refs_0_) | copy-start | bytes 393220
  11.4 64.2 %collective-permute-start.9 = (bf16[256,2048]{1,0:T(8,128)(2,1)}, bf16[256,2048]{1,0:T(8,128)(2,1)S(1)}, u32[]{:S(2)}, u32[]{:S(2)}) collective-permute-start(bf16[256,2048]{1,0:T(8,128)(2,1)} %get-tuple-element.15), channel_id=1, source_target_pairs={{0,2},{1,3},{2,0},{3,1},{4,6},{5,7},{6,4},{7,5},{8,10},{9,11},{10,... | collective-permute-start | bytes 3145736 | tf_op jit(solution)/shard_map/ppermute | solution.py:33
  39.5 74.0 %collective-permute-start.8 = (bf16[512,2048]{1,0:T(8,128)(2,1)}, bf16[512,2048]{1,0:T(8,128)(2,1)}, u32[]{:S(2)}, u32[]{:S(2)}) collective-permute-start(bf16[512,2048]{1,0:T(8,128)(2,1)} %collective-permute-done.7.w_near_own), channel_id=1, source_target_pairs={{0,128},{128,0},{1,129},{129,1},{2,130},{130,2},{3,131},{131,3},{4... | collective-permute-start | bytes 6291464 | tf_op jit(solution)/shard_map/ppermute | solution.py:726
  48.8 32.9 %all-to-all-start = ((bf16[4,512,256]{2,1,0:T(8,128)(2,1)}), bf16[4,512,256]{2,1,0:T(8,128)(2,1)S(1)}, u32[]{:S(2)}, u32[]{:S(2)}) async-start(bf16[4,512,256]{2,1,0:T(8,128)(2,1)} %get-tuple-element.13), calls=%async_computation | async-start | bytes 2097152 | tf_op jit(solution)/shard_map/all_to_all | solution.py:730
  56.4 6.8 %collective-permute-start = (bf16[128,512]{1,0:T(8,128)(2,1)S(1)}, bf16[128,512]{1,0:T(8,128)(2,1)S(1)}, u32[]{:S(2)}, u32[]{:S(2)}) collective-permute-start(bf16[128,512]{1,0:T(8,128)(2,1)S(1)} %copy-done.4), channel_id=1, source_target_pairs={{0,16},{16,32},{32,48},{48,64},{64,80},{80,96},{96,112},{112,0},{1... | collective-permute-start | bytes 393224 | tf_op jit(solution)/shard_map/ppermute | solution.py:33
  56.4 6.8 %collective-permute-start.1 = (bf16[128,512]{1,0:T(8,128)(2,1)S(1)}, bf16[128,512]{1,0:T(8,128)(2,1)S(1)}, u32[]{:S(2)}, u32[]{:S(2)}) collective-permute-start(bf16[128,512]{1,0:T(8,128)(2,1)S(1)} %copy-done.4), channel_id=1, source_target_pairs={{0,112},{16,0},{32,16},{48,32},{64,48},{80,64},{96,80},{112,96},{1... | collective-permute-start | bytes 393224 | tf_op jit(solution)/shard_map/ppermute | solution.py:33
  63.2 6.2 %collective-permute-start.2 = (bf16[128,512]{1,0:T(8,128)(2,1)S(1)}, bf16[128,512]{1,0:T(8,128)(2,1)S(1)}, u32[]{:S(2)}, u32[]{:S(2)}) collective-permute-start(bf16[128,512]{1,0:T(8,128)(2,1)S(1)} %collective-permute-done.refs_1_), channel_id=1, source_target_pairs={{0,16},{16,32},{32,48},{48,64},{64,80},{80,96},{96,112},{112,0},{1... | collective-permute-start | bytes 393224 | tf_op jit(solution)/shard_map/ppermute | solution.py:33
  63.2 6.2 %collective-permute-start.3 = (bf16[128,512]{1,0:T(8,128)(2,1)S(1)}, bf16[128,512]{1,0:T(8,128)(2,1)S(1)}, u32[]{:S(2)}, u32[]{:S(2)}) collective-permute-start(bf16[128,512]{1,0:T(8,128)(2,1)S(1)} %collective-permute-done.1.refs_2_), channel_id=1, source_target_pairs={{0,112},{16,0},{32,16},{48,32},{64,48},{80,64},{96,80},{112,96},{1... | collective-permute-start | bytes 393224 | tf_op jit(solution)/shard_map/ppermute | solution.py:33
  69.4 6.2 %collective-permute-start.4 = (bf16[128,512]{1,0:T(8,128)(2,1)S(1)}, bf16[128,512]{1,0:T(8,128)(2,1)S(1)}, u32[]{:S(2)}, u32[]{:S(2)}) collective-permute-start(bf16[128,512]{1,0:T(8,128)(2,1)S(1)} %collective-permute-done.2.refs_3_), channel_id=1, source_target_pairs={{0,16},{16,32},{32,48},{48,64},{64,80},{80,96},{96,112},{112,0},{1... | collective-permute-start | bytes 393224 | tf_op jit(solution)/shard_map/ppermute | solution.py:33
  69.4 6.3 %collective-permute-start.5 = (bf16[128,512]{1,0:T(8,128)(2,1)S(1)}, bf16[128,512]{1,0:T(8,128)(2,1)S(1)}, u32[]{:S(2)}, u32[]{:S(2)}) collective-permute-start(bf16[128,512]{1,0:T(8,128)(2,1)S(1)} %collective-permute-done.3.refs_4_), channel_id=1, source_target_pairs={{0,112},{16,0},{32,16},{48,32},{64,48},{80,64},{96,80},{112,96},{1... | collective-permute-start | bytes 393224 | tf_op jit(solution)/shard_map/ppermute | solution.py:33
  75.6 6.2 %collective-permute-start.6 = (bf16[128,512]{1,0:T(8,128)(2,1)S(1)}, bf16[128,512]{1,0:T(8,128)(2,1)S(1)}, u32[]{:S(2)}, u32[]{:S(2)}) collective-permute-start(bf16[128,512]{1,0:T(8,128)(2,1)S(1)} %collective-permute-done.4.refs_5_), channel_id=1, source_target_pairs={{0,16},{16,32},{32,48},{48,64},{64,80},{80,96},{96,112},{112,0},{1... | collective-permute-start | bytes 393224 | tf_op jit(solution)/shard_map/ppermute | solution.py:33
  75.6 37.9 %collective-permute-start.10 = (bf16[256,2048]{1,0:T(8,128)(2,1)S(1)}, bf16[256,2048]{1,0:T(8,128)(2,1)}, u32[]{:S(2)}, u32[]{:S(2)}) collective-permute-start(bf16[256,2048]{1,0:T(8,128)(2,1)S(1)} %collective-permute-done.9.w_far_own), channel_id=1, source_target_pairs={{0,128},{128,0},{1,129},{129,1},{2,130},{130,2},{3,131},{131,3},{4... | collective-permute-start | bytes 3145736 | tf_op jit(solution)/shard_map/ppermute | solution.py:727
  94.1 7.3 %copy-start.7 = (f32[32,8]{0,1:T(8,128)S(1)}, f32[32,8]{0,1:T(8,128)}, u32[]{:S(2)}) copy-start(f32[32,8]{0,1:T(8,128)} %param.29) | copy-start | bytes 3076
  94.1 7.3 %copy-start.8 = (s32[32,8]{0,1:T(8,128)S(1)}, s32[32,8]{0,1:T(8,128)}, u32[]{:S(2)}) copy-start(s32[32,8]{0,1:T(8,128)} %param.28) | copy-start | bytes 3076
  94.1 19.3 %copy-start = (bf16[128,2048]{1,0:T(8,128)(2,1)S(1)}, bf16[128,2048]{1,0:T(8,128)(2,1)}, u32[]{:S(2)}) copy-start(bf16[128,2048]{1,0:T(8,128)(2,1)} %tokens_ref.3) | copy-start | bytes 1572868
  94.1 19.3 %copy-start.1 = (bf16[128,2048]{1,0:T(8,128)(2,1)S(1)}, bf16[128,2048]{1,0:T(8,128)(2,1)}, u32[]{:S(2)}) copy-start(bf16[128,2048]{1,0:T(8,128)(2,1)} %tangents_ref.3) | copy-start | bytes 1572868
  94.1 19.3 %copy-start.5 = (f32[2048]{0:T(1024)S(1)}, f32[2048]{0:T(1024)}, u32[]{:S(2)}) copy-start(f32[2048]{0:T(1024)} %param.18) | copy-start | bytes 24580
  94.2 19.3 %all-to-all-start.1 = ((bf16[16,136,256]{2,1,0:T(8,128)(2,1)}), bf16[16,136,256]{2,1,0:T(8,128)(2,1)S(1)}, u32[]{:S(2)}, u32[]{:S(2)}) async-start(bf16[16,136,256]{2,1,0:T(8,128)(2,1)} %attend.1), calls=%async_computation.1 | async-start | bytes 2228224 | tf_op jit(solution)/shard_map/all_to_all | solution.py:752
  120.3 0.8 copy-start.2
  121.1 9.0 %collective-permute-start.12 = (bf16[72,2048]{1,0:T(8,128)(2,1)S(1)}, bf16[72,2048]{1,0:T(8,128)(2,1)S(1)}, u32[]{:S(2)}, u32[]{:S(2)}) collective-permute-start(bf16[72,2048]{1,0:T(8,128)(2,1)S(1)} %get-tuple-element.17.refs_0_), channel_id=1, source_target_pairs={{0,16},{16,32},{32,48},{48,64},{64,80},{80,96},{96,112},{112,0},{1... | collective-permute-start | bytes 884744 | tf_op jit(solution)/shard_map/ppermute | solution.py:33
  121.1 9.0 %collective-permute-start.11 = (bf16[72,2048]{1,0:T(8,128)(2,1)S(1)}, bf16[72,2048]{1,0:T(8,128)(2,1)S(1)}, u32[]{:S(2)}, u32[]{:S(2)}) collective-permute-start(bf16[72,2048]{1,0:T(8,128)(2,1)S(1)} %get-tuple-element.17.refs_0_), channel_id=1, source_target_pairs={{0,112},{16,0},{32,16},{48,32},{64,48},{80,64},{96,80},{112,96},{1... | collective-permute-start | bytes 884744 | tf_op jit(solution)/shard_map/ppermute | solution.py:33
  130.1 10.2 %collective-permute-start.17 = (bf16[72,2048]{1,0:T(8,128)(2,1)S(1)}, bf16[72,2048]{1,0:T(8,128)(2,1)S(1)}, u32[]{:S(2)}, u32[]{:S(2)}) collective-permute-start(bf16[72,2048]{1,0:T(8,128)(2,1)S(1)} %collective-permute-done.12.refs_2_), channel_id=1, source_target_pairs={{0,16},{16,32},{32,48},{48,64},{64,80},{80,96},{96,112},{112,0},{1... | collective-permute-start | bytes 884744 | tf_op jit(solution)/shard_map/ppermute | solution.py:33
  130.1 10.3 %collective-permute-start.13 = (bf16[72,2048]{1,0:T(8,128)(2,1)S(1)}, bf16[72,2048]{1,0:T(8,128)(2,1)S(1)}, u32[]{:S(2)}, u32[]{:S(2)}) collective-permute-start(bf16[72,2048]{1,0:T(8,128)(2,1)S(1)} %collective-permute-done.11.refs_1_), channel_id=1, source_target_pairs={{0,112},{16,0},{32,16},{48,32},{64,48},{80,64},{96,80},{112,96},{1... | collective-permute-start | bytes 884744 | tf_op jit(solution)/shard_map/ppermute | solution.py:33
  140.3 10.9 %collective-permute-start.19 = (bf16[72,2048]{1,0:T(8,128)(2,1)S(1)}, bf16[72,2048]{1,0:T(8,128)(2,1)S(1)}, u32[]{:S(2)}, u32[]{:S(2)}) collective-permute-start(bf16[72,2048]{1,0:T(8,128)(2,1)S(1)} %collective-permute-done.17.refs_0_), channel_id=1, source_target_pairs={{0,16},{16,32},{32,48},{48,64},{64,80},{80,96},{96,112},{112,0},{1... | collective-permute-start | bytes 884744 | tf_op jit(solution)/shard_map/ppermute | solution.py:33
  140.4 10.8 %collective-permute-start.18 = (bf16[72,2048]{1,0:T(8,128)(2,1)S(1)}, bf16[72,2048]{1,0:T(8,128)(2,1)S(1)}, u32[]{:S(2)}, u32[]{:S(2)}) collective-permute-start(bf16[72,2048]{1,0:T(8,128)(2,1)S(1)} %collective-permute-done.13.refs_3_), channel_id=1, source_target_pairs={{0,112},{16,0},{32,16},{48,32},{64,48},{80,64},{96,80},{112,96},{1... | collective-permute-start | bytes 884744 | tf_op jit(solution)/shard_map/ppermute | solution.py:33
  151.1 7.9 %collective-permute-start.20 = (bf16[72,2048]{1,0:T(8,128)(2,1)S(1)}, bf16[72,2048]{1,0:T(8,128)(2,1)S(1)}, u32[]{:S(2)}, u32[]{:S(2)}) collective-permute-start(bf16[72,2048]{1,0:T(8,128)(2,1)S(1)} %collective-permute-done.19.refs_2_), channel_id=1, source_target_pairs={{0,16},{16,32},{32,48},{48,64},{64,80},{80,96},{96,112},{112,0},{1... | collective-permute-start | bytes 884744 | tf_op jit(solution)/shard_map/ppermute | solution.py:33
  161.0 7.6 %copy-start.6 = (bf16[1,2048,384]{2,1,0:T(8,128)(2,1)S(1)}, bf16[1,2048,384]{2,1,0:T(8,128)(2,1)}, u32[]{:S(2)}) copy-start(bf16[1,2048,384]{2,1,0:T(8,128)(2,1)} %param.25) | copy-start | bytes 4718596
  161.0 23.1 %all-to-all-start.4 = ((bf16[16,24,2048]{2,1,0:T(8,128)(2,1)}), bf16[16,24,2048]{2,1,0:T(8,128)(2,1)}, u32[]{:S(2)}, u32[]{:S(2)}) async-start(bf16[16,24,2048]{2,1,0:T(8,128)(2,1)} %bitcast.31), calls=%async_computation.4 | async-start | bytes 3145728 | tf_op jit(solution)/shard_map/all_to_all | solution.py:789
  168.7 21.9 %collective-permute-start.14 = (bf16[2048,384]{1,0:T(8,128)(2,1)S(1)}, bf16[2048,384]{1,0:T(8,128)(2,1)}, u32[]{:S(2)}, u32[]{:S(2)}) collective-permute-start(bf16[2048,384]{1,0:T(8,128)(2,1)S(1)} %bitcast.45), channel_id=1, source_target_pairs={{0,128},{128,0},{1,129},{129,1},{2,130},{130,2},{3,131},{131,3},{4... | collective-permute-start | bytes 4718600 | tf_op jit(solution)/shard_map/ppermute | solution.py:676
  168.8 21.8 %collective-permute-start.15 = (bf16[2048,384]{1,0:T(8,128)(2,1)}, bf16[2048,384]{1,0:T(8,128)(2,1)}, u32[]{:S(2)}, u32[]{:S(2)}) collective-permute-start(bf16[2048,384]{1,0:T(8,128)(2,1)} %bitcast.46), channel_id=1, source_target_pairs={{0,128},{128,0},{1,129},{129,1},{2,130},{130,2},{3,131},{131,3},{4... | collective-permute-start | bytes 4718600 | tf_op jit(solution)/shard_map/ppermute | solution.py:676
  169.3 21.3 %collective-permute-start.16 = (bf16[2048,384]{1,0:T(8,128)(2,1)}, bf16[2048,384]{1,0:T(8,128)(2,1)}, u32[]{:S(2)}, u32[]{:S(2)}) collective-permute-start(bf16[2048,384]{1,0:T(8,128)(2,1)} %bitcast.49), channel_id=1, source_target_pairs={{0,128},{128,0},{1,129},{129,1},{2,130},{130,2},{3,131},{131,3},{4... | collective-permute-start | bytes 4718600 | tf_op jit(solution)/shard_map/ppermute | solution.py:676
  184.1 22.1 %all-to-all-start.2 = ((bf16[16,24,2048]{2,1,0:T(8,128)(2,1)}), bf16[16,24,2048]{2,1,0:T(8,128)(2,1)}, u32[]{:S(2)}, u32[]{:S(2)}) async-start(bf16[16,24,2048]{2,1,0:T(8,128)(2,1)} %bitcast.24), calls=%async_computation.2 | async-start | bytes 3145728 | tf_op jit(solution)/shard_map/all_to_all | solution.py:789
  206.2 22.1 %all-to-all-start.5 = ((bf16[16,24,2048]{2,1,0:T(8,128)(2,1)}), bf16[16,24,2048]{2,1,0:T(8,128)(2,1)S(1)}, u32[]{:S(2)}, u32[]{:S(2)}) async-start(bf16[16,24,2048]{2,1,0:T(8,128)(2,1)} %bitcast.53), calls=%async_computation.5 | async-start | bytes 3145728 | tf_op jit(solution)/shard_map/all_to_all | solution.py:796
  228.3 21.4 %all-to-all-start.3 = ((bf16[16,24,2048]{2,1,0:T(8,128)(2,1)}), bf16[16,24,2048]{2,1,0:T(8,128)(2,1)S(1)}, u32[]{:S(2)}, u32[]{:S(2)}) async-start(bf16[16,24,2048]{2,1,0:T(8,128)(2,1)} %bitcast.52), calls=%async_computation.3 | async-start | bytes 3145728 | tf_op jit(solution)/shard_map/all_to_all | solution.py:796
  235.1 8.6 %collective-permute-start.21 = (bf16[64,2048]{1,0:T(8,128)(2,1)S(1)}, bf16[64,2048]{1,0:T(8,128)(2,1)S(1)}, u32[]{:S(2)}, u32[]{:S(2)}) collective-permute-start(bf16[64,2048]{1,0:T(8,128)(2,1)S(1)} %get-tuple-element.26), channel_id=1, source_target_pairs={{0,16},{16,32},{32,48},{48,64},{64,80},{80,96},{96,112},{112,0},{1... | collective-permute-start | bytes 786440 | tf_op jit(solution)/shard_map/ppermute | solution.py:33
  235.2 8.5 %collective-permute-start.25 = (bf16[64,2048]{1,0:T(8,128)(2,1)S(1)}, bf16[64,2048]{1,0:T(8,128)(2,1)S(1)}, u32[]{:S(2)}, u32[]{:S(2)}) collective-permute-start(bf16[64,2048]{1,0:T(8,128)(2,1)S(1)} %get-tuple-element.27), channel_id=1, source_target_pairs={{0,112},{16,0},{32,16},{48,32},{64,48},{80,64},{96,80},{112,96},{1... | collective-permute-start | bytes 786440 | tf_op jit(solution)/shard_map/ppermute | solution.py:33
  243.8 9.8 %collective-permute-start.22 = (bf16[64,2048]{1,0:T(8,128)(2,1)S(1)}, bf16[64,2048]{1,0:T(8,128)(2,1)S(1)}, u32[]{:S(2)}, u32[]{:S(2)}) collective-permute-start(bf16[64,2048]{1,0:T(8,128)(2,1)S(1)} %get-tuple-element.24), channel_id=1, source_target_pairs={{0,16},{16,32},{32,48},{48,64},{64,80},{80,96},{96,112},{112,0},{1... | collective-permute-start | bytes 786440 | tf_op jit(solution)/shard_map/ppermute | solution.py:33
  250.6 19.8 %copy-start.3 = (f32[64,2048]{1,0:T(8,128)S(1)}, f32[64,2048]{1,0:T(8,128)}, u32[]{:S(2)}) copy-start(f32[64,2048]{1,0:T(8,128)} %copy-done.2) | copy-start | bytes 1572868
  250.7 7.7 %collective-permute-start.26 = (bf16[64,2048]{1,0:T(8,128)(2,1)S(1)}, bf16[64,2048]{1,0:T(8,128)(2,1)S(1)}, u32[]{:S(2)}, u32[]{:S(2)}) collective-permute-start(bf16[64,2048]{1,0:T(8,128)(2,1)S(1)} %get-tuple-element.25), channel_id=1, source_target_pairs={{0,112},{16,0},{32,16},{48,32},{64,48},{80,64},{96,80},{112,96},{1... | collective-permute-start | bytes 786440 | tf_op jit(solution)/shard_map/ppermute | solution.py:33
  253.6 9.0 %collective-permute-start.23 = (bf16[64,2048]{1,0:T(8,128)(2,1)S(1)}, bf16[64,2048]{1,0:T(8,128)(2,1)S(1)}, u32[]{:S(2)}, u32[]{:S(2)}) collective-permute-start(bf16[64,2048]{1,0:T(8,128)(2,1)S(1)} %fusion.3), channel_id=1, source_target_pairs={{0,16},{16,32},{32,48},{48,64},{64,80},{80,96},{96,112},{112,0},{1... | collective-permute-start | bytes 786440 | tf_op jit(solution)/shard_map/ppermute | solution.py:33
  262.7 7.7 %collective-permute-start.24 = (bf16[64,2048]{1,0:T(8,128)(2,1)S(1)}, bf16[64,2048]{1,0:T(8,128)(2,1)S(1)}, u32[]{:S(2)}, u32[]{:S(2)}) collective-permute-start(bf16[64,2048]{1,0:T(8,128)(2,1)S(1)} %get-tuple-element.22), channel_id=1, source_target_pairs={{0,16},{16,32},{32,48},{48,64},{64,80},{80,96},{96,112},{112,0},{1... | collective-permute-start | bytes 786440 | tf_op jit(solution)/shard_map/ppermute | solution.py:33
  262.8 7.6 %collective-permute-start.27 = (bf16[64,2048]{1,0:T(8,128)(2,1)S(1)}, bf16[64,2048]{1,0:T(8,128)(2,1)S(1)}, u32[]{:S(2)}, u32[]{:S(2)}) collective-permute-start(bf16[64,2048]{1,0:T(8,128)(2,1)S(1)} %get-tuple-element.23), channel_id=1, source_target_pairs={{0,112},{16,0},{32,16},{48,32},{64,48},{80,64},{96,80},{112,96},{1... | collective-permute-start | bytes 786440 | tf_op jit(solution)/shard_map/ppermute | solution.py:33
